TPU v7x, 32 devices: a whole 2x2x4 slice. The times are simulated.
32 devices in a mesh: expert: 8 (over z, y), tensor: 4 (over x, core).
Axes of the slice: x: 2, y: 2, z: 4, core: 2. Of those that a mesh axis runs over, the one named last changes fastest.
Arguments:
- hidden_in: bfloat16 [4096, 2048], P('expert'), may hold values from -6 to 6
- seq_lengths: int32 [8], P('expert'), may hold values from 256 to 512, as said below
- expert_ids: int32 [4096, 4], P('expert'), may hold values from 0 to 15, all different within a row; in each aligned block of 512 rows (0 to 511, 512 to 1023, ...) at most 192 rows name the same one
- attn_gain: bfloat16 [2048], replicated, may hold values from 0.5 to 1.5
- w_query: bfloat16 [2048, 2048], P(None, 'tensor'), may hold values from -0.125 to 0.125
- w_key: bfloat16 [2048, 2048], P(None, 'tensor'), may hold values from -0.125 to 0.125
- w_value: bfloat16 [2048, 2048], P(None, 'tensor'), may hold values from -0.125 to 0.125
- b_query: bfloat16 [16, 128], P('tensor'), may hold values from -3 to 3
- b_key: bfloat16 [16, 128], P('tensor'), may hold values from -3 to 3
- b_value: bfloat16 [16, 128], P('tensor'), may hold values from -0.1796875 to 0.1796875
- w_output: bfloat16 [2048, 2048], P('tensor'), may hold values from -1 to 1
- ffn_gain: bfloat16 [2048], replicated, may hold values from 0.5 to 1.5
- w_router: bfloat16 [2048, 16], replicated, may hold values from -0.0625 to 0.0625
- w_sigmoid: bfloat16 [2048], replicated, may hold values from -0.125 to 0.125
- shared_gate: bfloat16 [2048, 5632], P(None, 'tensor'), may hold values from -0.125 to 0.125
- shared_up: bfloat16 [2048, 5632], P(None, 'tensor'), may hold values from -0.125 to 0.125
- shared_down: bfloat16 [5632, 2048], P('tensor'), may hold values from -0.078125 to 0.078125
- expert_gate: bfloat16 [16, 2048, 1408], P('expert', None, 'tensor'), may hold values from -0.125 to 0.125
- expert_up: bfloat16 [16, 2048, 1408], P('expert', None, 'tensor'), may hold values from -0.125 to 0.125
- expert_down: bfloat16 [16, 1408, 2048], P('expert', 'tensor'), may hold values from -1.25 to 1.25
- out_grad: bfloat16 [4096, 2048], P('expert'), may hold values from -6 to 6
Outputs:
- layer_out: bfloat16 [4096, 2048], P('expert')
- grad_in: bfloat16 [4096, 2048], P('expert')
- grad_attn_gain: float32 [2048], P('expert')
- grad_w_query: float32 [2048, 2048], P('expert', 'tensor')
- grad_w_key: float32 [2048, 2048], P('expert', 'tensor')
- grad_w_value: float32 [2048, 2048], P('expert', 'tensor')
- grad_b_query: float32 [16, 128], P('tensor', 'expert')
- grad_b_key: float32 [16, 128], P('tensor', 'expert')
- grad_b_value: float32 [16, 128], P('tensor', 'expert')
- grad_w_output: float32 [2048, 2048], P('tensor', 'expert')
- grad_ffn_gain: float32 [2048], P('expert')
- grad_w_router: float32 [2048, 16], P('expert')
- grad_w_sigmoid: float32 [2048], P('expert')
- grad_shared_gate: float32 [2048, 5632], P('expert', 'tensor')
- grad_shared_up: float32 [2048, 5632], P('expert', 'tensor')
- grad_shared_down: float32 [5632, 2048], P('tensor', 'expert')
- grad_expert_gate: float32 [16, 2048, 1408], P('expert', None, 'tensor')
- grad_expert_up: float32 [16, 2048, 1408], P('expert', None, 'tensor')
- grad_expert_down: float32 [16, 1408, 2048], P('expert', 'tensor')
Inputs may be any that keep to these rules, and one draw needn't show every extreme that they name: `expert_ids`: in each aligned block of 512 rows (the tokens of one sequence) no expert is named by more than 192 rows, and in some block an expert is named by exactly 192 rows; a row names 4 different experts. `seq_lengths`: some sequence has exactly 512 valid tokens.
All inputs are finite; a program needn't handle non-finite values.
Results may differ from a plain program's by a relative error of at most 0.025.
Values may be sent and summed in bfloat16 or wider, within the bound.
A program may use at most 384 MiB of HBM per device.

v0:
```python
import math

import jax
import jax.numpy as jnp
from jax import lax
from jax.sharding import PartitionSpec as P

rope_base = 1000000.0
norm_eps = 1e-06


def rms_norm(values, gain):
    return values * lax.rsqrt(jnp.mean(values * values, axis=-1, keepdims=True) + norm_eps) * gain


def rotary_tables(length, head_width):
    half_width = head_width // 2
    freq = jnp.exp(
        jnp.arange(half_width, dtype=jnp.float32) * (-2.0 * math.log(rope_base) / head_width)
    )
    angle = jnp.arange(length, dtype=jnp.float32)[:, None] * freq[None, :]
    angle = jnp.concatenate([angle, angle], axis=1)
    return (jnp.cos(angle)[:, None, :], jnp.sin(angle)[:, None, :])


def rotate(values):
    half_width = values.shape[-1] // 2
    return jnp.concatenate([-values[..., half_width:], values[..., :half_width]], axis=-1)


def matmul(left, right):
    return jnp.dot(left, right, preferred_element_type=jnp.float32)


def contract_rows(left, right):
    return lax.dot_general(
        left, right, (((0,), (0,)), ((), ())), preferred_element_type=jnp.float32
    )


def times_transposed(left, right):
    return lax.dot_general(
        left, right, (((1,), (1,)), ((), ())), preferred_element_type=jnp.float32
    )


def block_allowed(first_row, block_rows, key_count, length):
    query_pos = first_row + jnp.arange(block_rows)[:, None]
    key_pos = jnp.arange(key_count)[None, :]
    return (key_pos <= query_pos) & (key_pos < length)


def attend_forward(query, key, value, length, block_rows, score_scale):
    key_count = query.shape[0]
    scores = (
        jnp.einsum("qhd,khd->hqk", query, key, preferred_element_type=jnp.float32) * score_scale
    )
    allowed = block_allowed(0, block_rows, key_count, length)
    scores = jnp.where(allowed[None], scores, -1e30)
    highest = jnp.max(scores, axis=-1, keepdims=True)
    log_total = highest + jnp.log(jnp.sum(jnp.exp(scores - highest), axis=-1, keepdims=True))
    probs = jnp.exp(scores - log_total)
    contexts = jnp.einsum(
        "hqk,khd->qhd", probs.astype(jnp.bfloat16), value, preferred_element_type=jnp.float32
    )
    totals = [log_total]
    return (contexts.astype(jnp.bfloat16), totals)


def attend_backward(query, key, value, d_context, totals, length, block_rows, score_scale):
    key_count = query.shape[0]
    d_query_parts = []
    d_key = jnp.zeros(key.shape, jnp.float32)
    d_value = jnp.zeros(value.shape, jnp.float32)
    for block_index, first_row in enumerate(range(0, key_count, block_rows)):
        scores = (
            jnp.einsum("qhd,khd->hqk", query, key, preferred_element_type=jnp.float32) * score_scale
        )
        allowed = block_allowed(first_row, block_rows, key_count, length)
        probs = jnp.exp(jnp.where(allowed[None], scores, -1e30) - totals[block_index])
        d_probs = jnp.einsum("qhd,khd->hqk", d_context, value, preferred_element_type=jnp.float32)
        row_dot = jnp.sum(probs * d_probs, axis=-1, keepdims=True)
        d_scores = (probs * (d_probs - row_dot)).astype(jnp.bfloat16)
        d_query_parts.append(
            jnp.einsum("hqk,khd->qhd", d_scores, key, preferred_element_type=jnp.float32)
            * score_scale
        )
        d_key = (
            jnp.einsum("hqk,qhd->khd", d_scores, query, preferred_element_type=jnp.float32)
            * score_scale
        )
        d_value = jnp.einsum(
            "hqk,qhd->khd",
            probs.astype(jnp.bfloat16),
            d_context,
            preferred_element_type=jnp.float32,
        )
    return (d_query_parts[0], d_key, d_value)


def send_tokens(send_rows):
    share = send_rows.shape[2] // lax.axis_size("tensor")
    first_col = lax.axis_index("tensor") * share
    columns = lax.dynamic_slice_in_dim(send_rows, first_col, share, 2)
    arrived = lax.all_to_all(columns, "expert", split_axis=0, concat_axis=0, tiled=True)
    return lax.all_gather(arrived, "tensor", axis=2, tiled=True)


def return_rows(owner_rows):
    return lax.all_to_all(
        owner_rows.astype(jnp.bfloat16), "expert", split_axis=0, concat_axis=0, tiled=True
    ).astype(owner_rows.dtype)


def on_device(
    hidden_in,
    seq_lengths,
    expert_ids,
    attn_gain,
    w_query,
    w_key,
    w_value,
    b_query,
    b_key,
    b_value,
    w_output,
    ffn_gain,
    w_router,
    w_sigmoid,
    shared_gate,
    shared_up,
    shared_down,
    expert_gate,
    expert_up,
    expert_down,
    out_grad,
):
    tokens_here = hidden_in.shape[0]
    model_width = hidden_in.shape[1]
    head_count = b_query.shape[0]
    head_width = b_query.shape[1]
    top_count = expert_ids.shape[1]
    experts_all = w_router.shape[1]
    experts_here = expert_gate.shape[0]
    group_count = lax.axis_size("expert")
    capacity = 3 * tokens_here * top_count // (2 * experts_all)
    block_rows = min(512, tokens_here)
    score_scale = 1.0 / math.sqrt(head_width)
    length = seq_lengths[0]
    valid = (jnp.arange(tokens_here) < length).astype(jnp.float32)
    first_rank = (lax.axis_index("tensor") == 0).astype(jnp.float32)
    resid_in = hidden_in.astype(jnp.float32)
    gain_attn = attn_gain.astype(jnp.float32)
    normed_attn = rms_norm(resid_in, gain_attn).astype(jnp.bfloat16)
    cosine, sine = rotary_tables(tokens_here, head_width)
    query_pre = (matmul(normed_attn, w_query) + b_query.reshape(-1).astype(jnp.float32)).reshape(
        tokens_here, head_count, head_width
    )
    key_pre = (matmul(normed_attn, w_key) + b_key.reshape(-1).astype(jnp.float32)).reshape(
        tokens_here, head_count, head_width
    )
    value_pre = matmul(normed_attn, w_value) + b_value.reshape(-1).astype(jnp.float32)
    query = (query_pre * cosine + rotate(query_pre) * sine).astype(jnp.bfloat16)
    key = (key_pre * cosine + rotate(key_pre) * sine).astype(jnp.bfloat16)
    value = value_pre.astype(jnp.bfloat16).reshape(tokens_here, head_count, head_width)
    context, totals = attend_forward(query, key, value, length, block_rows, score_scale)
    context_flat = context.reshape(tokens_here, head_count * head_width)
    attn_out = lax.psum(matmul(context_flat, w_output), "tensor")
    resid = resid_in + attn_out
    gain_ffn = ffn_gain.astype(jnp.float32)
    normed_ffn = rms_norm(resid, gain_ffn).astype(jnp.bfloat16)
    logits = matmul(normed_ffn, w_router)
    route_probs = jax.nn.softmax(logits, axis=-1)
    onehot = (expert_ids[:, :, None] == jnp.arange(experts_all)[None, None, :]).astype(jnp.float32)
    gates = jnp.sum(route_probs[:, None, :] * onehot, axis=-1)
    sig = jax.nn.sigmoid(jnp.dot(normed_ffn, w_sigmoid, preferred_element_type=jnp.float32))
    shared_a = matmul(normed_ffn, shared_gate)
    shared_b = matmul(normed_ffn, shared_up)
    shared_hidden = (jax.nn.silu(shared_a) * shared_b).astype(jnp.bfloat16)
    shared_out = matmul(shared_hidden, shared_down)
    flat_ids = expert_ids.reshape(-1)
    assigned = flat_ids.shape[0]
    hot = (flat_ids[:, None] == jnp.arange(experts_all)[None, :]).astype(jnp.int32)
    rank = jnp.sum((jnp.cumsum(hot, axis=0) - hot) * hot, axis=1)
    slot = flat_ids * capacity + rank
    slots_all = experts_all * capacity
    assign_of = (
        jnp.zeros((slots_all,), jnp.int32).at[slot].set(jnp.arange(assigned, dtype=jnp.int32))
    )
    filled = jnp.zeros((slots_all,), jnp.float32).at[slot].set(1.0)
    token_of = assign_of // top_count
    send_rows = (normed_ffn[token_of] * filled.astype(jnp.bfloat16)[:, None]).reshape(
        group_count, experts_here * capacity, model_width
    )
    received = send_tokens(send_rows).reshape(group_count, experts_here, capacity, model_width)
    expert_a = jnp.einsum(
        "gecd,edf->gecf", received, expert_gate, preferred_element_type=jnp.float32
    )
    expert_b = jnp.einsum("gecd,edf->gecf", received, expert_up, preferred_element_type=jnp.float32)
    expert_hidden = (jax.nn.silu(expert_a) * expert_b).astype(jnp.bfloat16)
    expert_out = jnp.einsum(
        "gecf,efd->gecd", expert_hidden, expert_down, preferred_element_type=jnp.float32
    )
    masked_grad = out_grad.astype(jnp.float32) * valid[:, None]
    returned = return_rows(
        expert_out.reshape(group_count, experts_here * capacity, model_width)
    ).reshape(slots_all, model_width)
    row_width = returned.shape[1]
    expert_rows = returned[slot].reshape(tokens_here, top_count, row_width)
    routed_part = jnp.sum(gates[:, :, None] * expert_rows, axis=1)
    ffn_part = sig[:, None] * shared_out + routed_part
    gate_grad_part = jnp.sum(masked_grad[:, None, :] * expert_rows, axis=-1)
    sig_grad_part = jnp.sum(masked_grad * shared_out, axis=-1)
    ffn_total = lax.psum(ffn_part.astype(jnp.bfloat16), "tensor").astype(jnp.float32)
    layer_out = (resid + ffn_total).astype(jnp.bfloat16)
    slot_grad = (gates.reshape(-1)[assign_of] * filled)[:, None] * masked_grad[token_of]
    send_grads = slot_grad.astype(jnp.bfloat16).reshape(
        group_count, experts_here * capacity, model_width
    )
    d_expert_out = send_tokens(send_grads).reshape(group_count, experts_here, capacity, model_width)
    d_expert_hidden = jnp.einsum(
        "gecd,efd->gecf", d_expert_out, expert_down, preferred_element_type=jnp.float32
    )
    grad_expert_down = jnp.einsum(
        "gecf,gecd->efd", expert_hidden, d_expert_out, preferred_element_type=jnp.float32
    )
    sigma_a = jax.nn.sigmoid(expert_a)
    d_expert_a = (d_expert_hidden * expert_b * sigma_a * (1.0 + expert_a * (1.0 - sigma_a))).astype(
        jnp.bfloat16
    )
    d_expert_b = (d_expert_hidden * expert_a * sigma_a).astype(jnp.bfloat16)
    grad_expert_gate = jnp.einsum(
        "gecd,gecf->edf", received, d_expert_a, preferred_element_type=jnp.float32
    )
    grad_expert_up = jnp.einsum(
        "gecd,gecf->edf", received, d_expert_b, preferred_element_type=jnp.float32
    )
    d_expert_in = jnp.einsum(
        "gecf,edf->gecd", d_expert_a, expert_gate, preferred_element_type=jnp.float32
    ) + jnp.einsum("gecf,edf->gecd", d_expert_b, expert_up, preferred_element_type=jnp.float32)
    d_back_rows = return_rows(
        d_expert_in.reshape(group_count, experts_here * capacity, model_width)
    ).reshape(slots_all, model_width)
    d_from_experts = jnp.sum(
        d_back_rows[slot].reshape(tokens_here, top_count, d_back_rows.shape[1]), axis=1
    )
    d_shared_out = (sig[:, None] * masked_grad).astype(jnp.bfloat16)
    grad_shared_down = contract_rows(shared_hidden, d_shared_out)
    d_shared_hidden = times_transposed(d_shared_out, shared_down)
    sigma_shared = jax.nn.sigmoid(shared_a)
    d_shared_a = (
        d_shared_hidden * shared_b * sigma_shared * (1.0 + shared_a * (1.0 - sigma_shared))
    ).astype(jnp.bfloat16)
    d_shared_b = (d_shared_hidden * shared_a * sigma_shared).astype(jnp.bfloat16)
    grad_shared_gate = contract_rows(normed_ffn, d_shared_a)
    grad_shared_up = contract_rows(normed_ffn, d_shared_b)
    d_from_shared = times_transposed(d_shared_a, shared_gate) + times_transposed(
        d_shared_b, shared_up
    )
    gate_grad, sig_grad = lax.psum((gate_grad_part, sig_grad_part), "tensor")
    per_expert = jnp.sum(gate_grad[:, :, None] * onehot, axis=1)
    d_logits = (
        route_probs * (per_expert - jnp.sum(route_probs * per_expert, axis=-1, keepdims=True))
    ).astype(jnp.bfloat16)
    d_sig_logit = (sig_grad * sig * (1.0 - sig)).astype(jnp.bfloat16)
    grad_w_router = contract_rows(normed_ffn, d_logits)
    grad_w_sigmoid = contract_rows(normed_ffn, d_sig_logit)
    d_from_gates = (
        times_transposed(d_logits, w_router)
        + d_sig_logit.astype(jnp.float32)[:, None] * w_sigmoid.astype(jnp.float32)[None, :]
    )
    d_normed_ffn = lax.psum(
        (d_from_experts + d_from_shared + first_rank * d_from_gates).astype(jnp.bfloat16), "tensor"
    ).astype(jnp.float32)
    normed_again, ffn_norm_back = jax.vjp(rms_norm, resid, gain_ffn)
    d_resid_norm, grad_ffn_gain = ffn_norm_back(d_normed_ffn)
    d_resid = masked_grad + d_resid_norm
    d_attn = d_resid.astype(jnp.bfloat16)
    grad_w_output = contract_rows(context_flat, d_attn)
    d_context = (
        times_transposed(d_attn, w_output)
        .astype(jnp.bfloat16)
        .reshape(tokens_here, head_count, head_width)
    )
    d_query_rot, d_key_rot, d_value_all = attend_backward(
        query, key, value, d_context, totals, length, block_rows, score_scale
    )
    d_query = (
        (d_query_rot * cosine - rotate(d_query_rot) * sine)
        .astype(jnp.bfloat16)
        .reshape(tokens_here, head_count * head_width)
    )
    d_key = (
        (d_key_rot * cosine - rotate(d_key_rot) * sine)
        .astype(jnp.bfloat16)
        .reshape(tokens_here, head_count * head_width)
    )
    d_value = d_value_all.astype(jnp.bfloat16).reshape(tokens_here, head_count * head_width)
    grad_w_query = contract_rows(normed_attn, d_query)
    grad_w_key = contract_rows(normed_attn, d_key)
    grad_w_value = contract_rows(normed_attn, d_value)
    grad_b_query = jnp.sum(d_query.astype(jnp.float32), axis=0).reshape(head_count, head_width)
    grad_b_key = jnp.sum(d_key.astype(jnp.float32), axis=0).reshape(head_count, head_width)
    grad_b_value = jnp.sum(d_value.astype(jnp.float32), axis=0).reshape(head_count, head_width)
    d_normed_attn = lax.psum(
        (
            times_transposed(d_query, w_query)
            + times_transposed(d_key, w_key)
            + times_transposed(d_value, w_value)
        ).astype(jnp.bfloat16),
        "tensor",
    ).astype(jnp.float32)
    normed_first, attn_norm_back = jax.vjp(rms_norm, resid_in, gain_attn)
    d_input_norm, grad_attn_gain = attn_norm_back(d_normed_attn)
    grad_in = (d_resid + d_input_norm).astype(jnp.bfloat16)
    summed = (
        lax.psum_scatter(
            grad_attn_gain.astype(jnp.bfloat16), "expert", scatter_dimension=0, tiled=True
        ).astype(jnp.float32),
        lax.psum_scatter(
            grad_w_query.astype(jnp.bfloat16), "expert", scatter_dimension=0, tiled=True
        ).astype(jnp.float32),
        lax.psum_scatter(
            grad_w_key.astype(jnp.bfloat16), "expert", scatter_dimension=0, tiled=True
        ).astype(jnp.float32),
        lax.psum_scatter(
            grad_w_value.astype(jnp.bfloat16), "expert", scatter_dimension=0, tiled=True
        ).astype(jnp.float32),
        lax.psum_scatter(
            grad_b_query.astype(jnp.bfloat16), "expert", scatter_dimension=1, tiled=True
        ).astype(jnp.float32),
        lax.psum_scatter(
            grad_b_key.astype(jnp.bfloat16), "expert", scatter_dimension=1, tiled=True
        ).astype(jnp.float32),
        lax.psum_scatter(
            grad_b_value.astype(jnp.bfloat16), "expert", scatter_dimension=1, tiled=True
        ).astype(jnp.float32),
        lax.psum_scatter(
            grad_w_output.astype(jnp.bfloat16), "expert", scatter_dimension=1, tiled=True
        ).astype(jnp.float32),
        lax.psum_scatter(
            grad_ffn_gain.astype(jnp.bfloat16), "expert", scatter_dimension=0, tiled=True
        ).astype(jnp.float32),
        lax.psum_scatter(
            grad_w_router.astype(jnp.bfloat16), "expert", scatter_dimension=0, tiled=True
        ).astype(jnp.float32),
        lax.psum_scatter(
            grad_w_sigmoid.astype(jnp.bfloat16), "expert", scatter_dimension=0, tiled=True
        ).astype(jnp.float32),
        lax.psum_scatter(
            grad_shared_gate.astype(jnp.bfloat16), "expert", scatter_dimension=0, tiled=True
        ).astype(jnp.float32),
        lax.psum_scatter(
            grad_shared_up.astype(jnp.bfloat16), "expert", scatter_dimension=0, tiled=True
        ).astype(jnp.float32),
        lax.psum_scatter(
            grad_shared_down.astype(jnp.bfloat16), "expert", scatter_dimension=1, tiled=True
        ).astype(jnp.float32),
    )
    return (
        layer_out,
        grad_in,
        summed[0],
        summed[1],
        summed[2],
        summed[3],
        summed[4],
        summed[5],
        summed[6],
        summed[7],
        summed[8],
        summed[9],
        summed[10],
        summed[11],
        summed[12],
        summed[13],
        grad_expert_gate,
        grad_expert_up,
        grad_expert_down,
    )


def solution(mesh):
    placed = (
        P("expert", None),
        P("expert"),
        P("expert", None),
        P(),
        P(None, "tensor"),
        P(None, "tensor"),
        P(None, "tensor"),
        P("tensor", None),
        P("tensor", None),
        P("tensor", None),
        P("tensor", None),
        P(),
        P(),
        P(),
        P(None, "tensor"),
        P(None, "tensor"),
        P("tensor", None),
        P("expert", None, "tensor"),
        P("expert", None, "tensor"),
        P("expert", "tensor", None),
        P("expert", None),
    )
    return jax.shard_map(
        on_device,
        mesh=mesh,
        in_specs=placed,
        out_specs=(
            P("expert", None),
            P("expert", None),
            P("expert"),
            P("expert", "tensor"),
            P("expert", "tensor"),
            P("expert", "tensor"),
            P("tensor", "expert"),
            P("tensor", "expert"),
            P("tensor", "expert"),
            P("tensor", "expert"),
            P("expert"),
            P("expert", None),
            P("expert"),
            P("expert", "tensor"),
            P("expert", "tensor"),
            P("tensor", "expert"),
            P("expert", None, "tensor"),
            P("expert", None, "tensor"),
            P("expert", "tensor", None),
        ),
        check_vma=False,
    )
```

profile of v0, /device:TPU:21, one launch (start us, length us, event | category | flops | bytes accessed | tf_op | source)
XLA Modules:
  0.0 2114.2 jit_solution(7408387298047432109)
XLA Ops:
  31.3 4.5 reduce-window.6
  36.6 8.1 scatter_custom_fusion
  44.7 8.1 scatter_custom_fusion.1
  52.8 63.7 %all-reduce.10.cloned.1.call-done = f32[512,2048]{1,0:T(8,128)} async-done(((f32[512,2048]{1,0:T(8,128)}), f32[512,2048]{1,0:T(8,128)}) %all-reduce.10.cloned.1.call-update) | async-done | bytes 4194320 | tf_op jit(solution)/shard_map/psum | solution.py:168
  124.4 17.4 gather_fusion.2
  141.9 25.7 %gather_fusion = bf16[3072,2048]{1,0:T(8,128)(2,1)} fusion(bf16[512,2048]{1,0:T(8,128)(2,1)} %copy-done.2, s32[3072]{0:T(1024)S(1)} %get-tuple-element.66), kind=kCustom, calls=%fused_computation | custom fusion | bytes 25178112 | tf_op jit(solution)/shard_map/gather | solution.py:192
  169.9 72.5 %all_to_all.20 = bf16[8,384,512]{2,1,0:T(8,128)(2,1)} all-to-all(bf16[8,384,512]{2,1,0:T(8,128)(2,1)S(1)} %dynamic-slice_multiply_fusion.1), channel_id=1, replica_groups=mesh['expert'=8,'tensor'=4] {'expert'}, dimensions={0} | all-to-all | bytes 6291456 | tf_op jit(solution)/shard_map/all_to_all | solution.py:105
  243.1 7.0 fusion.96
  250.2 9.5 multiply_convert_fusion.5
  259.7 6.3 multiply_reduce_fusion.3
  266.0 26.5 %gather_fusion.3 = f32[3072,2048]{1,0:T(8,128)} fusion(f32[512,2048]{1,0:T(8,128)} %get-tuple-element.47, s32[3072]{0:T(1024)S(1)} %get-tuple-element.66), kind=kCustom, calls=%fused_computation.3 | custom fusion | bytes 50343936 | tf_op jit(solution)/shard_map/gather | solution.py:216
  295.7 73.8 %all_to_all.21 = bf16[8,384,512]{2,1,0:T(8,128)(2,1)} all-to-all(bf16[8,384,512]{2,1,0:T(8,128)(2,1)S(1)} %fusion.9), channel_id=1, replica_groups=mesh['expert'=8,'tensor'=4] {'expert'}, dimensions={0} | all-to-all | bytes 6291456 | tf_op jit(solution)/shard_map/all_to_all | solution.py:105
  369.6 12.0 fusion.5
  381.7 8.6 fusion.7
  390.3 64.2 %all-gather.5.cloned.1.call-done = bf16[8,384,2048]{2,1,0:T(8,128)(2,1)} async-done(((bf16[8,384,512]{2,1,0:T(8,128)(2,1)}), bf16[8,384,2048]{2,1,0:T(8,128)(2,1)}) %all-gather.5.cloned.1.call-update) | async-done | bytes 12582928 | tf_op jit(solution)/shard_map/all_gather | solution.py:106
  454.5 14.4 fusion.18
  468.9 7.1 convert_bitcast_fusion
  476.1 5.1 copy.122
  481.1 5.6 all-to-all-start.1
  486.7 13.5 fusion.39
  500.3 15.7 fusion
  516.0 10.7 copy.125
  526.7 229.6 %all-to-all-done.1 = bf16[8,384,2048]{2,1,0:T(8,128)(2,1)} async-done(((bf16[8,384,2048]{2,1,0:T(8,128)(2,1)}), bf16[8,384,2048]{2,1,0:T(8,128)(2,1)}, u32[]{:S(2)}, u32[]{:S(2)}) %all-to-all-start.1) | async-done | bytes 12582944 | tf_op jit(solution)/shard_map/all_to_all | solution.py:110
  756.3 8.5 all-to-all-start.3
  766.1 14.4 bitcast_convert_fusion.1
  780.5 24.7 %gather_fusion.1 = f32[2048,2048]{1,0:T(8,128)} fusion(f32[3072,2048]{1,0:T(8,128)} %bitcast_convert_fusion.1, s32[2048]{0:T(1024)S(1)} %broadcast_clamp_fusion), kind=kCustom, calls=%fused_computation.1 | custom fusion | bytes 33562624 | tf_op jit(solution)/shard_map/gather | solution.py:209
  805.2 19.0 reshape.346
  824.2 20.4 multiply_reduce_fusion
  844.6 14.0 all-reduce.3
  859.5 8.1 multiply_convert_fusion.3
  867.6 8.8 fusion.98
  876.3 7.6 fusion.97
  884.0 150.3 %all-to-all-done.3 = bf16[8,384,2048]{2,1,0:T(8,128)(2,1)} async-done(((bf16[8,384,2048]{2,1,0:T(8,128)(2,1)}), bf16[8,384,2048]{2,1,0:T(8,128)(2,1)}, u32[]{:S(2)}, u32[]{:S(2)}) %all-to-all-start.3) | async-done | bytes 12582944 | tf_op jit(solution)/shard_map/all_to_all | solution.py:110
  1034.2 14.4 bitcast_convert_fusion
  1048.6 24.7 %gather_fusion.4 = f32[2048,2048]{1,0:T(8,128)} fusion(f32[3072,2048]{1,0:T(8,128)} %bitcast_convert_fusion, s32[2048]{0:T(1024)S(1)} %broadcast_clamp_fusion), kind=kCustom, calls=%fused_computation.4 | custom fusion | bytes 33562624 | tf_op jit(solution)/shard_map/gather | solution.py:245
  1073.3 19.0 reshape.351
  1092.3 15.1 reduce_sum.223
  1107.4 7.2 add_convert_fusion.2
  1115.7 5.2 add_convert_fusion.4
  1121.2 46.7 %all-reduce.12.cloned.1.call-done = bf16[512,2048]{1,0:T(8,128)(2,1)} async-done(((bf16[512,2048]{1,0:T(8,128)(2,1)}), bf16[512,2048]{1,0:T(8,128)(2,1)}) %all-reduce.12.cloned.1.call-update) | async-done | bytes 2097168 | tf_op jit(solution)/shard_map/psum | solution.py:272
  1197.9 4.9 fusion.100
  1203.8 6.8 add_convert_fusion.1
  1210.7 5.0 convolution_convert_fusion.3
  1215.7 4.5 convolution_convert_fusion.4
  1220.3 4.4 convolution_convert_fusion.5
  1224.8 4.4 convolution_convert_fusion.6
  1229.3 6.7 convolution_convert_fusion.2
  1236.0 6.6 convolution_convert_fusion.1
  1243.1 7.8 convolution_convert_fusion
  1252.8 10.1 convolution_bitcast_fusion
  1262.9 10.5 convolution_bitcast_fusion.1
  1273.5 8.3 fusion.33
  1284.8 48.5 %reduce-scatter.36.cloned.1.call-done = bf16[16,4]{1,0:T(8,128)(2,1)} async-done(((bf16[128,4]{1,0:T(8,128)(2,1)}), bf16[16,4]{1,0:T(8,128)(2,1)}) %reduce-scatter.36.cloned.1.call-update) | async-done | bytes 144
  1334.7 54.9 %reduce-scatter.34.cloned.1.call-done = bf16[16,4]{1,0:T(8,128)(2,1)} async-done(((bf16[128,4]{1,0:T(8,128)(2,1)}), bf16[16,4]{1,0:T(8,128)(2,1)}) %reduce-scatter.34.cloned.1.call-update) | async-done | bytes 144
  1390.9 89.5 %all-reduce.14.cloned.1.call-done = (bf16[512,2048]{1,0:T(8,128)(2,1)}, bf16[512,2048]{1,0:T(8,128)(2,1)}) async-done(((bf16[512,2048]{1,0:T(8,128)(2,1)}, bf16[512,2048]{1,0:T(8,128)(2,1)}), (bf16[512,2048]{1,0:T(8,128)(2,1)}, bf16[512,2048]{1,0:T(8,128)(2,1)})) %all-reduce.14.cloned.1.call-update) | async-done | bytes 4194320 | tf_op jit(solution)/shard_map/psum | solution.py:214
  1484.4 25.0 %all-reduce.4 = (bf16[2048]{0:T(1024)(128)(2,1)S(1)}, bf16[2048]{0:T(1024)(128)(2,1)S(1)}, bf16[2048]{0:T(1024)(128)(2,1)S(1)}) all-reduce(bf16[2048]{0:T(1024)(128)(2,1)S(1)} %get-tuple-element.23, bf16[2048]{0:T(1024)(128)(2,1)S(1)} %get-tuple-element.21, ...), channel_id=2, replica_groups=mesh['expert'=8,'tensor'=4] {'expert'}, use_global_device_ids=true, to_apply=%region_28.29.clone | all-reduce | flops 6144 | bytes 24576
  1511.3 5.2 add_convert_fusion.3
  1520.1 30.3 %reduce-scatter.24.cloned.1.call-done = bf16[512,256]{1,0:T(8,128)(2,1)} async-done(((bf16[512,2048]{1,0:T(8,128)(2,1)}), bf16[512,256]{1,0:T(8,128)(2,1)}) %reduce-scatter.24.cloned.1.call-update) | async-done | bytes 262160 | tf_op jit(solution)/shard_map/reduce_scatter | solution.py:338
  1552.1 68.8 %reduce-scatter.22.cloned.1.call-done = bf16[256,512]{1,0:T(8,128)(2,1)} async-done(((bf16[2048,512]{1,0:T(8,128)(2,1)}), bf16[256,512]{1,0:T(8,128)(2,1)}) %reduce-scatter.22.cloned.1.call-update) | async-done | bytes 262160 | tf_op jit(solution)/shard_map/reduce_scatter | solution.py:326
  1622.9 68.3 %reduce-scatter.20.cloned.1.call-done = bf16[256,512]{1,0:T(8,128)(2,1)} async-done(((bf16[2048,512]{1,0:T(8,128)(2,1)}), bf16[256,512]{1,0:T(8,128)(2,1)}) %reduce-scatter.20.cloned.1.call-update) | async-done | bytes 262160 | tf_op jit(solution)/shard_map/reduce_scatter | solution.py:323
  1693.1 68.8 %reduce-scatter.18.cloned.1.call-done = bf16[256,512]{1,0:T(8,128)(2,1)} async-done(((bf16[2048,512]{1,0:T(8,128)(2,1)}), bf16[256,512]{1,0:T(8,128)(2,1)}) %reduce-scatter.18.cloned.1.call-update) | async-done | bytes 262160 | tf_op jit(solution)/shard_map/reduce_scatter | solution.py:320
  1763.7 113.7 %reduce-scatter.28.cloned.1.call-done = bf16[256,1408]{1,0:T(8,128)(2,1)} async-done(((bf16[2048,1408]{1,0:T(8,128)(2,1)}), bf16[256,1408]{1,0:T(8,128)(2,1)}) %reduce-scatter.28.cloned.1.call-update) | async-done | bytes 720912 | tf_op jit(solution)/shard_map/reduce_scatter | solution.py:350
  1879.6 111.4 %reduce-scatter.30.cloned.1.call-done = bf16[256,1408]{1,0:T(8,128)(2,1)} async-done(((bf16[2048,1408]{1,0:T(8,128)(2,1)}), bf16[256,1408]{1,0:T(8,128)(2,1)}) %reduce-scatter.30.cloned.1.call-update) | async-done | bytes 720912 | tf_op jit(solution)/shard_map/reduce_scatter | solution.py:353
  1993.3 111.9 %reduce-scatter.32.cloned.1.call-done = bf16[1408,256]{1,0:T(8,128)(2,1)} async-done(((bf16[1408,2048]{1,0:T(8,128)(2,1)}), bf16[1408,256]{1,0:T(8,128)(2,1)}) %reduce-scatter.32.cloned.1.call-update) | async-done | bytes 720912 | tf_op jit(solution)/shard_map/reduce_scatter | solution.py:356
  (307 shorter events, 103.5 us)
Async XLA Ops:
  7.2 447.3 %copy-start = (bf16[2,352,2048]{2,1,0:T(8,128)(2,1)S(1)}, bf16[2,352,2048]{2,1,0:T(8,128)(2,1)}, u32[]{:S(2)}) copy-start(bf16[2,352,2048]{2,1,0:T(8,128)(2,1)} %param.40) | copy-start | bytes 8650756
  7.2 109.3 %all-reduce.10.cloned.1.call-start = ((), (), s32[]{:S(2)}) async-start(), calls=%async_computation.15 | async-start | bytes 8388608 | tf_op jit(solution)/shard_map/psum | solution.py:168
  10.2 12.8 copy-start.62
  12.9 10.1 copy-start.49
  13.2 11.3 copy-start.16
  30.0 339.6 %all-gather.3.cloned.1.call-start = ((), (), s32[]{:S(2)}) async-start(), calls=%async_computation.16 | async-start | bytes 15728640 | tf_op jit(solution)/shard_map/all_gather | solution.py:106
  30.9 89.2 %copy-start.45 = (f32[2048]{0:T(1024)}, f32[2048]{0:T(1024)S(1)}, u32[]{:S(2)}) copy-start(f32[2048]{0:T(1024)S(1)} %convert_element_type.289) | copy-start | bytes 24580
  36.6 8.1 copy-start.56
  123.4 18.4 copy-start.51
  123.5 18.4 copy-start.54
  124.2 17.6 copy-start.25
  242.5 212.0 %all-gather.5.cloned.1.call-start = ((), (), s32[]{:S(2)}) async-start(), calls=%async_computation.17 | async-start | bytes 15728640 | tf_op jit(solution)/shard_map/all_gather | solution.py:106
  243.1 16.7 copy-start.67
  243.1 7.1 copy-start.3
  243.1 16.6 slice-start.3
  250.2 9.6 copy-start.78
  250.2 9.6 copy-start.34
  250.2 9.6 slice-start.4
  259.7 6.3 copy-start.74
  369.6 12.1 copy-start.24
  369.6 12.0 copy-start.72
  468.9 7.1 copy-start.77
  481.1 275.2 %all-to-all-start.1 = ((bf16[8,384,2048]{2,1,0:T(8,128)(2,1)}), bf16[8,384,2048]{2,1,0:T(8,128)(2,1)}, u32[]{:S(2)}, u32[]{:S(2)}) async-start(bf16[8,384,2048]{2,1,0:T(8,128)(2,1)} %bitcast.206), calls=%async_computation.1 | async-start | bytes 25165824 | tf_op jit(solution)/shard_map/all_to_all | solution.py:110
  756.3 8.5 copy-start.66
  756.3 9.1 copy-start.57
  756.3 9.1 copy-start.4
  756.3 277.9 %all-to-all-start.3 = ((bf16[8,384,2048]{2,1,0:T(8,128)(2,1)}), bf16[8,384,2048]{2,1,0:T(8,128)(2,1)}, u32[]{:S(2)}, u32[]{:S(2)}) async-start(bf16[8,384,2048]{2,1,0:T(8,128)(2,1)} %bitcast.205), calls=%async_computation.3 | async-start | bytes 25165824 | tf_op jit(solution)/shard_map/all_to_all | solution.py:110
  764.8 403.1 %all-reduce.12.cloned.1.call-start = ((), (), s32[]{:S(2)}) async-start(), calls=%async_computation.18 | async-start | bytes 4194304 | tf_op jit(solution)/shard_map/psum | solution.py:272
  805.2 19.0 copy-start.26
  824.2 20.4 copy-start.71
  824.2 34.6 %copy-start.44 = (s32[512,4]{0,1:T(4,128)S(1)}, s32[512,4]{0,1:T(4,128)}, u32[]{:S(2)}) copy-start(s32[512,4]{0,1:T(4,128)} %param.23) | copy-start | bytes 24580
  824.2 34.6 %copy-start.37 = (f32[512,16]{0,1:T(8,128)S(1)}, f32[512,16]{0,1:T(8,128)}, u32[]{:S(2)}) copy-start(f32[512,16]{0,1:T(8,128)} %copy-done.36) | copy-start | bytes 98308
  824.2 34.6 %copy-start.52 = (f32[512]{0:T(512)S(1)}, f32[512]{0:T(512)}, u32[]{:S(2)}) copy-start(f32[512]{0:T(512)} %copy-done.51) | copy-start | bytes 6148
  824.2 34.6 %copy-start.55 = (f32[512]{0:T(512)S(1)}, f32[512]{0:T(512)}, u32[]{:S(2)}) copy-start(f32[512]{0:T(512)} %copy-done.54) | copy-start | bytes 6148
  824.2 35.2 %copy-start.35 = (bf16[512,2048]{1,0:T(8,128)(2,1)S(1)}, bf16[512,2048]{1,0:T(8,128)(2,1)}, u32[]{:S(2)}) copy-start(bf16[512,2048]{1,0:T(8,128)(2,1)} %param.41) | copy-start | bytes 6291460
  824.2 35.2 %copy-start.68 = (f32[512]{0:T(512)S(1)}, f32[512]{0:T(512)}, u32[]{:S(2)}) copy-start(f32[512]{0:T(512)} %copy-done.67) | copy-start | bytes 6148
  867.5 8.8 copy-start.75
  867.5 8.8 copy-start.76
  1092.3 15.1 copy-start.42
  1092.3 15.1 copy-start.53
  1107.4 7.3 copy-start.5
  1114.6 167.5 %reduce-scatter.26.cloned.1.call-start = ((), (), s32[]{:S(2)}) async-start(), calls=%async_computation.23 | async-start | bytes 73728 | tf_op jit(solution)/shard_map/reduce_scatter | solution.py:344
  1115.7 52.1 %copy-start.46 = (f32[2048]{0:T(1024)S(1)}, f32[2048]{0:T(1024)}, u32[]{:S(2)}) copy-start(f32[2048]{0:T(1024)} %copy-done.45) | copy-start | bytes 24580
  1115.7 52.1 %copy-start.59 = (f32[512]{0:T(512)S(1)}, f32[512]{0:T(512)}, u32[]{:S(2)}) copy-start(f32[512]{0:T(512)} %copy-done.58) | copy-start | bytes 6148
  1120.9 51.2 %copy-start.65 = (f32[512]{0:T(512)S(1)}, f32[512]{0:T(512)}, u32[]{:S(2)}) copy-start(f32[512]{0:T(512)} %copy-done.64) | copy-start | bytes 6148
  1121.0 162.5 %reduce-scatter.38.cloned.1.call-start = ((), (), s32[]{:S(2)}) async-start(), calls=%async_computation.29 | async-start | bytes 36864
  1190.7 142.6 %reduce-scatter.36.cloned.1.call-start = ((), (), s32[]{:S(2)}) async-start(), calls=%async_computation.28 | async-start | bytes 36864
  1197.8 191.8 %reduce-scatter.34.cloned.1.call-start = ((), (), s32[]{:S(2)}) async-start(), calls=%async_computation.27 | async-start | bytes 36864
  1203.5 276.9 %all-reduce.14.cloned.1.call-start = ((), (), s32[]{:S(2)}) async-start(), calls=%async_computation.30 | async-start | bytes 8388608 | tf_op jit(solution)/shard_map/psum | solution.py:214
  1210.6 339.7 %reduce-scatter.24.cloned.1.call-start = ((), (), s32[]{:S(2)}) async-start(), calls=%async_computation.22 | async-start | bytes 2359296 | tf_op jit(solution)/shard_map/reduce_scatter | solution.py:338
  1215.7 405.3 %reduce-scatter.22.cloned.1.call-start = ((), (), s32[]{:S(2)}) async-start(), calls=%async_computation.21 | async-start | bytes 2359296 | tf_op jit(solution)/shard_map/reduce_scatter | solution.py:326
  1220.3 471.0 %reduce-scatter.20.cloned.1.call-start = ((), (), s32[]{:S(2)}) async-start(), calls=%async_computation.20 | async-start | bytes 2359296 | tf_op jit(solution)/shard_map/reduce_scatter | solution.py:323
  1224.7 537.1 %reduce-scatter.18.cloned.1.call-start = ((), (), s32[]{:S(2)}) async-start(), calls=%async_computation.19 | async-start | bytes 2359296 | tf_op jit(solution)/shard_map/reduce_scatter | solution.py:320
  1229.2 648.1 %reduce-scatter.28.cloned.1.call-start = ((), (), s32[]{:S(2)}) async-start(), calls=%async_computation.24 | async-start | bytes 6488064 | tf_op jit(solution)/shard_map/reduce_scatter | solution.py:350
  1236.0 755.0 %reduce-scatter.30.cloned.1.call-start = ((), (), s32[]{:S(2)}) async-start(), calls=%async_computation.25 | async-start | bytes 6488064 | tf_op jit(solution)/shard_map/reduce_scatter | solution.py:353
  1242.7 862.5 %reduce-scatter.32.cloned.1.call-start = ((), (), s32[]{:S(2)}) async-start(), calls=%async_computation.26 | async-start | bytes 6488064 | tf_op jit(solution)/shard_map/reduce_scatter | solution.py:356
  1252.8 10.1 copy-start.19
  1252.8 20.6 slice-start
  1252.8 20.6 slice-start.1
  1262.9 10.5 slice-start.2
  1273.5 8.3 copy-start.70
  1281.7 229.5 %copy-start.61 = (f32[512]{0:T(512)S(1)}, f32[512]{0:T(512)}, u32[]{:S(2)}) copy-start(f32[512]{0:T(512)} %copy-done.60) | copy-start | bytes 6148
  1511.3 6.2 copy-start.15
  1621.0 486.5 %copy-start.1 = (bf16[2,352,2048]{2,1,0:T(8,128)(2,1)S(1)}, bf16[2,352,2048]{2,1,0:T(8,128)(2,1)}, u32[]{:S(2)}) copy-start(bf16[2,352,2048]{2,1,0:T(8,128)(2,1)} %param.40) | copy-start | bytes 8650756
  (38 other events, 116.1 us)
Sparse Core Ops, SparseCore 0:
  30.1 86.3 all-reduce.9
  242.6 84.6 all-gather.2
  369.7 84.7 all-gather.4
  1114.8 53.0 all-reduce.11
  1170.8 50.6 reduce-scatter.25
  1224.5 52.5 reduce-scatter.37
  1280.8 52.5 reduce-scatter.35
  1337.0 52.5 reduce-scatter.33
  1392.6 87.7 all-reduce.13
  1484.2 66.1 reduce-scatter.23
  1554.3 66.6 reduce-scatter.21
  1624.8 66.4 reduce-scatter.19
  1695.2 66.5 reduce-scatter.17
  1765.8 111.4 reduce-scatter.27
  1881.2 109.7 reduce-scatter.29
  1995.0 110.1 reduce-scatter.31
where the time goes:
time: 2130 us; the launch traced here: 2110 us
  waiting for transfers between devices  1320 us (62%)
  matrix products  233 us (11%)
  local copies, waits for them, and re-layouts  204 us (10%)
  blocking collectives  185 us (9%)
  other arithmetic  138 us (6%)
    all_to_all x2, waiting for transfers between devices, return_rows(): lax.all_to_all(owner_rows.astype(jnp.bfloat16), 'expert', split_axis=0, c...  380 us
    all_to_all x2, blocking collectives, send_tokens(): lax.all_to_all(columns, 'expert', split_axis=0, concat_axis=0, tiled=True)  146 us
    reduce_scatter x1, waiting for transfers between devices, on_device(): lax.psum_scatter(grad_shared_gate.astype(jnp.bfloat16), 'expert', scatter...  114 us
    reduce_scatter x1, waiting for transfers between devices, on_device(): lax.psum_scatter(grad_shared_down.astype(jnp.bfloat16), 'expert', scatter...  112 us
    reduce_scatter x1, waiting for transfers between devices, on_device(): lax.psum_scatter(grad_shared_up.astype(jnp.bfloat16), 'expert', scatter_d...  111 us
    unnamed x19, waiting for transfers between devices  104 us
    psum x1, waiting for transfers between devices, on_device(): lax.psum(ffn_part.astype(jnp.bfloat16), 'tensor').astype(jnp.float32)  89.5 us
    reduce_scatter x1, waiting for transfers between devices, on_device(): lax.psum_scatter(grad_w_value.astype(jnp.bfloat16), 'expert', scatter_dim...  68.8 us
  transfers between devices with their start and end apart: 18, of which 15 were waited for; matrix products, arithmetic and copies ran while one was open for 18% of the time, Pallas kernels for 0%

commit v1 on v0

v1 whole, which is shorter than its diff:
```python
import functools
import math

import jax
import jax.numpy as jnp
from jax import lax
from jax.experimental import pallas as pl
from jax.experimental.pallas import tpu as pltpu
from jax.sharding import PartitionSpec as P

rope_base = 1000000.0
norm_eps = 1e-06
f32 = jnp.float32
bf16 = jnp.bfloat16
whole = pl.BlockSpec(memory_space=pltpu.VMEM)
in_place = pl.BlockSpec(memory_space=pl.ANY)


def rms_scale(values):
    return lax.rsqrt(jnp.mean(values * values, axis=-1, keepdims=True) + norm_eps)


def matmul(left, right):
    return jnp.dot(left, right, preferred_element_type=f32)


def contract_rows(left, right):
    return lax.dot_general(left, right, (((0,), (0,)), ((), ())), preferred_element_type=f32)


def times_transposed(left, right):
    return lax.dot_general(left, right, (((1,), (1,)), ((), ())), preferred_element_type=f32)


def rotate(values):
    half_width = values.shape[-1] // 2
    return jnp.concatenate([-values[..., half_width:], values[..., :half_width]], axis=-1)


def flip_bit(value, bit):
    return value + bit * (1 - 2 * lax.rem(lax.div(value, bit), 2))


class Peers:
    def __init__(self, groups, lanes):
        self.groups, self.lanes = groups, lanes
        self.far = groups // 2
        self.chips = lanes // 2
        self.group = lax.axis_index("expert")
        self.lane = lax.axis_index("tensor")
        self.core = lax.rem(self.lane, 2)
        self.chip = lax.div(self.lane, 2)
        if groups == 8:
            z, y = lax.div(self.group, 2), lax.rem(self.group, 2)
            self.place = z + y * (7 - 2 * z)
        else:
            self.place = self.group

    def group_at(self, offset):
        place = lax.rem(self.place + (offset + self.groups), self.groups)
        if self.groups == 8:
            y = lax.div(place, 4)
            return 2 * (place + y * (7 - 2 * place)) + y
        return place

    def at(self, offset):
        return (self.group_at(offset), self.lane)

    def other_core(self):
        return (self.group, self.lane + 1 - 2 * self.core)

    def chip_bits(self):
        return [1 << i for i in range(self.chips.bit_length() - 1)]

    def other_chip(self, bit):
        return (self.group, 2 * flip_bit(self.chip, bit) + self.core)

    def offsets(self):
        return [0] + [s * k for k in range(1, self.far) for s in (1, -1)] + [self.far]

    def meet(self, peers):
        barrier = pltpu.get_barrier_semaphore()
        for peer in peers:
            pl.semaphore_signal(
                barrier, inc=1, device_id=peer, device_id_type=pl.DeviceIdType.MESH
            )
        pl.semaphore_wait(barrier, len(peers))


class Copies:
    def __init__(self, send_sems, recv_sems):
        self.send_sems, self.recv_sems = send_sems, recv_sems
        self.started = []
        self.count = 0

    def start(self, source, target, peer, arriving=None):
        index = self.count
        self.count += 1

        def copy(source, target):
            return pltpu.make_async_remote_copy(
                src_ref=source,
                dst_ref=target,
                send_sem=self.send_sems.at[index],
                recv_sem=self.recv_sems.at[index],
                device_id=peer,
                device_id_type=pl.DeviceIdType.MESH,
            )

        mine = copy(source, target)
        mine.start()
        self.started.append(mine)
        arriving = target if arriving is None else arriving
        return copy(arriving, arriving).wait_recv

    def finish(self):
        for copy in self.started:
            copy.wait_send()


def tiles(rows, size, step):
    def body(i, carry):
        step(pl.ds(pl.multiple_of(i * size, size), size))
        return carry

    lax.fori_loop(0, rows // size, body, 0)


def gather_kernel(
    groups, lanes, part, hidden, gain, grad, ids,
    resid, normed, tokens_all, grads_all, ids_all,
    total, from_core, from_chip, send_sems, recv_sems, local_sems,
):
    peers = Peers(groups, lanes)
    far, bits = peers.far, peers.chip_bits()
    seq, _ = grad.shape
    half = seq // 2
    piece = seq // lanes
    half_rows = pl.ds(pl.multiple_of(peers.core * half, half), half)
    other_rows = pl.ds(pl.multiple_of((1 - peers.core) * half, half), half)
    first = pl.multiple_of((peers.core * peers.chips + peers.chip) * piece, piece)
    me = peers.group
    others = [k for k in peers.offsets() if k != 0]
    peers.meet(
        [peers.at(k) for k in others]
        + [peers.other_core()]
        + [peers.other_chip(b) for b in bits]
    )
    copies = Copies(send_sems, recv_sems)

    own_grad = pltpu.make_async_copy(grad, grads_all.at[me], local_sems.at[0])
    own_grad.start()

    def hop(array, k, start, size, source=None):
        held = peers.group_at(k + 1 if k < 0 else k - 1)
        rows = pl.ds(pl.multiple_of(start, size), size)
        return copies.start(
            array.at[held, rows] if source is None else source,
            array.at[held, rows],
            peers.at(1) if k < 0 else peers.at(-1),
            array.at[peers.group_at(k), rows],
        )

    def chip_swap(array, k, bit):
        slot = peers.group_at(k)
        size = bit * piece
        start = (peers.core * peers.chips + lax.div(peers.chip, bit) * bit) * piece
        theirs = (peers.core * peers.chips + lax.div(flip_bit(peers.chip, bit), bit) * bit) * piece
        rows = pl.ds(pl.multiple_of(start, size), size)
        arriving = pl.ds(pl.multiple_of(theirs, size), size)
        return copies.start(
            array.at[slot, rows], array.at[slot, rows], peers.other_chip(bit),
            array.at[slot, arriving],
        )

    def core_swap(array, k, source=None):
        slot = peers.group_at(k)
        return copies.start(
            array.at[slot, half_rows] if source is None else source,
            array.at[slot, half_rows],
            peers.other_core(),
            array.at[slot, other_rows],
        )

    ids_all[me] = ids[...]
    late = [
        copies.start(ids, ids_all.at[me], peers.at(k), ids_all.at[peers.group_at(-k)])
        for k in others
    ]
    own_piece = grad.at[pl.ds(first, piece)]
    g_ring = {k: hop(grads_all, k, first, piece, own_piece) for k in (-1, 1)}
    got_core = copies.start(part.at[other_rows], from_core, peers.other_core())
    got_core()
    start_of_half = peers.core * half

    def add_core(rows):
        mine = pl.ds(pl.multiple_of(start_of_half + rows.start, rows.size), rows.size)
        both = part[mine, :].astype(f32) + from_core[rows, :].astype(f32)
        total[rows, :] = both.astype(bf16)

    tiles(half, 32, add_core)
    got_chip = copies.start(total, from_chip.at[0], peers.other_chip(bits[0]))
    chip_copy = copies.started.pop()
    for k in range(2, far):
        for s in (-1, 1):
            g_ring[s * (k - 1)]()
            g_ring[s * k] = hop(grads_all, s * k, first, piece)
        if k == 2:
            got_chip()
            for i, bit in enumerate(bits):

                def add_chip(rows, i=i):
                    both = total[rows, :].astype(f32) + from_chip[i, rows, :].astype(f32)
                    if i + 1 < len(bits):
                        total[rows, :] = both.astype(bf16)
                        return
                    both = hidden[rows, :].astype(f32) + both
                    resid[rows, :] = both
                    normed[rows, :] = (both * rms_scale(both) * gain[...]).astype(bf16)

                chip_copy.wait_send()
                tiles(half, 32, add_chip)
                if i + 1 < len(bits):
                    copies.start(total, from_chip.at[i + 1], peers.other_chip(bits[i + 1]))()
                    chip_copy = copies.started.pop()
            x_ring = {k2: hop(tokens_all, k2, start_of_half, half, normed) for k2 in (-1, 1)}
            late.append(core_swap(tokens_all, 0, normed))
            own_rows = pltpu.make_async_copy(
                normed, tokens_all.at[me, half_rows], local_sems.at[1]
            )
            own_rows.start()
    for s in (-1, 1):
        g_ring[s * (far - 1)]()
    ahead_half = hop(grads_all, -far, first, piece // 2)
    back_half = hop(grads_all, far, first + piece // 2, piece // 2)
    order = [s * k for k in range(1, far) for s in (-1, 1)] + [far]
    swaps = {k: chip_swap(grads_all, k, bits[0]) for k in order[:-1]}
    ahead_half()
    back_half()
    swaps[far] = chip_swap(grads_all, far, bits[0])

    def finish_grads(ks):
        for k in ks:
            swaps[k]()
            for bit in bits[1:]:
                chip_swap(grads_all, k, bit)()
            late.append(core_swap(grads_all, k))

    for k in range(2, far):
        finish_grads([-(k - 1), k - 1])
        for s in (-1, 1):
            x_ring[s * (k - 1)]()
            x_ring[s * k] = hop(tokens_all, s * k, start_of_half, half)
            late.append(core_swap(tokens_all, s * (k - 1)))
    for s in (-1, 1):
        x_ring[s * (far - 1)]()
    ahead_half = hop(tokens_all, -far, start_of_half, half // 2)
    back_half = hop(tokens_all, far, start_of_half + half // 2, half // 2)
    for s in (-1, 1):
        late.append(core_swap(tokens_all, s * (far - 1)))
    finish_grads([1 - far, far - 1, far])
    ahead_half()
    back_half()
    late.append(core_swap(tokens_all, far))
    for wait in late:
        wait()
    own_grad.wait()
    own_rows.wait()
    copies.finish()


def gather_tokens(groups, lanes, part, hidden_half, gain, grad, ids):
    seq, width = grad.shape
    half = seq // 2
    bits = (lanes // 2).bit_length() - 1
    copies = 2 * groups + 2 + bits + groups * (bits + 4)
    return pl.pallas_call(
        functools.partial(gather_kernel, groups, lanes),
        out_shape=(
            jax.ShapeDtypeStruct((half, width), f32),
            jax.ShapeDtypeStruct((half, width), bf16),
            jax.ShapeDtypeStruct((groups, seq, width), bf16),
            jax.ShapeDtypeStruct((groups, seq, width), bf16),
            jax.ShapeDtypeStruct((groups,) + ids.shape, jnp.int32),
        ),
        in_specs=[whole, whole, whole, in_place, whole],
        out_specs=(whole, whole, in_place, in_place, whole),
        scratch_shapes=[
            pltpu.VMEM((half, width), bf16),
            pltpu.VMEM((half, width), bf16),
            pltpu.VMEM((max(bits, 1), half, width), bf16),
            pltpu.SemaphoreType.DMA((copies,)),
            pltpu.SemaphoreType.DMA((copies,)),
            pltpu.SemaphoreType.DMA((2,)),
        ],
        compiler_params=pltpu.CompilerParams(
            collective_id=0, has_side_effects=True, vmem_limit_bytes=40 * 1024 * 1024
        ),
        name="gather_tokens",
    )(part, hidden_half, gain, grad, ids)


def reduce_kernel(
    groups, lanes, tokens, parts, small,
    total, small_total,
    kept, from_core, from_ring, from_chip, small_in, small_swap,
    send_sems, recv_sems, local_sems,
):
    peers = Peers(groups, lanes)
    far, bits = peers.far, peers.chip_bits()
    rows_all = kept.shape[1]
    half = rows_all // 2
    me = peers.group
    offsets = [far] + [s * k for k in range(far - 1, 0, -1) for s in (1, -1)] + [0]
    number = {k: i for i, k in enumerate(offsets)}
    others = [k for k in offsets if k != 0]
    peers.meet(
        [peers.at(k) for k in others]
        + [peers.other_core()]
        + [peers.other_chip(b) for b in bits]
    )
    copies = Copies(send_sems, recv_sems)
    if tokens:
        keep_rows = pl.ds(pl.multiple_of(peers.core * rows_all, rows_all), rows_all)
        give_rows = pl.ds(pl.multiple_of((1 - peers.core) * rows_all, rows_all), rows_all)
    loads, given = {}, {}
    for k in offsets:
        slot = peers.group_at(k)
        source = parts.at[slot, keep_rows] if tokens else parts.at[slot]
        loads[k] = pltpu.make_async_copy(source, kept.at[number[k]], local_sems.at[number[k]])
        loads[k].start()
        if tokens:
            given[k] = copies.start(
                parts.at[slot, give_rows], from_core.at[number[k]], peers.other_core()
            )
    small_got = [
        copies.start(small.at[peers.group_at(k)], small_in.at[number[k]], peers.at(k))
        for k in others
    ]

    def ready(k):
        loads[k].wait()
        if tokens:
            given[k]()

    def add(k, start, size, arrived=None):
        i = number[k]

        def step(rows):
            at = pl.ds(pl.multiple_of(start + rows.start, rows.size), rows.size)
            value = kept[i, at, :].astype(f32)
            if tokens:
                value = value + from_core[i, at, :].astype(f32)
            if arrived is not None:
                value = value + from_ring[arrived, at, :].astype(f32)
            kept[i, at, :] = value.astype(bf16)

        tiles(size, 32, step)

    def send(k, start, size, ahead, arriving):
        rows = pl.ds(start, size)
        return copies.start(
            kept.at[number[k], rows],
            from_ring.at[arriving, rows],
            peers.at(1) if ahead else peers.at(-1),
        )

    ready(far)
    add(far, 0, half)
    up = send(far, 0, half, True, 0)
    add(far, half, half)
    down = send(far, half, half, False, 0)
    up_at = down_at = 0
    for k in range(far - 1, 0, -1):
        ready(k)
        ready(-k)
        if k == far - 1:
            add(k, half, half)
            add(-k, 0, half)
            up()
            add(k, 0, half, up_at)
        else:
            up()
            add(k, 0, rows_all, up_at)
        up = send(k, 0, rows_all, True, 2 * (far - k) - 1)
        down()
        if k == far - 1:
            add(-k, half, half, down_at)
        else:
            add(-k, 0, rows_all, down_at)
        down = send(-k, 0, rows_all, False, 2 * (far - k))
        up_at, down_at = 2 * (far - k) - 1, 2 * (far - k)
    ready(0)

    for wait in small_got:
        wait()
    small_sum = small[me]
    for k in others:
        small_sum = small_sum + small_in[number[k]]
    small_total[...] = small_sum
    for i, peer in enumerate([peers.other_core()] + [peers.other_chip(b) for b in bits]):
        small_swap[2 * i] = small_total[...]
        copies.start(small_swap.at[2 * i], small_swap.at[2 * i + 1], peer)()
        small_total[...] = small_swap[2 * i] + small_swap[2 * i + 1]

    up()
    down()
    home = number[0]

    def last(rows):
        value = kept[home, rows, :].astype(f32)
        if tokens:
            value = value + from_core[home, rows, :].astype(f32)
        value = value + from_ring[up_at, rows, :].astype(f32)
        value = value + from_ring[down_at, rows, :].astype(f32)
        if tokens:
            kept[home, rows, :] = value.astype(bf16)
        else:
            total[rows, :] = value

    tiles(rows_all, 32, last)
    if tokens:
        for i, bit in enumerate(bits):
            wait = copies.start(kept.at[home], from_chip.at[i], peers.other_chip(bit))
            wait()
            copies.started.pop().wait_send()

            def join(rows, i=i):
                value = kept[home, rows, :].astype(f32) + from_chip[i, rows, :].astype(f32)
                if i + 1 < len(bits):
                    kept[home, rows, :] = value.astype(bf16)
                else:
                    total[rows, :] = value

            tiles(rows_all, 32, join)
    copies.finish()


def reduce_parts(groups, lanes, parts, small, tokens, collective_id):
    rows = parts.shape[1] // 2 if tokens else parts.shape[1]
    width = parts.shape[2]
    bits = (lanes // 2).bit_length() - 1
    far = groups // 2
    copies = (groups if tokens else 0) + (groups - 1) + 2 * far + (1 + bits) + bits
    shape = (rows, width)
    return pl.pallas_call(
        functools.partial(reduce_kernel, groups, lanes, tokens),
        out_shape=(
            jax.ShapeDtypeStruct(shape, f32),
            jax.ShapeDtypeStruct(small.shape[1:], f32),
        ),
        in_specs=[in_place, whole],
        out_specs=(whole, whole),
        scratch_shapes=[
            pltpu.VMEM((groups,) + shape, bf16),
            pltpu.VMEM(((groups if tokens else 1),) + shape, bf16),
            pltpu.VMEM((2 * far - 1,) + shape, bf16),
            pltpu.VMEM(((max(bits, 1) if tokens else 1),) + shape, bf16),
            pltpu.VMEM(small.shape, f32),
            pltpu.VMEM((2 * (1 + bits),) + small.shape[1:], f32),
            pltpu.SemaphoreType.DMA((copies,)),
            pltpu.SemaphoreType.DMA((copies,)),
            pltpu.SemaphoreType.DMA((groups,)),
        ],
        compiler_params=pltpu.CompilerParams(
            collective_id=collective_id,
            has_side_effects=True,
            vmem_limit_bytes=58 * 1024 * 1024,
        ),
        name="reduce_tokens" if tokens else "reduce_weights",
    )(parts, small)


def attend_forward(query, key, value, allowed, score_scale):
    scores = jnp.einsum("qhd,khd->hqk", query, key, preferred_element_type=f32) * score_scale
    scores = jnp.where(allowed[None], scores, -1e30)
    highest = jnp.max(scores, axis=-1, keepdims=True)
    log_total = highest + jnp.log(jnp.sum(jnp.exp(scores - highest), axis=-1, keepdims=True))
    probs = jnp.exp(scores - log_total)
    contexts = jnp.einsum("hqk,khd->qhd", probs.astype(bf16), value, preferred_element_type=f32)
    return contexts.astype(bf16), log_total


def attend_backward(query, key, value, d_context, log_total, allowed, score_scale):
    scores = jnp.einsum("qhd,khd->hqk", query, key, preferred_element_type=f32) * score_scale
    probs = jnp.exp(jnp.where(allowed[None], scores, -1e30) - log_total)
    d_probs = jnp.einsum("qhd,khd->hqk", d_context, value, preferred_element_type=f32)
    row_dot = jnp.sum(probs * d_probs, axis=-1, keepdims=True)
    d_scores = (probs * (d_probs - row_dot)).astype(bf16)
    d_query = jnp.einsum("hqk,khd->qhd", d_scores, key, preferred_element_type=f32) * score_scale
    d_key = jnp.einsum("hqk,qhd->khd", d_scores, query, preferred_element_type=f32) * score_scale
    d_value = jnp.einsum("hqk,qhd->khd", probs.astype(bf16), d_context, preferred_element_type=f32)
    return d_query, d_key, d_value


def norm_backward(values, scale, gain, d_normed):
    inner = d_normed * gain
    mean = jnp.mean(inner * values, axis=-1, keepdims=True)
    return scale * inner - values * (scale * scale * scale) * mean


def gated_backward(a, b, d_hidden):
    sigma = jax.nn.sigmoid(a)
    d_a = (d_hidden * b * sigma * (1.0 + a * (1.0 - sigma))).astype(bf16)
    d_b = (d_hidden * a * sigma).astype(bf16)
    return d_a, d_b


class Experts:
    def __init__(self, weights, router, w_sigmoid, first_expert, capacity):
        (self.gate, self.up, self.down, self.s_gate, self.s_up, self.s_down) = weights
        self.router = router
        self.w_sigmoid = w_sigmoid
        self.first = first_expert
        self.capacity = capacity

    def run(self, tokens, grads, ids):
        held = self.gate.shape[0]
        m, s, d = tokens.shape
        local = jnp.arange(held, dtype=jnp.int32) + self.first
        named = jnp.any(ids[:, None, :, :] == local[None, :, None, None], axis=2)
        earlier = (jnp.arange(s)[:, None] < jnp.arange(s)[None, :]).astype(bf16)
        rank = jnp.einsum(
            "met,tu->meu", named.astype(bf16), earlier, preferred_element_type=f32
        ).astype(jnp.int32)
        place = jnp.where(named, rank, -1)
        pick = (
            place[:, :, None, :] == jnp.arange(self.capacity, dtype=jnp.int32)[None, None, :, None]
        )
        pick_flat = pick.astype(bf16).reshape(m, held * self.capacity, s)
        shape4 = (m, held, self.capacity, d)
        rows = jnp.einsum("mrt,mtd->mrd", pick_flat, tokens, preferred_element_type=f32)
        rows = rows.astype(bf16).reshape(shape4)
        row_grads = jnp.einsum("mrt,mtd->mrd", pick_flat, grads, preferred_element_type=f32)
        row_grads = row_grads.astype(bf16).reshape(shape4)
        logits = jnp.einsum("mtd,de->mte", tokens, self.router, preferred_element_type=f32)
        probs = jax.nn.softmax(logits, axis=-1)
        mine = lax.dynamic_slice_in_dim(probs, self.first, held, 2)
        gate_rows = jnp.sum(
            jnp.where(pick, jnp.swapaxes(mine, 1, 2)[:, :, None, :], 0.0), axis=-1, keepdims=True
        )
        sig = jax.nn.sigmoid(
            jnp.einsum("mtd,d->mt", tokens, self.w_sigmoid, preferred_element_type=f32)
        )[:, :, None]
        a = jnp.einsum("mecd,edf->mecf", rows, self.gate, preferred_element_type=f32)
        b = jnp.einsum("mecd,edf->mecf", rows, self.up, preferred_element_type=f32)
        u = jnp.einsum("mecd,efd->mecf", row_grads, self.down, preferred_element_type=f32)
        hidden = (jax.nn.silu(a) * b).astype(bf16).astype(f32)
        d_gate_rows = jnp.sum(hidden * u, axis=-1, keepdims=True)
        gated_hidden = (hidden * gate_rows).astype(bf16)
        d_a, d_b = gated_backward(a, b, u * gate_rows)
        out_rows = jnp.einsum(
            "mecf,efd->mecd", gated_hidden, self.down, preferred_element_type=f32
        ).astype(bf16)
        in_rows = (
            jnp.einsum("mecf,edf->mecd", d_a, self.gate, preferred_element_type=f32)
            + jnp.einsum("mecf,edf->mecd", d_b, self.up, preferred_element_type=f32)
        ).astype(bf16)
        s_a = jnp.einsum("mtd,df->mtf", tokens, self.s_gate, preferred_element_type=f32)
        s_b = jnp.einsum("mtd,df->mtf", tokens, self.s_up, preferred_element_type=f32)
        s_u = jnp.einsum("mtd,fd->mtf", grads, self.s_down, preferred_element_type=f32)
        s_hidden = (jax.nn.silu(s_a) * s_b).astype(bf16).astype(f32)
        d_sig = jnp.sum(s_hidden * s_u, axis=-1)
        s_gated = (s_hidden * sig).astype(bf16)
        s_d_a, s_d_b = gated_backward(s_a, s_b, s_u * sig)
        flat = (m, held * self.capacity, d)
        outs = jnp.einsum(
            "mrt,mrd->mtd", pick_flat, out_rows.reshape(flat), preferred_element_type=f32
        ) + jnp.einsum("mtf,fd->mtd", s_gated, self.s_down, preferred_element_type=f32)
        d_in = (
            jnp.einsum("mrt,mrd->mtd", pick_flat, in_rows.reshape(flat), preferred_element_type=f32)
            + jnp.einsum("mtf,df->mtd", s_d_a, self.s_gate, preferred_element_type=f32)
            + jnp.einsum("mtf,df->mtd", s_d_b, self.s_up, preferred_element_type=f32)
        )
        d_gates = jnp.sum(jnp.where(pick, d_gate_rows, 0.0), axis=2)
        saved = (rows, row_grads, gated_hidden, d_a, d_b, tokens, grads, s_gated, s_d_a, s_d_b)
        return outs.astype(bf16), d_in.astype(bf16), d_gates, d_sig, saved

    def weight_grads(self, saved):
        rows, row_grads, gated_hidden, d_a, d_b, tokens, grads, s_gated, s_d_a, s_d_b = saved
        return (
            jnp.einsum("mecd,mecf->edf", rows, d_a, preferred_element_type=f32),
            jnp.einsum("mecd,mecf->edf", rows, d_b, preferred_element_type=f32),
            jnp.einsum("mecf,mecd->efd", gated_hidden, row_grads, preferred_element_type=f32),
            jnp.einsum("mtd,mtf->df", tokens, s_d_a, preferred_element_type=f32),
            jnp.einsum("mtd,mtf->df", tokens, s_d_b, preferred_element_type=f32),
            jnp.einsum("mtf,mtd->fd", s_gated, grads, preferred_element_type=f32),
        )


def on_device(
    hidden_in,
    seq_lengths,
    expert_ids,
    attn_gain,
    w_query,
    w_key,
    w_value,
    b_query,
    b_key,
    b_value,
    w_output,
    ffn_gain,
    w_router,
    w_sigmoid,
    shared_gate,
    shared_up,
    shared_down,
    expert_gate,
    expert_up,
    expert_down,
    out_grad,
):
    seq, width = hidden_in.shape
    heads, head_width = b_query.shape
    head_all = heads * head_width
    top_count = expert_ids.shape[1]
    experts_all = w_router.shape[1]
    held = expert_gate.shape[0]
    groups = lax.axis_size("expert")
    lane_count = lax.axis_size("tensor")
    group = lax.axis_index("expert")
    lane = lax.axis_index("tensor")
    capacity = 3 * seq * top_count // (2 * experts_all)
    score_scale = 1.0 / math.sqrt(head_width)
    length = seq_lengths[0]
    half = seq // 2
    features = width // groups
    half_start = (lane % 2) * half

    def half_of(array):
        return lax.dynamic_slice_in_dim(array, half_start, half, 0)

    def swap(values, bit):
        return lax.ppermute(values, "tensor", [(i, i ^ bit) for i in range(lane_count)])

    def sum_lanes(values):
        other = lax.dynamic_slice_in_dim(values, half - half_start, half, 0)
        total = (half_of(values).astype(f32) + swap(other, 1).astype(f32)).astype(bf16)
        for bit in range(1, (lane_count // 2).bit_length()):
            total32 = total.astype(f32) + swap(total, 1 << bit).astype(f32)
            total = total32.astype(bf16)
        return total32

    def both_halves(mine):
        other = swap(mine, 1)
        lower = jnp.where(half_start == 0, mine, other)
        upper = jnp.where(half_start == 0, other, mine)
        return jnp.concatenate([lower, upper], axis=0)

    hidden = hidden_in.astype(f32)
    position = jnp.arange(seq, dtype=jnp.int32)
    grad_low = jnp.where((position < length)[:, None], out_grad, jnp.zeros_like(out_grad))

    gain_attn = attn_gain.astype(f32)
    attn_scale = rms_scale(hidden)
    normed_attn = (hidden * attn_scale * gain_attn).astype(bf16)
    freq = jnp.exp(
        jnp.arange(head_width // 2, dtype=f32) * (-2.0 * math.log(rope_base) / head_width)
    )
    angle = position.astype(f32)[:, None] * freq[None, :]
    angle = jnp.concatenate([angle, angle], axis=1)
    cosine, sine = jnp.cos(angle)[:, None, :], jnp.sin(angle)[:, None, :]
    by_head = (seq, heads, head_width)
    query_pre = (matmul(normed_attn, w_query) + b_query.reshape(-1).astype(f32)).reshape(by_head)
    key_pre = (matmul(normed_attn, w_key) + b_key.reshape(-1).astype(f32)).reshape(by_head)
    value_pre = matmul(normed_attn, w_value) + b_value.reshape(-1).astype(f32)
    query = (query_pre * cosine + rotate(query_pre) * sine).astype(bf16)
    key = (key_pre * cosine + rotate(key_pre) * sine).astype(bf16)
    value = value_pre.astype(bf16).reshape(by_head)
    allowed = (position[None, :] <= position[:, None]) & (position[None, :] < length)
    context, log_total = attend_forward(query, key, value, allowed, score_scale)
    context_flat = context.reshape(seq, head_all)
    gain_ffn = ffn_gain.astype(f32)
    ids = jnp.pad(expert_ids.T, ((0, -top_count % 8), (0, 0)), constant_values=-1)
    resid, normed, tokens_all, grads_all, ids_all = gather_tokens(
        groups,
        lane_count,
        matmul(context_flat, w_output).astype(bf16),
        half_of(hidden_in),
        gain_ffn[None, :],
        grad_low,
        ids,
    )

    ffn_scale = rms_scale(resid)
    logits = matmul(normed, w_router)
    route_probs = jax.nn.softmax(logits, axis=-1)
    sig = jax.nn.sigmoid(jnp.dot(normed, w_sigmoid, preferred_element_type=f32))

    units = shared_gate.shape[1] // groups
    experts = Experts(
        (
            expert_gate,
            expert_up,
            expert_down,
            lax.dynamic_slice_in_dim(shared_gate, group * units, units, 1),
            lax.dynamic_slice_in_dim(shared_up, group * units, units, 1),
            lax.dynamic_slice_in_dim(shared_down, group * units, units, 0),
        ),
        w_router,
        w_sigmoid,
        group * held,
        capacity,
    )
    outs, d_in, d_gates, d_sig, saved = experts.run(tokens_all, grads_all, ids_all[:, :top_count])
    g_gate, g_up, g_down, g_s_gate, g_s_up, g_s_down = experts.weight_grads(saved)

    spread = (
        (group * held + jnp.arange(held))[:, None] == jnp.arange(experts_all)[None, :]
    ).astype(f32)
    small = jnp.concatenate(
        [
            jnp.sum(d_gates[:, :, None, :] * spread[None, :, :, None], axis=1),
            d_sig[:, None, :],
            jnp.zeros((groups, -(experts_all + 1) % 8, seq), f32),
        ],
        axis=1,
    )
    d_in_sum, small = reduce_parts(groups, lane_count, d_in, small, True, 1)
    small = half_of(small.T)
    d_probs_route, sig_grad = small[:, :experts_all], small[:, experts_all]
    d_logits = (
        route_probs
        * (d_probs_route - jnp.sum(route_probs * d_probs_route, axis=-1, keepdims=True))
    ).astype(bf16)
    d_sig_logit = (sig_grad * sig * (1.0 - sig)).astype(bf16)
    d_from_gates = (
        times_transposed(d_logits, w_router)
        + d_sig_logit.astype(f32)[:, None] * w_sigmoid.astype(f32)[None, :]
    )
    d_normed = d_in_sum + d_from_gates
    d_resid = half_of(grad_low).astype(f32) + norm_backward(resid, ffn_scale, gain_ffn, d_normed)
    d_attn = both_halves(d_resid.astype(bf16))

    d_context = times_transposed(d_attn, w_output).astype(bf16).reshape(by_head)
    d_query_rot, d_key_rot, d_value_all = attend_backward(
        query, key, value, d_context, log_total, allowed, score_scale
    )

    def unrope(values):
        return (values * cosine - rotate(values) * sine).astype(bf16).reshape(seq, head_all)

    d_query, d_key = unrope(d_query_rot), unrope(d_key_rot)
    d_value = d_value_all.astype(bf16).reshape(seq, head_all)
    d_normed_attn = (
        times_transposed(d_query, w_query)
        + times_transposed(d_key, w_key)
        + times_transposed(d_value, w_value)
    )
    grads = [contract_rows(normed_attn, d) for d in (d_query, d_key, d_value)]
    grads.append(contract_rows(d_attn, context_flat))
    grads = jnp.concatenate([g.astype(bf16) for g in grads], axis=1)

    rows = half // (lane_count // 2)
    start = (lane // 2) * rows
    mine = [
        lax.dynamic_slice_in_dim(a, start, rows, 0)
        for a in (d_normed * resid * ffn_scale, normed, d_logits, d_sig_logit[:, None])
    ]
    router_part = contract_rows(jnp.concatenate([mine[2], mine[3]], axis=1), mine[1])
    bias_part = jnp.concatenate(
        [jnp.sum(d.astype(f32), axis=0) for d in (d_query, d_key, d_value)]
    ).reshape(-1, features)
    to_groups = jnp.concatenate(
        [
            router_part,
            jnp.sum(mine[0], axis=0)[None],
            jnp.sum(d_normed_attn * hidden * attn_scale, axis=0)[None],
        ],
        axis=0,
    )
    to_groups = jnp.swapaxes(to_groups.reshape(-1, groups, features), 0, 1)
    lane_slots = (jnp.arange(lane_count) == lane).astype(f32)[:, None, None] * bias_part[None]
    lane_slots = lane_slots.reshape(-1, features)
    small = jnp.concatenate(
        [to_groups, jnp.broadcast_to(lane_slots[None], (groups,) + lane_slots.shape)], axis=1
    )
    small = jnp.pad(small, ((0, 0), (0, -small.shape[1] % 8), (0, 0)))
    grads, small = reduce_parts(
        groups, lane_count, grads.reshape(groups, features, -1), small, False, 2
    )
    biases = lax.dynamic_slice_in_dim(
        small, experts_all + 3 + lane * bias_part.shape[0], bias_part.shape[0], 0
    ).reshape(3, heads, head_width)
    biases = lax.dynamic_slice_in_dim(
        biases, group * (head_width // groups), head_width // groups, 2
    )

    outs = lax.psum_scatter(
        outs.reshape(groups * seq, width), ("expert", "tensor"), scatter_dimension=0, tiled=True
    )
    outs = lax.all_gather(outs, "tensor", axis=0, tiled=True)
    layer_out = both_halves((resid + half_of(outs).astype(f32)).astype(bf16))
    d_normed_in = sum_lanes(d_normed_attn.astype(bf16))
    grad_in = d_resid + norm_backward(half_of(hidden), half_of(attn_scale), gain_attn, d_normed_in)
    grad_in = both_halves(grad_in.astype(bf16))

    wide = jnp.concatenate([g_s_gate, g_s_up], axis=1).astype(bf16)
    wide = lax.all_to_all(wide, "expert", split_axis=0, concat_axis=1, tiled=True).astype(f32)
    wide = wide.reshape(features, groups, 2, units)
    grad_shared_gate = wide[:, :, 0].reshape(features, groups * units)
    grad_shared_up = wide[:, :, 1].reshape(features, groups * units)
    grad_shared_down = lax.all_to_all(
        g_s_down.astype(bf16), "expert", split_axis=1, concat_axis=0, tiled=True
    ).astype(f32)
    return (
        layer_out,
        grad_in,
        small[experts_all + 2],
        grads[:, :head_all],
        grads[:, head_all : 2 * head_all],
        grads[:, 2 * head_all : 3 * head_all],
        biases[0],
        biases[1],
        biases[2],
        grads[:, 3 * head_all :].T,
        small[experts_all + 1],
        small[:experts_all].T,
        small[experts_all],
        grad_shared_gate,
        grad_shared_up,
        grad_shared_down,
        g_gate,
        g_up,
        g_down,
    )


def solution(mesh):
    placed = (
        P("expert", None),
        P("expert"),
        P("expert", None),
        P(),
        P(None, "tensor"),
        P(None, "tensor"),
        P(None, "tensor"),
        P("tensor", None),
        P("tensor", None),
        P("tensor", None),
        P("tensor", None),
        P(),
        P(),
        P(),
        P(None, "tensor"),
        P(None, "tensor"),
        P("tensor", None),
        P("expert", None, "tensor"),
        P("expert", None, "tensor"),
        P("expert", "tensor", None),
        P("expert", None),
    )
    return jax.shard_map(
        on_device,
        mesh=mesh,
        in_specs=placed,
        out_specs=(
            P("expert", None),
            P("expert", None),
            P("expert"),
            P("expert", "tensor"),
            P("expert", "tensor"),
            P("expert", "tensor"),
            P("tensor", "expert"),
            P("tensor", "expert"),
            P("tensor", "expert"),
            P("tensor", "expert"),
            P("expert"),
            P("expert", None),
            P("expert"),
            P("expert", "tensor"),
            P("expert", "tensor"),
            P("tensor", "expert"),
            P("expert", None, "tensor"),
            P("expert", None, "tensor"),
            P("expert", "tensor", None),
        ),
        check_vma=False,
    )
```

time: 2130 us -> 937 us (0.44)
  waiting for transfers between devices: 1320 us -> 0.05 us
  Pallas kernels: 0 us -> 387 us
  blocking collectives: 185 us -> 0 us
  matrix products: 233 us -> 377 us
  local copies, waits for them, and re-layouts: 204 us -> 60 us
  other arithmetic: 138 us -> 61.2 us
    reduce_scatter x8 -> x1, waiting for transfers between devices: 573 us -> 0.01 us  [on_device(): lax.psum_scatter(outs.reshape(groups * seq, width), ('expert', 'tensor'),...]
    pallas_call x0 -> x3, Pallas kernels: none -> 387 us  [the longest x2 233 us: reduce_parts(): pl.pallas_call(functools.partial(reduce_kernel, groups, lanes, tokens), o...]
    all_to_all x2, waiting for transfers between devices: 380 us -> 0.01 us  [the longest x1 0.01 us: on_device(): lax.all_to_all(g_s_down.astype(bf16), 'expert', split_axis=1, concat_axis...]
    dot_general x24 -> x37, matrix products: 144 us -> 347 us  [the longest x1 30 us: run(): jnp.einsum('mtf,df->mtd', s_d_b, self.s_up, preferred_element_type=f32)]
    psum x3 -> x0, waiting for transfers between devices: 200 us -> none  [the longest x1 89.5 us: on_device(): lax.psum(ffn_part.astype(jnp.bfloat16), 'tensor').astype(jnp.float32)]
    all_to_all x2 -> x0, blocking collectives: 146 us -> none  [send_tokens(): lax.all_to_all(columns, 'expert', split_axis=0, concat_axis=0, tiled=True)]
    gather x5 -> x0, local copies, waits for them, and re-layouts: 119 us -> none  [the longest x1 26.5 us: on_device(): masked_grad[token_of]]
    unnamed x19 -> x2, waiting for transfers between devices: 104 us -> 0.03 us
  transfers between devices with their start and end apart: 18 -> 9, of which waited for: 15 -> 0; matrix products, arithmetic and copies ran while one was open for 18% -> 30% of each run, Pallas kernels for 0% -> 25%
where the time goes in v1:
time: 937 us; the launch traced here: 925 us
  Pallas kernels  387 us (41%)
  matrix products  377 us (40%)
  other arithmetic  61.2 us (7%)
  local copies, waits for them, and re-layouts  60 us (6%)
  starting transfers between devices  23.1 us (2%)
  between operations  16.5 us (2%)
    pallas_call x2, Pallas kernels, reduce_parts(): pl.pallas_call(functools.partial(reduce_kernel, groups, lanes, tokens), o...  233 us
    pallas_call x1, Pallas kernels, gather_tokens(): pl.pallas_call(functools.partial(gather_kernel, groups, lanes), out_shape...  154 us
    dot_general x1, matrix products, run(): jnp.einsum('mtf,df->mtd', s_d_b, self.s_up, preferred_element_type=f32)  30 us
    dot_general x1, matrix products, run(): jnp.einsum('mrt,mrd->mtd', pick_flat, in_rows.reshape(flat), preferred_el...  20.7 us
    dot_general x1, matrix products, run(): jnp.einsum('mrt,mrd->mtd', pick_flat, out_rows.reshape(flat), preferred_e...  20 us
  transfers between devices with their start and end apart: 9, of which 0 were waited for; matrix products, arithmetic and copies ran while one was open for 30% of the time, Pallas kernels for 25%

profile of v1, /device:TPU:21, one launch (start us, length us, event | category | flops | bytes accessed | tf_op | source)
XLA Modules:
  0.0 925.1 jit_solution(577580016848721273)
XLA Ops:
  10.2 2.1 multiply_reduce_fusion.2
  14.7 1.7 broadcast_multiply_fusion.2
  17.9 2.0 broadcast_select_fusion.grad
  27.3 2.1 copy-done.31
  34.0 154.4 %gather_tokens.1 = (f32[256,2048]{1,0:T(8,128)S(1)}, bf16[256,2048]{1,0:T(8,128)(2,1)S(1)}, bf16[8,512,2048]{2,1,0:T(8,128)(2,1)}, bf16[8,512,2048]{2,1,0:T(8,128)(2,1)}, s32[8,8,512]{2,1,0:T(8,128)S(1)}) custom-call(bf16[512,2048]{1,0:T(8,128)(2,1)S(1)} %convolution_convert_fusion.6.part, bf16[256,2048]{1,0:T(8,128)(2,1)S(1)} %constant_dynamic-slice_fusion.6.hidden, ...), custom_call_target="tpu_custom_call" | custom-call | tf_op jit(solution)/shard_map/gather_tokens/pallas_call | solution.py:277
  188.5 11.3 %fusion.119 = f32[1,8,512]{2,0,1:T(1,128)S(1)} fusion(bf16[8,512,2048]{2,1,0:T(8,128)(2,1)} %get-tuple-element.30, bf16[2048,1,1]{0,1,2:T(2,128)(2,1)S(1)} %reshape.386), kind=kOutput, calls=%fused_computation.244 | convolution fusion | flops 16777216 | bytes 16797696 | tf_op jit(solution)/shard_map/mtd,d->mt/dot_general | solution.py:543
  200.2 10.2 %fusion.116 = (f32[8,512]{1,0:T(8,128)S(1)}, f32[8,512,16]{1,2,0:T(8,128)S(1)}) fusion(bf16[8,512,2048]{2,1,0:T(8,128)(2,1)} %get-tuple-element.30, bf16[2048,16]{0,1:T(8,128)(2,1)S(1)} %copy-done.47), kind=kOutput, calls=%fused_computation.241 | convolution fusion | flops 268496896 | bytes 17121280 | tf_op jit(solution)/shard_map/mtd,de->mte/dot_general | solution.py:536
  210.4 13.6 %fusion.60 = f32[8,512,176]{1,2,0:T(8,128)} fusion(bf16[8,512,2048]{2,1,0:T(8,128)(2,1)} %get-tuple-element.30, bf16[2048,1408]{1,0:T(8,128)(2,1)} %param.36, s32[]{:T(128)S(6)} %select_n.100), kind=kOutput, calls=%fused_computation.126 | convolution fusion | flops 2952790016 | bytes 20709380 | tf_op jit(solution)/shard_map/mtd,df->mtf/dot_general | solution.py:560
  224.0 13.8 %fusion.64 = f32[8,512,176]{1,2,0:T(8,128)} fusion(bf16[8,512,2048]{2,1,0:T(8,128)(2,1)} %get-tuple-element.30, bf16[2048,1408]{1,0:T(8,128)(2,1)} %param.35, s32[]{:T(128)S(6)} %select_n.100), kind=kOutput, calls=%fused_computation.130 | convolution fusion | flops 2952790016 | bytes 20709380 | tf_op jit(solution)/shard_map/mtd,df->mtf/dot_general | solution.py:559
  238.8 15.9 %convolution_convert_fusion.1 = bf16[8,384,2048]{2,1,0:T(8,128)(2,1)} fusion(pred[8,384,512]{2,1,0:T(32,128)(4,1)S(1)} %bitcast_compare_fusion, bf16[8,512,2048]{2,1,0:T(8,128)(2,1)} %get-tuple-element.30), kind=kOutput, calls=%fused_computation.15 | convolution fusion | flops 6448742400 | bytes 30932992 | tf_op jit(solution)/shard_map/mrt,mtd->mrd/dot_general | solution.py:532
  254.7 15.3 %convolution_convert_fusion = bf16[8,384,2048]{2,1,0:T(8,128)(2,1)} fusion(pred[8,384,512]{2,1,0:T(32,128)(4,1)S(1)} %bitcast_compare_fusion, bf16[8,512,2048]{2,1,0:T(8,128)(2,1)} %get-tuple-element.31), kind=kOutput, calls=%fused_computation.14 | convolution fusion | flops 6448742400 | bytes 30932992 | tf_op jit(solution)/shard_map/mrt,mtd->mrd/dot_general | solution.py:534
  270.0 11.1 %fusion.5 = f32[2,8,192,352]{3,2,1,0:T(8,128)S(1)} fusion(bf16[8,2,192,2048]{3,2,1,0:T(8,128)(2,1)} %bitcast.316, bf16[2,2048,352]{1,2,0:T(8,128)(2,1)} %param.39), kind=kOutput, calls=%fused_computation.9 | convolution fusion | flops 4429185024 | bytes 19791872 | tf_op jit(solution)/shard_map/mecd,edf->mecf/dot_general | solution.py:546
  281.1 8.6 fusion.7
  289.7 13.3 %fusion.10 = (f32[8,2,192]{2,0,1:T(8,128)S(1)}, bf16[8,2,192,352]{3,2,0,1:T(8,128)(2,1)}, f32[2,8,192,352]{3,2,1,0:T(8,128)}) fusion(f32[2,8,192,352]{3,2,1,0:T(8,128)S(1)} %fusion.5, f32[2,8,192,352]{3,2,1,0:T(8,128)} %fusion.7, bf16[2,352,2048]{2,1,0:T(8,128)(2,1)S(1)} %copy-done, bf16[8,2,192,2048]{3,2,1,0:T(8,128)(2,1)} %bitcast.320), kind=kOutput, calls=%fused_computation.23 | convolution fusion | flops 4438914048 | bytes 30617600 | tf_op jit(solution)/shard_map/mecd,efd->mecf/dot_general | solution.py:547
  303.1 2.4 select_reduce_fusion
  305.5 9.1 convert_bitcast_fusion
  314.6 5.4 copy.160
  320.0 20.0 %fusion.118 = f32[8,512,2048]{2,1,0:T(8,128)} fusion(pred[8,384,512]{2,1,0:T(32,128)(4,1)S(1)} %copy-done.15, bf16[8,384,2048]{2,1,0:T(8,128)(2,1)} %bitcast.279), kind=kOutput, calls=%fused_computation.243 | convolution fusion | flops 6442450944 | bytes 47710208 | tf_op jit(solution)/shard_map/mrt,mrd->mtd/dot_general | solution.py:567
  340.0 16.1 %fusion.26 = (f32[8,512]{1,0:T(8,128)S(1)}, bf16[8,512,176]{1,2,0:T(8,128)(2,1)S(1)}, bf16[8,512,176]{1,2,0:T(8,128)(2,1)}, bf16[8,512,176]{1,2,0:T(8,128)(2,1)}) fusion(f32[8,512,176]{1,2,0:T(8,128)} %fusion.60, f32[8,512,176]{1,2,0:T(8,128)} %fusion.64, f32[8,512]{1,0:T(8,128)S(1)} %fusion.87, bf16[8,512,2048]{2,1,0:T(8,128)(2,1)} %get-tuple-element.31, ...), kind=kOutput, calls=%fused_computation.62 | convolution fusion | flops 2967203840 | bytes 27623428 | tf_op jit(solution)/shard_map/mtd,fd->mtf/dot_general | solution.py:561
  356.1 17.1 %add_convert_fusion.1 = bf16[8,512,2048]{2,1,0:T(8,128)(2,1)} fusion(f32[8,512,2048]{2,1,0:T(8,128)} %fusion.118, bf16[8,512,176]{1,2,0:T(8,128)(2,1)S(1)} %get-tuple-element.145, f32[8,512]{1,0:T(8,128)S(1)} %fusion.87, bf16[1408,2048]{1,0:T(8,128)(2,1)} %param.37, s32[]{:T(128)S(6)} %select_n.100), kind=kOutput, calls=%fused_computation.1 | convolution fusion | flops 2971729920 | bytes 52510724 | tf_op jit(solution)/shard_map/mtf,fd->mtd/dot_general | solution.py:569
  373.2 7.6 fusion.35
  381.7 6.0 all-to-all-start.1
  387.8 7.8 fusion.20
  395.6 11.9 %fusion.29 = f32[2,8,192,2048]{3,2,1,0:T(8,128)} fusion(bf16[8,2,192,352]{3,2,0,1:T(8,128)(2,1)S(1)} %get-tuple-element.151, bf16[2,2048,352]{1,2,0:T(8,128)(2,1)S(1)} %copy-done.27), kind=kOutput, calls=%fused_computation.65 | convolution fusion | flops 4429185024 | bytes 30212096 | tf_op jit(solution)/shard_map/mecf,edf->mecd/dot_general | solution.py:556
  407.5 16.0 %fusion = bf16[8,2,192,2048]{3,2,0,1:T(8,128)(2,1)} fusion(f32[2,8,192,2048]{3,2,1,0:T(8,128)} %fusion.29, bf16[8,2,192,352]{3,2,0,1:T(8,128)(2,1)} %get-tuple-element.150, bf16[2,2048,352]{1,2,0:T(8,128)(2,1)} %param.39), kind=kOutput, calls=%fused_computation.3 | convolution fusion | flops 4441767936 | bytes 42795008 | tf_op jit(solution)/shard_map/mecf,edf->mecd/dot_general | solution.py:557
  423.5 10.9 %copy.165 = bf16[8,2,192,2048]{3,2,1,0:T(8,128)(2,1)} copy(bf16[8,2,192,2048]{3,2,0,1:T(8,128)(2,1)} %fusion) | data formatting | bytes 25165824 | tf_op jit(solution)/shard_map/convert_element_type | solution.py:558
  435.6 20.7 %fusion.120 = f32[8,512,2048]{2,1,0:T(8,128)} fusion(pred[8,384,512]{2,1,0:T(32,128)(4,1)S(1)} %copy-done.16, bf16[8,384,2048]{2,1,0:T(8,128)(2,1)} %bitcast.278), kind=kOutput, calls=%fused_computation.245 | convolution fusion | flops 6442450944 | bytes 47710208 | tf_op jit(solution)/shard_map/mrt,mrd->mtd/dot_general | solution.py:571
  456.3 18.6 %fusion.62 = f32[8,512,2048]{2,1,0:T(8,128)} fusion(bf16[8,512,176]{1,2,0:T(8,128)(2,1)} %get-tuple-element.152, bf16[2048,1408]{1,0:T(8,128)(2,1)} %param.35, s32[]{:T(128)S(6)} %select_n.100), kind=kOutput, calls=%fused_computation.128 | convolution fusion | flops 2952790016 | bytes 36044804 | tf_op jit(solution)/shard_map/mtf,df->mtd/dot_general | solution.py:572
  474.8 30.0 %add_convert_fusion.parts = bf16[8,512,2048]{2,1,0:T(8,128)(2,1)} fusion(f32[8,512,2048]{2,1,0:T(8,128)} %fusion.120, f32[8,512,2048]{2,1,0:T(8,128)} %fusion.62, bf16[8,512,176]{1,2,0:T(8,128)(2,1)S(1)} %copy-done.39, bf16[2048,1408]{1,0:T(8,128)(2,1)} %param.36, s32[]{:T(128)S(6)} %select_n.100), kind=kOutput, calls=%fused_computation | convolution fusion | flops 2977955840 | bytes 86376448 | tf_op jit(solution)/shard_map/mtf,df->mtd/dot_general | solution.py:573
  504.8 137.2 %reduce_tokens.1 = (f32[256,2048]{1,0:T(8,128)}, f32[24,512]{1,0:T(8,128)}) custom-call(bf16[8,512,2048]{2,1,0:T(8,128)(2,1)} %add_convert_fusion.parts, f32[8,24,512]{2,1,0:T(8,128)} %maximum_maximum_fusion.small), custom_call_target="tpu_custom_call" | custom-call | tf_op jit(solution)/shard_map/reduce_tokens/pallas_call | solution.py:446
  644.7 1.6 fusion.117
  647.7 3.7 multiply_reduce_fusion.5
  651.4 8.7 fusion.36
  660.1 8.7 fusion.37
  668.9 4.1 convert_element_type.260
  674.3 2.0 copy.226
  678.1 2.3 pad_maximum_fusion.4
  680.5 12.5 %fusion.21 = f32[2,352,2048]{2,1,0:T(8,128)} fusion(bf16[8,2,192,2048]{3,2,1,0:T(8,128)(2,1)} %bitcast.321, bf16[8,2,192,352]{3,2,0,1:T(8,128)(2,1)S(1)} %copy-done.68, f32[8,2,192]{2,0,1:T(8,128)S(1)} %copy.159), kind=kOutput, calls=%fused_computation.50 | convolution fusion | flops 4432429056 | bytes 20525056 | tf_op jit(solution)/shard_map/mecf,mecd->efd/dot_general | solution.py:584
  692.9 10.1 %all-to-all-start = ((bf16[8,256,352]{1,2,0:T(8,128)(2,1)}), bf16[8,256,352]{1,2,0:T(8,128)(2,1)}, u32[]{:S(2)}, u32[]{:S(2)}) async-start(bf16[8,256,352]{1,2,0:T(8,128)(2,1)} %pad_maximum_fusion.4), calls=%async_computation.1 | async-start | bytes 2883584 | tf_op jit(solution)/shard_map/all_to_all | solution.py:800
  703.0 10.1 %convolution_bitcast_fusion = f32[2,2048,352]{1,2,0:T(8,128)} fusion(bf16[8,2,192,2048]{3,2,1,0:T(8,128)(2,1)} %bitcast.317, bf16[8,2,192,352]{3,2,0,1:T(8,128)(2,1)} %get-tuple-element.150), kind=kOutput, calls=%fused_computation.51 | convolution fusion | flops 4429185024 | bytes 20512768 | tf_op jit(solution)/shard_map/mecd,mecf->edf/dot_general | solution.py:583
  713.1 5.5 fusion.110
  718.6 2.5 collective-permute-start.1
  721.1 10.5 %convolution_bitcast_fusion.1 = f32[2,2048,352]{1,2,0:T(8,128)} fusion(bf16[8,2,192,2048]{3,2,1,0:T(8,128)(2,1)} %bitcast.318, bf16[8,2,192,352]{3,2,0,1:T(8,128)(2,1)S(1)} %copy-done.13), kind=kOutput, calls=%fused_computation.52 | convolution fusion | flops 4429185024 | bytes 20512768 | tf_op jit(solution)/shard_map/mecd,mecf->edf/dot_general | solution.py:582
  731.6 2.3 convert_element_type.340
  734.0 1.6 convert_element_type.339
  735.6 1.8 fusion.114
  737.4 3.0 copy.183
  743.1 1.7 broadcast_select_fusion.4
  747.8 2.2 convert_reduce_fusion
  757.1 2.7 convolution_convert_fusion.5
  759.8 3.3 fusion.122
  763.1 2.8 convolution_convert_fusion.4
  765.9 3.6 fusion.123
  769.5 3.8 convolution_convert_fusion.3
  773.4 6.1 multiply_reduce_fusion
  783.6 4.1 pad_maximum_fusion
  787.7 12.3 %copy.173 = bf16[2048,2048]{1,0:T(8,128)(2,1)} copy(bf16[2048,2048]{0,1:T(8,128)(2,1)} %pad_maximum_fusion) | data formatting | bytes 16777216 | tf_op jit(solution)/shard_map/concatenate | solution.py:753
  800.0 1.9 add_convert_fusion.4
  802.9 95.8 %reduce_weights.1 = (f32[256,2048]{1,0:T(8,128)}, f32[48,256]{1,0:T(8,128)}) custom-call(bf16[8,256,2048]{2,1,0:T(8,128)(2,1)} %bitcast.280, f32[8,48,256]{2,1,0:T(8,128)} %select_maximum_fusion.small), custom_call_target="tpu_custom_call" | custom-call | tf_op jit(solution)/shard_map/reduce_weights/pallas_call | solution.py:446
  898.8 2.7 slice_bitcast_fusion
  903.8 2.1 multiply_reduce_fusion.3
  905.9 2.3 add_convert_fusion.3
  908.2 3.2 collective-permute-start.4
  912.0 1.7 broadcast_select_fusion.6
  (254 shorter events, 53.2 us)
Async XLA Ops:
  7.2 282.5 %copy-start = (bf16[2,352,2048]{2,1,0:T(8,128)(2,1)S(1)}, bf16[2,352,2048]{2,1,0:T(8,128)(2,1)}, u32[]{:S(2)}) copy-start(bf16[2,352,2048]{2,1,0:T(8,128)(2,1)} %param.40) | copy-start | bytes 8650756
  7.2 661.6 %reduce-scatter.2.cloned.1.call-start = ((), (), s32[]{:S(2)}) async-start(), calls=%async_computation.3 | async-start | bytes 17301504 | tf_op jit(solution)/shard_map/reduce_scatter | solution.py:790
  7.3 192.6 %copy-start.61 = (s32[2]{0:T(128)}, s32[2]{0:T(128)S(1)}, u32[]{:S(2)}) copy-start(s32[2]{0:T(128)S(1)} %iota_add_fusion) | copy-start | bytes 28
  12.3 15.0 %copy-start.58 = (f32[512]{0:T(512)}, f32[512]{0:T(512)S(1)}, u32[]{:S(2)}) copy-start(f32[512]{0:T(512)S(1)} %add_rsqrt_fusion) | copy-start | bytes 6148
  13.1 14.2 %copy-start.54 = (f32[2048]{0:T(1024)}, f32[2048]{0:T(1024)S(1)}, u32[]{:S(2)}) copy-start(f32[2048]{0:T(1024)S(1)} %convert_element_type.261) | copy-start | bytes 24580
  14.6 16.3 %copy-start.18 = (pred[512,512]{0,1:T(8,128)(4,1)}, pred[512,512]{0,1:T(8,128)(4,1)S(1)}, u32[]{:S(2)}) copy-start(pred[512,512]{0,1:T(8,128)(4,1)S(1)} %fusion.66) | copy-start | bytes 786436
  16.4 7.6 copy-start.28
  16.4 3.5 copy-start.9
  16.4 3.5 copy-start.32
  19.9 14.1 %copy-start.2 = (bf16[512,2048]{1,0:T(8,128)(2,1)}, bf16[512,2048]{1,0:T(8,128)(2,1)S(1)}, u32[]{:S(2)}) copy-start(bf16[512,2048]{1,0:T(8,128)(2,1)S(1)} %broadcast_select_fusion.grad) | copy-start | bytes 6291460
  19.9 2.4 copy-start.34
  25.3 2.0 copy-start.22
  25.3 2.0 copy-start.24
  26.3 4.6 copy-start.7
  26.3 3.1 copy-start.31
  27.3 3.6 copy-start.52
  188.4 11.4 %copy-start.4 = (f32[256,2048]{1,0:T(8,128)}, f32[256,2048]{1,0:T(8,128)S(1)}, u32[]{:S(2)}) copy-start(f32[256,2048]{1,0:T(8,128)S(1)} %get-tuple-element.28) | copy-start | bytes 6291460
  188.4 11.4 %copy-start.6 = (bf16[256,2048]{1,0:T(8,128)(2,1)}, bf16[256,2048]{1,0:T(8,128)(2,1)S(1)}, u32[]{:S(2)}) copy-start(bf16[256,2048]{1,0:T(8,128)(2,1)S(1)} %get-tuple-element.33) | copy-start | bytes 3145732
  188.5 11.7 %copy-start.47 = (bf16[2048,16]{0,1:T(8,128)(2,1)S(1)}, bf16[2048,16]{0,1:T(8,128)(2,1)}, u32[]{:S(2)}) copy-start(bf16[2048,16]{0,1:T(8,128)(2,1)} %param.33) | copy-start | bytes 196612
  238.8 15.9 %copy-start.14 = (pred[8,384,512]{2,1,0:T(32,128)(4,1)}, pred[8,384,512]{2,1,0:T(32,128)(4,1)S(1)}, u32[]{:S(2)}) copy-start(pred[8,384,512]{2,1,0:T(32,128)(4,1)S(1)} %bitcast_compare_fusion) | copy-start | bytes 4718596
  270.0 11.1 %copy-start.26 = (bf16[2,2048,352]{1,2,0:T(8,128)(2,1)S(1)}, bf16[2,2048,352]{1,2,0:T(8,128)(2,1)}, u32[]{:S(2)}) copy-start(bf16[2,2048,352]{1,2,0:T(8,128)(2,1)} %param.38) | copy-start | bytes 8650756
  270.0 11.1 %copy-start.65 = (bf16[8,384,2048]{2,1,0:T(8,128)(2,1)S(1)}, bf16[8,384,2048]{2,1,0:T(8,128)(2,1)}, u32[]{:S(2)}) copy-start(bf16[8,384,2048]{2,1,0:T(8,128)(2,1)} %convolution_convert_fusion.1) | copy-start | bytes 37748740
  281.1 8.6 copy-start.21
  314.6 5.4 copy-start.15
  380.8 6.9 copy-start.56
  381.7 311.2 %all-to-all-start.1 = ((bf16[176,8,256]{2,0,1:T(8,128)(2,1)}), bf16[176,8,256]{2,0,1:T(8,128)(2,1)}, u32[]{:S(2)}, u32[]{:S(2)}) async-start(bf16[176,8,256]{2,0,1:T(8,128)(2,1)} %bitcast.272), calls=%async_computation.2 | async-start | bytes 1441792 | tf_op jit(solution)/shard_map/all_to_all | solution.py:804
  387.7 325.4 %all-gather.2.cloned.1.call-start = ((), (), s32[]{:S(2)}) async-start(), calls=%async_computation.4 | async-start | bytes 2621440 | tf_op jit(solution)/shard_map/all_gather | solution.py:793
  387.8 7.8 copy-start.27
  395.6 11.9 %copy-start.12 = (bf16[8,2,192,352]{3,2,0,1:T(8,128)(2,1)}, bf16[8,2,192,352]{3,2,0,1:T(8,128)(2,1)S(1)}, u32[]{:S(2)}) copy-start(bf16[8,2,192,352]{3,2,0,1:T(8,128)(2,1)S(1)} %get-tuple-element.151) | copy-start | bytes 6488068
  423.5 11.0 %copy-start.62 = (s32[2]{0:T(128)S(1)}, s32[2]{0:T(128)}, u32[]{:S(2)}) copy-start(s32[2]{0:T(128)} %copy-done.61) | copy-start | bytes 28
  423.5 12.1 %copy-start.16 = (pred[8,384,512]{2,1,0:T(32,128)(4,1)S(1)}, pred[8,384,512]{2,1,0:T(32,128)(4,1)}, u32[]{:S(2)}) copy-start(pred[8,384,512]{2,1,0:T(32,128)(4,1)} %copy-done.14) | copy-start | bytes 4718596
  456.3 18.6 %copy-start.39 = (bf16[8,512,176]{1,2,0:T(8,128)(2,1)S(1)}, bf16[8,512,176]{1,2,0:T(8,128)(2,1)}, u32[]{:S(2)}) copy-start(bf16[8,512,176]{1,2,0:T(8,128)(2,1)} %get-tuple-element.153) | copy-start | bytes 4325380
  504.8 139.8 %copy-start.48 = (bf16[2048,16]{0,1:T(8,128)(2,1)S(1)}, bf16[2048,16]{0,1:T(8,128)(2,1)}, u32[]{:S(2)}) copy-start(bf16[2048,16]{0,1:T(8,128)(2,1)} %param.33) | copy-start | bytes 196612
  642.0 5.6 copy-start.5
  647.6 3.8 copy-start.30
  651.4 8.7 copy-start.40
  660.1 8.8 copy-start.59
  676.6 3.9 copy-start.68
  692.9 41.0 %all-to-all-start = ((bf16[8,256,352]{1,2,0:T(8,128)(2,1)}), bf16[8,256,352]{1,2,0:T(8,128)(2,1)}, u32[]{:S(2)}, u32[]{:S(2)}) async-start(bf16[8,256,352]{1,2,0:T(8,128)(2,1)} %pad_maximum_fusion.4), calls=%async_computation.1 | async-start | bytes 2883584 | tf_op jit(solution)/shard_map/all_to_all | solution.py:800
  703.0 10.1 %copy-start.3 = (bf16[512,2048]{1,0:T(8,128)(2,1)S(1)}, bf16[512,2048]{1,0:T(8,128)(2,1)}, u32[]{:S(2)}) copy-start(bf16[512,2048]{1,0:T(8,128)(2,1)} %copy-done.2) | copy-start | bytes 6291460
  713.1 8.0 copy-start.13
  718.6 24.5 %collective-permute-start.1 = (bf16[256,2048]{1,0:T(8,128)(2,1)}, bf16[256,2048]{1,0:T(8,128)(2,1)}, u32[]{:S(2)}, u32[]{:S(2)}) collective-permute-start(bf16[256,2048]{1,0:T(8,128)(2,1)} %get-tuple-element.140), channel_id=1, source_target_pairs={{0,1},{1,0},{2,3},{3,2},{4,5},{5,4},{6,7},{7,6},{8,9},{9,8},{10,11... | collective-permute-start | bytes 3145736 | tf_op jit(solution)/shard_map/ppermute | solution.py:635
  737.4 3.0 copy-start.20
  742.0 2.9 copy-start.64
  742.0 170.0 %collective-permute-start = (bf16[256,2048]{1,0:T(8,128)(2,1)}, bf16[256,2048]{1,0:T(8,128)(2,1)}, u32[]{:S(2)}, u32[]{:S(2)}) collective-permute-start(bf16[256,2048]{1,0:T(8,128)(2,1)} %get-tuple-element.166), channel_id=1, source_target_pairs={{0,1},{1,0},{2,3},{3,2},{4,5},{5,4},{6,7},{7,6},{8,9},{9,8},{10,11... | collective-permute-start | bytes 3145736 | tf_op jit(solution)/shard_map/ppermute | solution.py:635
  744.9 2.9 copy-start.8
  744.9 2.9 copy-start.19
  744.9 2.9 copy-start.53
  747.8 2.2 copy-start.50
  757.1 2.7 copy-start.33
  763.1 2.8 copy-start.35
  769.5 3.9 copy-start.51
  773.3 7.5 copy-start.42
  773.4 7.5 copy-start.44
  773.4 7.5 copy-start.67
  779.5 2.6 copy-start.17
  780.7 2.2 copy-start.37
  780.7 2.9 copy-start.38
  780.7 19.3 %collective-permute-start.2 = (bf16[256,2048]{1,0:T(8,128)(2,1)}, bf16[256,2048]{1,0:T(8,128)(2,1)}, u32[]{:S(2)}, u32[]{:S(2)}) collective-permute-start(bf16[256,2048]{1,0:T(8,128)(2,1)} %constant_dynamic-slice_fusion.5), channel_id=1, source_target_pairs={{0,1},{1,0},{2,3},{3,2},{4,5},{5,4},{6,7},{7,6},{8,9},{9,8},{10,11... | collective-permute-start | bytes 3145736 | tf_op jit(solution)/shard_map/ppermute | solution.py:635
  802.0 101.8 %collective-permute-start.3 = (bf16[256,2048]{1,0:T(8,128)(2,1)S(1)}, bf16[256,2048]{1,0:T(8,128)(2,1)S(1)}, u32[]{:S(2)}, u32[]{:S(2)}) collective-permute-start(bf16[256,2048]{1,0:T(8,128)(2,1)S(1)} %add_convert_fusion.4), channel_id=1, source_target_pairs={{0,2},{1,3},{2,0},{3,1},{4,6},{5,7},{6,4},{7,5},{8,10},{9,11},{10,... | collective-permute-start | bytes 3145736 | tf_op jit(solution)/shard_map/ppermute | solution.py:635
  898.8 3.7 copy-start.57
  902.5 3.4 copy-start.11
  908.2 7.0 collective-permute-start.4
  915.2 2.6 copy-start.1
  (14 other events, 18.6 us)
Sparse Core Ops, SparseCore 0:
  373.4 195.7 reduce-scatter.1
  668.9 28.1 all-gather.1

commit v2 on v1

--- a/solution.py
+++ b/solution.py
@@ -90,12 +90,11 @@
 class Copies:
     def __init__(self, send_sems, recv_sems):
         self.send_sems, self.recv_sems = send_sems, recv_sems
-        self.started = []
-        self.count = 0
-
-    def start(self, source, target, peer, arriving=None):
-        index = self.count
-        self.count += 1
+        self.planned = []
+
+    def plan(self, source, target, peer, arriving=None, ends=True):
+        index = self.planned_count()
+        arriving = target if arriving is None else arriving
 
         def copy(source, target):
             return pltpu.make_async_remote_copy(
@@ -107,15 +106,27 @@
                 device_id_type=pl.DeviceIdType.MESH,
             )
 
-        mine = copy(source, target)
-        mine.start()
-        self.started.append(mine)
-        arriving = target if arriving is None else arriving
-        return copy(arriving, arriving).wait_recv
+        made = Planned(copy(source, target), copy(arriving, arriving))
+        self.planned.append((made, ends))
+        return made
+
+    def planned_count(self):
+        return len(self.planned)
+
+    def start(self, source, target, peer, arriving=None):
+        made = self.plan(source, target, peer, arriving)
+        made.start()
+        return made.wait
 
     def finish(self):
-        for copy in self.started:
-            copy.wait_send()
+        for made, ends in self.planned:
+            if ends:
+                made.sent()
+
+
+class Planned:
+    def __init__(self, mine, theirs):
+        self.start, self.sent, self.wait = mine.start, mine.wait_send, theirs.wait_recv
 
 
 def tiles(rows, size, step):
@@ -126,178 +137,877 @@
     lax.fori_loop(0, rows // size, body, 0)
 
 
-def gather_kernel(
-    groups, lanes, part, hidden, gain, grad, ids,
-    resid, normed, tokens_all, grads_all, ids_all,
-    total, from_core, from_chip, send_sems, recv_sems, local_sems,
-):
+def nt(left, right):
+    return lax.dot_general(left, right, (((1,), (1,)), ((), ())), preferred_element_type=f32)
+
+
+def spans(total, size):
+    return [(at, min(size, total - at)) for at in range(0, total, size)]
+
+
+class Sizes:
+    def __init__(self, **sizes):
+        self.__dict__.update(sizes)
+
+
+class Work:
+    def __init__(self, sizes, expert, bufs):
+        self.sizes, self.expert = sizes, expert
+        self.__dict__.update(bufs)
+
+    def place(self, s, ids):
+        z = self.sizes
+        named = jnp.max(jnp.where(ids == self.expert, 1.0, 0.0), axis=0, keepdims=True)
+        named = jnp.concatenate([named, jnp.zeros((7, z.seq), f32)], axis=0).astype(bf16)
+        along = nt(named, self.ranker[...]) - 1024.0
+        down = nt(self.ranker[...], named) - 1024.0
+        slots = lax.broadcasted_iota(jnp.int32, (z.capacity, z.seq), 0).astype(f32)
+        self.pick[s] = jnp.where(along[0:1, :] == slots, 1.0, 0.0).astype(bf16)
+        slots = lax.broadcasted_iota(jnp.int32, (z.seq, z.capacity), 1).astype(f32)
+        self.put[s] = jnp.where(down[:, 0:1] == slots, 1.0, 0.0).astype(bf16)
+
+    def rows_of(self, s):
+        return pl.ds(s * self.sizes.capacity, self.sizes.capacity)
+
+    def tokens_of(self, s):
+        return pl.ds(s * self.sizes.seq, self.sizes.seq)
+
+    def take(self):
+        z = self.sizes
+
+        def step(cols):
+            for s in range(2):
+                picked = matmul(self.pick[s], self.tokens[self.tokens_of(s), cols])
+                self.rows[self.rows_of(s), cols] = picked.astype(bf16)
+                picked = matmul(self.pick[s], self.grads[self.tokens_of(s), cols])
+                self.row_grads[self.rows_of(s), cols] = picked.astype(bf16)
+
+        tiles(z.width, 256, step)
+
+    def routed(self, small):
+        z = self.sizes
+        rows = self.rows[...]
+        logits = matmul(rows, self.router[...])
+        lanes = lax.broadcasted_iota(jnp.int32, logits.shape, 1)
+        logits = jnp.where(lanes < z.experts, logits, -1e30)
+        weights = jnp.exp(logits - jnp.max(logits, axis=1, keepdims=True))
+        mine = jnp.sum(jnp.where(lanes == self.expert, weights, 0.0), axis=1, keepdims=True)
+        gate = mine / jnp.sum(weights, axis=1, keepdims=True)
+        d_gate = jnp.zeros_like(gate)
+        for at, size in spans(z.ff, 256):
+            a = nt(self.rows[...], self.w_in[pl.ds(at, size), :])
+            b = nt(self.rows[...], self.w_in[pl.ds(z.ff + at, size), :])
+            u = nt(self.row_grads[...], self.w_out[pl.ds(at, size), :])
+            cols = pl.ds(at, size)
+            sigma = 1.0 / (1.0 + jnp.exp(-a))
+            silu = a * sigma
+            hidden = (silu * b).astype(bf16).astype(f32)
+            d_gate = d_gate + jnp.sum(hidden * u, axis=1, keepdims=True)
+            self.gated[:, cols] = (hidden * gate).astype(bf16)
+            d_hidden = u * gate
+            self.d_a[:, cols] = (d_hidden * b * sigma * (1.0 + a * (1.0 - sigma))).astype(bf16)
+            self.d_b[:, cols] = (d_hidden * silu).astype(bf16)
+        for s in range(2):
+            mine = d_gate[s * z.capacity : (s + 1) * z.capacity]
+            small[s][pl.ds(0, 1), :] = jnp.sum(
+                jnp.where(self.pick[s].astype(f32) > 0.5, mine, 0.0), axis=0, keepdims=True
+            )
+
+        def step(cols):
+            back = matmul(self.d_a[...], self.w_in[pl.ds(0, z.ff), cols])
+            back = back + matmul(self.d_b[...], self.w_in[pl.ds(z.ff, z.ff), cols])
+            self.d_rows[:, cols] = back.astype(bf16)
+
+        tiles(z.width, 256, step)
+
+    def shared(self, small):
+        z = self.sizes
+        for s in range(2):
+            at = self.tokens_of(s)
+            tokens = self.tokens[at, :]
+            logits = matmul(tokens, self.router[...])
+            lanes = lax.broadcasted_iota(jnp.int32, logits.shape, 1)
+            logit = jnp.sum(jnp.where(lanes == z.experts, logits, 0.0), axis=1, keepdims=True)
+            sig = 1.0 / (1.0 + jnp.exp(-logit))
+            both = matmul(tokens, self.s_in[...])
+            a, b = both[:, : z.units], both[:, z.units :]
+            u = nt(self.grads[at, :], self.s_out[...])
+            sigma = 1.0 / (1.0 + jnp.exp(-a))
+            silu = a * sigma
+            hidden = (silu * b).astype(bf16).astype(f32)
+            d_sig = lax.dot_general(
+                jnp.ones((8, z.units), f32),
+                hidden * u,
+                (((1,), (1,)), ((), ())),
+                precision=lax.Precision.HIGHEST,
+                preferred_element_type=f32,
+            )
+            small[s][pl.ds(1, 1), :] = d_sig[0:1]
+            self.s_gated[at, :] = (hidden * sig).astype(bf16)
+            d_hidden = u * sig
+            d_a = d_hidden * b * sigma * (1.0 + a * (1.0 - sigma))
+            self.s_d_both[at, : z.units] = d_a.astype(bf16)
+            self.s_d_both[at, z.units :] = (d_hidden * silu).astype(bf16)
+
+    def give(self):
+        z = self.sizes
+
+        def step(cols):
+            self.out_rows[...] = matmul(self.gated[...], self.w_out[:, cols]).astype(bf16)
+            out = matmul(self.s_gated[...], self.s_out[:, cols])
+            back = nt(self.s_d_both[...], self.s_in[cols, :])
+            for s in range(2):
+                at = slice(s * z.seq, (s + 1) * z.seq)
+                mine = out[at] + matmul(self.put[s], self.out_rows[self.rows_of(s), :])
+                self.out[self.tokens_of(s), cols] = mine.astype(bf16)
+                mine = back[at] + matmul(self.put[s], self.d_rows[self.rows_of(s), cols])
+                self.d_in[self.tokens_of(s), cols] = mine.astype(bf16)
+
+        tiles(z.width, 256, step)
+
+
+def experts_kernel(z, names, *refs):
+    r = Sizes(**dict(zip(names, refs)))
+    groups, lanes = z.groups, z.lanes
     peers = Peers(groups, lanes)
     far, bits = peers.far, peers.chip_bits()
-    seq, _ = grad.shape
-    half = seq // 2
-    piece = seq // lanes
-    half_rows = pl.ds(pl.multiple_of(peers.core * half, half), half)
-    other_rows = pl.ds(pl.multiple_of((1 - peers.core) * half, half), half)
-    first = pl.multiple_of((peers.core * peers.chips + peers.chip) * piece, piece)
+    seq = z.seq
+    half, piece = seq // 2, seq // lanes
+    core = peers.core
+    own = core * half
+    half_rows = pl.ds(pl.multiple_of(own, half), half)
+    other_rows = pl.ds(pl.multiple_of(half - own, half), half)
+    first = pl.multiple_of((core * peers.chips + peers.chip) * piece, piece)
     me = peers.group
     others = [k for k in peers.offsets() if k != 0]
-    peers.meet(
-        [peers.at(k) for k in others]
-        + [peers.other_core()]
-        + [peers.other_chip(b) for b in bits]
-    )
-    copies = Copies(send_sems, recv_sems)
-
-    own_grad = pltpu.make_async_copy(grad, grads_all.at[me], local_sems.at[0])
-    own_grad.start()
+    step_of = {k: 2 * k - 1 if k > 0 else -2 * k for k in peers.offsets()}
+    slot = {k: peers.group_at(k) for k in range(-far, far + 1)}
+    ahead, behind = peers.at(1), peers.at(-1)
+    core_peer = peers.other_core()
+    chip_peer = {b: peers.other_chip(b) for b in bits}
+    peers.meet([peers.at(k) for k in others] + [core_peer] + [chip_peer[b] for b in bits])
+    copies = Copies(r.send_sems, r.recv_sems)
+
+    def local(source, target, number):
+        return pltpu.make_async_copy(source, target, r.local_sems.at[number])
+
+    def remote(source, target, send_sem, recv_sem, peer):
+        return pltpu.make_async_remote_copy(
+            src_ref=source,
+            dst_ref=target,
+            send_sem=send_sem,
+            recv_sem=recv_sem,
+            device_id=peer,
+            device_id_type=pl.DeviceIdType.MESH,
+        )
+
+    ff_own = z.ff // 2
+    mine_at = pl.multiple_of(core * ff_own, 16)
+    theirs_at = pl.multiple_of((1 - core) * ff_own, 16)
+    weights, traded = [], []
+    for number, (source, target, base) in enumerate(
+        [(r.gate, r.w_in, 0), (r.up, r.w_in, z.ff), (r.down, r.w_out, 0)]
+    ):
+        rows = pl.ds(base + mine_at, ff_own)
+        weights.append(local(source.at[core], target.at[rows], number))
+        traded.append(
+            copies.plan(
+                source.at[1 - core],
+                target.at[rows],
+                core_peer,
+                target.at[pl.ds(base + theirs_at, ff_own)],
+            )
+        )
+    weights += [
+        local(r.s_in_hbm, r.s_in, 3),
+        local(r.s_out_hbm, r.s_out, 4),
+        local(r.router_hbm, r.router, 5),
+    ]
+    own_part = local(r.part.at[half_rows], r.total, 6)
+    own_grad = local(r.grad, r.grads_all.at[me], 7)
+    own_tokens = local(r.normed, r.tokens_all.at[me, half_rows], 8)
+    own_hidden = local(r.hidden.at[half_rows], r.stage.at[0], 9)
+    keep_resid = local(r.wide, r.resid, 10)
 
     def hop(array, k, start, size, source=None):
-        held = peers.group_at(k + 1 if k < 0 else k - 1)
+        held = slot[k + 1] if k < 0 else slot[k - 1]
         rows = pl.ds(pl.multiple_of(start, size), size)
-        return copies.start(
+        return copies.plan(
             array.at[held, rows] if source is None else source,
             array.at[held, rows],
-            peers.at(1) if k < 0 else peers.at(-1),
-            array.at[peers.group_at(k), rows],
+            ahead if k < 0 else behind,
+            array.at[slot[k], rows],
         )
 
     def chip_swap(array, k, bit):
-        slot = peers.group_at(k)
         size = bit * piece
-        start = (peers.core * peers.chips + lax.div(peers.chip, bit) * bit) * piece
-        theirs = (peers.core * peers.chips + lax.div(flip_bit(peers.chip, bit), bit) * bit) * piece
+        start = (core * peers.chips + lax.div(peers.chip, bit) * bit) * piece
+        theirs = (core * peers.chips + lax.div(flip_bit(peers.chip, bit), bit) * bit) * piece
         rows = pl.ds(pl.multiple_of(start, size), size)
         arriving = pl.ds(pl.multiple_of(theirs, size), size)
-        return copies.start(
-            array.at[slot, rows], array.at[slot, rows], peers.other_chip(bit),
-            array.at[slot, arriving],
+        return copies.plan(
+            array.at[slot[k], rows],
+            array.at[slot[k], rows],
+            chip_peer[bit],
+            array.at[slot[k], arriving],
         )
 
     def core_swap(array, k, source=None):
-        slot = peers.group_at(k)
-        return copies.start(
-            array.at[slot, half_rows] if source is None else source,
-            array.at[slot, half_rows],
-            peers.other_core(),
-            array.at[slot, other_rows],
+        return copies.plan(
+            array.at[slot[k], half_rows] if source is None else source,
+            array.at[slot[k], half_rows],
+            core_peer,
+            array.at[slot[k], other_rows],
         )
 
-    ids_all[me] = ids[...]
-    late = [
-        copies.start(ids, ids_all.at[me], peers.at(k), ids_all.at[peers.group_at(-k)])
-        for k in others
+    signed = [s * k for k in range(1, far) for s in (-1, 1)]
+    ids_got = [
+        copies.plan(r.ids, r.ids_all.at[me], peers.at(k), r.ids_all.at[slot[-k]]) for k in others
     ]
-    own_piece = grad.at[pl.ds(first, piece)]
-    g_ring = {k: hop(grads_all, k, first, piece, own_piece) for k in (-1, 1)}
-    got_core = copies.start(part.at[other_rows], from_core, peers.other_core())
-    got_core()
-    start_of_half = peers.core * half
+    own_piece = r.grad.at[pl.ds(first, piece)]
+    g_ring = {
+        k: hop(r.grads_all, k, first, piece, own_piece if abs(k) == 1 else None) for k in signed
+    }
+    g_ring[-far] = hop(r.grads_all, -far, first, piece // 2)
+    g_ring[far] = hop(r.grads_all, far, first + piece // 2, piece // 2)
+    x_ring = {
+        k: hop(r.tokens_all, k, own, half, r.normed if abs(k) == 1 else None) for k in signed
+    }
+    x_ring[-far] = hop(r.tokens_all, -far, own, half // 2)
+    x_ring[far] = hop(r.tokens_all, far, own + half // 2, half // 2)
+    g_chip = {k: [chip_swap(r.grads_all, k, b) for b in bits] for k in others}
+    g_core = {k: core_swap(r.grads_all, k) for k in others}
+    x_core = {
+        k: core_swap(r.tokens_all, k, r.normed if k == 0 else None) for k in peers.offsets()
+    }
+    part_core = copies.plan(r.part.at[other_rows], r.from_core, core_peer)
+    part_chip = [
+        copies.plan(r.total, r.part_chip.at[i], chip_peer[b], ends=False)
+        for i, b in enumerate(bits)
+    ]
+
+    ring_up, ring_down = {}, {}
+    lower, upper, all_rows = pl.ds(0, half // 2), pl.ds(half // 2, half // 2), pl.ds(0, half)
+    for k in range(far, 0, -1):
+        rows_up, rows_down = (lower, upper) if k == far else (all_rows, all_rows)
+        at_up, at_down = (0, 0) if k == far else (2 * (far - k) - 1, 2 * (far - k))
+        odd = k % 2
+        ring_up[k] = copies.plan(
+            r.stage.at[odd, rows_up], r.from_ring.at[at_up, rows_up], ahead, ends=False
+        )
+        ring_down[k] = copies.plan(
+            r.stage.at[odd if k == far else 2 + odd, rows_down],
+            r.from_ring.at[at_down, rows_down],
+            behind,
+            ends=False,
+        )
+    home_chip = [
+        copies.plan(r.total, r.from_chip.at[i], chip_peer[b], ends=False)
+        for i, b in enumerate(bits)
+    ]
+    small_peers = [core_peer] + [chip_peer[b] for b in bits]
+    small_swaps = [
+        copies.plan(r.small_swap.at[2 * i], r.small_swap.at[2 * i + 1], peer)
+        for i, peer in enumerate(small_peers)
+    ]
+
+    part_core.start()
+    own_part.start()
+    own_hidden.start()
+    g_ring[-1].start()
+    g_ring[1].start()
+    for copy in ids_got:
+        copy.start()
+    r.ids_all[me] = r.ids[...]
+    for copy in weights + traded:
+        copy.start()
+    own_grad.start()
+    token = lax.broadcasted_iota(jnp.int32, (seq, seq), 0)
+    other = lax.broadcasted_iota(jnp.int32, (seq, seq), 1)
+    ranks = jnp.where(other < token, 1.0, jnp.where(other == token, 1024.0, 0.0))
+    r.ranker[...] = ranks.astype(bf16)
+
+    own_part.wait()
+    part_core.wait()
 
     def add_core(rows):
-        mine = pl.ds(pl.multiple_of(start_of_half + rows.start, rows.size), rows.size)
-        both = part[mine, :].astype(f32) + from_core[rows, :].astype(f32)
-        total[rows, :] = both.astype(bf16)
+        both = r.total[rows, :].astype(f32) + r.from_core[rows, :].astype(f32)
+        r.total[rows, :] = both.astype(bf16)
 
     tiles(half, 32, add_core)
-    got_chip = copies.start(total, from_chip.at[0], peers.other_chip(bits[0]))
-    chip_copy = copies.started.pop()
+    part_chip[0].start()
+    own_hidden.wait()
     for k in range(2, far):
         for s in (-1, 1):
-            g_ring[s * (k - 1)]()
-            g_ring[s * k] = hop(grads_all, s * k, first, piece)
-        if k == 2:
-            got_chip()
-            for i, bit in enumerate(bits):
-
-                def add_chip(rows, i=i):
-                    both = total[rows, :].astype(f32) + from_chip[i, rows, :].astype(f32)
-                    if i + 1 < len(bits):
-                        total[rows, :] = both.astype(bf16)
-                        return
-                    both = hidden[rows, :].astype(f32) + both
-                    resid[rows, :] = both
-                    normed[rows, :] = (both * rms_scale(both) * gain[...]).astype(bf16)
-
-                chip_copy.wait_send()
-                tiles(half, 32, add_chip)
+            g_ring[s * (k - 1)].wait()
+            g_ring[s * k].start()
+        if k != 2:
+            continue
+        for i, bit in enumerate(bits):
+            part_chip[i].wait()
+            part_chip[i].sent()
+
+            def add_chip(rows, i=i):
+                both = r.total[rows, :].astype(f32) + r.part_chip[i, rows, :].astype(f32)
                 if i + 1 < len(bits):
-                    copies.start(total, from_chip.at[i + 1], peers.other_chip(bits[i + 1]))()
-                    chip_copy = copies.started.pop()
-            x_ring = {k2: hop(tokens_all, k2, start_of_half, half, normed) for k2 in (-1, 1)}
-            late.append(core_swap(tokens_all, 0, normed))
-            own_rows = pltpu.make_async_copy(
-                normed, tokens_all.at[me, half_rows], local_sems.at[1]
-            )
-            own_rows.start()
-    for s in (-1, 1):
-        g_ring[s * (far - 1)]()
-    ahead_half = hop(grads_all, -far, first, piece // 2)
-    back_half = hop(grads_all, far, first + piece // 2, piece // 2)
-    order = [s * k for k in range(1, far) for s in (-1, 1)] + [far]
-    swaps = {k: chip_swap(grads_all, k, bits[0]) for k in order[:-1]}
-    ahead_half()
-    back_half()
-    swaps[far] = chip_swap(grads_all, far, bits[0])
+                    r.total[rows, :] = both.astype(bf16)
+                    return
+                both = r.stage[0, rows, :].astype(f32) + both
+                r.wide[rows, :] = both
+                r.normed[rows, :] = (both * rms_scale(both) * r.gain[...]).astype(bf16)
+
+            tiles(half, 32, add_chip)
+            if i + 1 < len(bits):
+                part_chip[i + 1].start()
+        x_ring[-1].start()
+        x_ring[1].start()
+        x_core[0].start()
+        own_tokens.start()
+        keep_resid.start()
+    for k in signed[:-2]:
+        g_chip[k][0].start()
+    for copy in ids_got + weights + traded:
+        copy.wait()
+    own_grad.wait()
+    own_tokens.wait()
+    keep_resid.wait()
 
     def finish_grads(ks):
         for k in ks:
-            swaps[k]()
-            for bit in bits[1:]:
-                chip_swap(grads_all, k, bit)()
-            late.append(core_swap(grads_all, k))
-
-    for k in range(2, far):
-        finish_grads([-(k - 1), k - 1])
-        for s in (-1, 1):
-            x_ring[s * (k - 1)]()
-            x_ring[s * k] = hop(tokens_all, s * k, start_of_half, half)
-            late.append(core_swap(tokens_all, s * (k - 1)))
-    for s in (-1, 1):
-        x_ring[s * (far - 1)]()
-    ahead_half = hop(tokens_all, -far, start_of_half, half // 2)
-    back_half = hop(tokens_all, far, start_of_half + half // 2, half // 2)
-    for s in (-1, 1):
-        late.append(core_swap(tokens_all, s * (far - 1)))
-    finish_grads([1 - far, far - 1, far])
-    ahead_half()
-    back_half()
-    late.append(core_swap(tokens_all, far))
-    for wait in late:
-        wait()
-    own_grad.wait()
-    own_rows.wait()
+            for i in range(len(bits)):
+                g_chip[k][i].wait()
+                if i + 1 < len(bits):
+                    g_chip[k][i + 1].start()
+            g_core[k].start()
+
+    def events(p):
+        for q in range(far):
+
+            @pl.when(p == q)
+            def _(k=q + 1):
+                if k < far:
+                    for s in (-1, 1):
+                        x_ring[s * k].wait()
+                        if k + 1 < far:
+                            x_ring[s * (k + 1)].start()
+                    if k + 1 == far:
+                        x_ring[-far].start()
+                        x_ring[far].start()
+                    for s in (-1, 1):
+                        x_core[s * k].start()
+                else:
+                    x_ring[-far].wait()
+                    x_ring[far].wait()
+                    x_core[far].start()
+                if k == 1:
+                    for s in (-1, 1):
+                        g_ring[s * (far - 1)].wait()
+                        g_ring[s * far].start()
+                        g_chip[s * (far - 1)][0].start()
+                if k == 2:
+                    g_ring[-far].wait()
+                    g_ring[far].wait()
+                    g_chip[far][0].start()
+                finish_grads([-k, k] if k < far else [far])
+                x_core[1 - k].wait()
+                x_core[k].wait()
+                g_core[k].wait()
+                if k > 1:
+                    g_core[1 - k].wait()
+
+    def small_copy(i, peer):
+        return remote(
+            r.small_out.at[i], r.small_in.at[i], r.small_send.at[i], r.small_recv.at[i], peer
+        )
+
+    def given_copy(i, source):
+        return remote(source, r.given.at[i], r.give_send.at[i], r.give_recv.at[i], core_peer)
+
+    def main(tokens, grads, rows, row_grads, d_rows, out_rows, gated, d_a, d_b, s_gated,
+             s_d_both, out, d_in, pick, put):
+        work = Work(
+            z,
+            me * 2 + core,
+            dict(
+                tokens=tokens, grads=grads, rows=rows, row_grads=row_grads, d_rows=d_rows,
+                out_rows=out_rows, gated=gated, d_a=d_a, d_b=d_b, s_gated=s_gated,
+                s_d_both=s_d_both, out=out, d_in=d_in, pick=pick, put=put, w_in=r.w_in,
+                w_out=r.w_out, s_in=r.s_in, s_out=r.s_out, router=r.router, ranker=r.ranker,
+            ),
+        )
+
+        def leave(p, slots):
+            found = []
+            for s in range(2):
+                i = 2 * p + s
+                keep = pl.ds(pl.multiple_of(s * seq + own, half), half)
+                give = pl.ds(pl.multiple_of(s * seq + half - own, half), half)
+                sent = given_copy(i, d_in.at[give])
+                kept = local(d_in.at[keep], r.kept.at[i], 12 + s)
+                found += [(kept.start, kept.wait), (sent.start, sent.wait_send)]
+                for lane in range(lanes):
+                    from_row = s * seq + (lane % 2 * peers.chips + lane // 2) * piece
+                    stored = local(
+                        out.at[pl.ds(from_row, piece)],
+                        r.outs_all.at[slots[s], pl.ds(lane * piece, piece)],
+                        25 + s * lanes + lane,
+                    )
+                    found.append((stored.start, stored.wait))
+            return found
+
+        def loop(p, carry):
+            slots = [peers.group_at(-p), peers.group_at(p + 1)]
+            events(p)
+            loads = []
+            for s in range(2):
+                at = pl.ds(s * seq, seq)
+                loads.append(local(r.tokens_all.at[slots[s]], tokens.at[at], s))
+                loads.append(local(r.grads_all.at[slots[s]], grads.at[at], 2 + s))
+            for copy in loads:
+                copy.start()
+            for s in range(2):
+                work.place(s, r.ids_all[slots[s]])
+            for copy in loads:
+                copy.wait()
+            at = pl.ds(pl.multiple_of(p * 2 * z.capacity, 2 * z.capacity), 2 * z.capacity)
+            saves = [
+                local(source, target.at[at], 16 + n)
+                for n, (source, target) in enumerate(
+                    [
+                        (rows, r.rows_all),
+                        (row_grads, r.row_grads_all),
+                        (gated, r.gated_all),
+                        (d_a, r.d_a_all),
+                        (d_b, r.d_b_all),
+                    ]
+                )
+            ]
+            for s in range(2):
+                mine = pl.ds(s * seq, seq)
+                saves.append(local(s_gated.at[mine], r.s_gated_all.at[slots[s]], 21 + 2 * s))
+                saves.append(local(s_d_both.at[mine], r.s_d_both_all.at[slots[s]], 22 + 2 * s))
+            small = [r.small_out.at[2 * p], r.small_out.at[2 * p + 1]]
+            work.take()
+            for copy in saves[:2]:
+                copy.start()
+            work.routed(small)
+            for copy in saves[2:5]:
+                copy.start()
+            work.shared(small)
+            for copy in saves[5:]:
+                copy.start()
+            small_copy(2 * p + 1, (slots[1], peers.lane)).start()
+
+            @pl.when(p > 0)
+            def _():
+                small_copy(2 * p, (slots[0], peers.lane)).start()
+                for _, wait in leave(p - 1, slots):
+                    wait()
+
+            work.give()
+            for start, _ in leave(p, slots):
+                start()
+            for copy in saves:
+                copy.wait()
+            return carry
+
+        lax.fori_loop(0, far, loop, 0)
+        for _, wait in leave(far - 1, [me, me]):
+            wait()
+
+    pl.run_scoped(
+        main,
+        tokens=pltpu.VMEM((2 * seq, z.width), bf16),
+        grads=pltpu.VMEM((2 * seq, z.width), bf16),
+        rows=pltpu.VMEM((2 * z.capacity, z.width), bf16),
+        row_grads=pltpu.VMEM((2 * z.capacity, z.width), bf16),
+        d_rows=pltpu.VMEM((2 * z.capacity, z.width), bf16),
+        out_rows=pltpu.VMEM((2 * z.capacity, 256), bf16),
+        gated=pltpu.VMEM((2 * z.capacity, z.ff), bf16),
+        d_a=pltpu.VMEM((2 * z.capacity, z.ff), bf16),
+        d_b=pltpu.VMEM((2 * z.capacity, z.ff), bf16),
+        s_gated=pltpu.VMEM((2 * seq, z.units), bf16),
+        s_d_both=pltpu.VMEM((2 * seq, 2 * z.units), bf16),
+        out=pltpu.VMEM((2 * seq, z.width), bf16),
+        d_in=pltpu.VMEM((2 * seq, z.width), bf16),
+        pick=pltpu.VMEM((2, z.capacity, seq), bf16),
+        put=pltpu.VMEM((2, seq, z.capacity), bf16),
+    )
+
+    def fetch(k, place, core_place):
+        i = step_of[k]
+        given_copy(i, r.given.at[i]).wait_recv()
+        loads = [
+            local(r.kept.at[i], r.stage.at[place], 0),
+            local(r.given.at[i], r.stage_core.at[core_place], 1),
+        ]
+        for copy in loads:
+            copy.start()
+        for copy in loads:
+            copy.wait()
+
+    def arrived(ring, index, rows, place):
+        ring.wait()
+        copy = local(r.from_ring.at[index, rows], r.stage_ring.at[place, rows], 2 + place)
+        copy.start()
+        copy.wait()
+
+    def add(place, core_place, start, size, ring_place=None):
+        def step(rows):
+            at = pl.ds(pl.multiple_of(start + rows.start, rows.size), rows.size)
+            value = r.stage[place, at, :].astype(f32) + r.stage_core[core_place, at, :].astype(f32)
+            if ring_place is not None:
+                value = value + r.stage_ring[ring_place, at, :].astype(f32)
+            r.stage[place, at, :] = value.astype(bf16)
+
+        tiles(size, 32, step)
+
+    def ring_stage(k):
+        odd = k % 2
+        if k + 2 <= far:
+            ring_up[k + 2].sent()
+            ring_down[k + 2].sent()
+        fetch(k, odd, 0)
+        fetch(-k, 2 + odd, 1)
+        at = 0 if k == far - 1 else 2 * (far - k) - 3
+        if k == far - 1:
+            add(odd, 0, half // 2, half // 2)
+            add(2 + odd, 1, 0, half // 2)
+            arrived(ring_up[far], 0, lower, 0)
+            add(odd, 0, 0, half // 2, 0)
+        else:
+            arrived(ring_up[k + 1], at, all_rows, 0)
+            add(odd, 0, 0, half, 0)
+        ring_up[k].start()
+        if k == far - 1:
+            arrived(ring_down[far], 0, upper, 1)
+            add(2 + odd, 1, half // 2, half // 2, 1)
+        else:
+            arrived(ring_down[k + 1], at + 1, all_rows, 1)
+            add(2 + odd, 1, 0, half, 1)
+        ring_down[k].start()
+
+    fetch(far, far % 2, 0)
+    add(far % 2, 0, 0, half)
+    ring_up[far].start()
+    ring_down[far].start()
+
+    features = z.width // groups
+
+    def columns_of(t):
+        return pl.ds(pl.multiple_of(t * features, features), features)
+
+    def routed_grads(gated, d_a, d_b, rows, row_grads, wide_in, wide_out):
+        whole_loads = [
+            local(r.gated_all, gated, 4),
+            local(r.d_a_all, d_a, 5),
+            local(r.d_b_all, d_b, 6),
+        ]
+
+        def loads(t):
+            odd = lax.rem(t, 2)
+            cols = columns_of(t)
+            return [
+                local(r.rows_all.at[:, cols], rows.at[odd], 7 + odd),
+                local(r.row_grads_all.at[:, cols], row_grads.at[odd], 9 + odd),
+            ]
+
+        def stores(t):
+            odd = lax.rem(t, 2)
+            cols = columns_of(t)
+            found = []
+            for n, (source, base, target) in enumerate(
+                [
+                    (wide_in, 0, r.g_gate),
+                    (wide_in, z.ff, r.g_up),
+                    (wide_out, 0, r.g_down),
+                ]
+            ):
+                here = source.at[odd, pl.ds(base + mine_at, ff_own)]
+                there = source.at[odd, pl.ds(base + theirs_at, ff_own)]
+                kept = local(here, target.at[core, :, cols], 11 + 2 * n + odd)
+                sent = remote(
+                    there,
+                    target.at[core, :, cols],
+                    r.grad_send.at[2 * n + odd],
+                    r.grad_recv.at[n * groups + t],
+                    core_peer,
+                )
+                found.append((kept, sent))
+            return found
+
+        def settle(t):
+            for kept, sent in stores(t):
+                kept.wait()
+                sent.wait_send()
+
+        def unit(t, carry):
+            odd = lax.rem(t, 2)
+
+            @pl.when(t + 1 < groups)
+            def _():
+                for copy in loads(t + 1):
+                    copy.start()
+
+            for copy in loads(t):
+                copy.wait()
+
+            @pl.when(t >= 2)
+            def _():
+                settle(t - 2)
+
+            wide_in[odd, pl.ds(0, z.ff), :] = contract_rows(d_a[...], rows[odd])
+            wide_in[odd, pl.ds(z.ff, z.ff), :] = contract_rows(d_b[...], rows[odd])
+            wide_out[odd] = contract_rows(gated[...], row_grads[odd])
+            for kept, sent in stores(t):
+                kept.start()
+                sent.start()
+            return carry
+
+        for copy in whole_loads + loads(0):
+            copy.start()
+        for copy in whole_loads:
+            copy.wait()
+        lax.fori_loop(0, groups // 2, unit, 0)
+        ring_stage(far - 1)
+        lax.fori_loop(groups // 2, groups, unit, 0)
+        settle(groups - 2)
+        settle(groups - 1)
+
+    tile_rows = groups * z.capacity
+    pl.run_scoped(
+        routed_grads,
+        gated=pltpu.VMEM((tile_rows, z.ff), bf16),
+        d_a=pltpu.VMEM((tile_rows, z.ff), bf16),
+        d_b=pltpu.VMEM((tile_rows, z.ff), bf16),
+        rows=pltpu.VMEM((2, tile_rows, features), bf16),
+        row_grads=pltpu.VMEM((2, tile_rows, features), bf16),
+        wide_in=pltpu.VMEM((2, 2 * z.ff, features), f32),
+        wide_out=pltpu.VMEM((2, z.ff, features), f32),
+    )
+
+    def shared_grads(s_gated, s_d_both, tokens, grads, wide):
+        whole_loads = [local(r.s_gated_all, s_gated, 4), local(r.s_d_both_all, s_d_both, 5)]
+
+        def loads(t):
+            odd = lax.rem(t, 2)
+            cols = columns_of(t)
+            return [
+                local(r.tokens_all.at[:, :, cols], tokens.at[odd], 7 + odd),
+                local(r.grads_all.at[:, :, cols], grads.at[odd], 9 + odd),
+            ]
+
+        def store(t):
+            odd = lax.rem(t, 2)
+            return local(wide.at[odd], r.s_grads.at[t], 11 + odd)
+
+        def flat(array):
+            return array.reshape(groups * seq, array.shape[-1])
+
+        def unit(t, carry):
+            odd = lax.rem(t, 2)
+
+            @pl.when(t + 1 < groups)
+            def _():
+                for copy in loads(t + 1):
+                    copy.start()
+
+            for copy in loads(t):
+                copy.wait()
+
+            @pl.when(t >= 2)
+            def _():
+                store(t - 2).wait()
+
+            both = contract_rows(flat(s_d_both[...]), flat(tokens[odd]))
+            wide[odd, pl.ds(0, 2 * z.units), :] = both.astype(bf16)
+            out = contract_rows(flat(s_gated[...]), flat(grads[odd]))
+            wide[odd, pl.ds(2 * z.units, z.units), :] = out.astype(bf16)
+            store(t).start()
+            return carry
+
+        for copy in whole_loads + loads(0):
+            copy.start()
+        for copy in whole_loads:
+            copy.wait()
+        stages = list(range(far - 2, 0, -1))
+        done = 0
+        for n, k in enumerate(stages):
+            upto = groups * (n + 1) // len(stages) if n + 1 < len(stages) else groups
+            lax.fori_loop(done, upto, unit, 0)
+            done = upto
+            ring_stage(k)
+        store(groups - 2).wait()
+        store(groups - 1).wait()
+
+    pl.run_scoped(
+        shared_grads,
+        s_gated=pltpu.VMEM((groups, seq, z.units), bf16),
+        s_d_both=pltpu.VMEM((groups, seq, 2 * z.units), bf16),
+        tokens=pltpu.VMEM((2, groups, seq, features), bf16),
+        grads=pltpu.VMEM((2, groups, seq, features), bf16),
+        wide=pltpu.VMEM((2, 3 * z.units, features), bf16),
+    )
+    ring_up[2].sent()
+    ring_down[2].sent()
+    fetch(0, 0, 0)
+
+    r.small_total[...] = jnp.zeros_like(r.small_total)
+    d_sig = r.small_out[0, pl.ds(1, 1), :]
+    r.small_total[pl.ds(me * 2 + core, 1), :] = r.small_out[0, pl.ds(0, 1), :]
+    for k in others:
+        i = step_of[k]
+        copy = small_copy(i, peers.at(k))
+        copy.wait_recv()
+        copy.wait_send()
+        d_sig = d_sig + r.small_in[i, pl.ds(1, 1), :]
+        r.small_total[pl.ds(slot[-k] * 2 + core, 1), :] = r.small_in[i, pl.ds(0, 1), :]
+    r.small_total[pl.ds(z.experts, 1), :] = d_sig
+    for i, copy in enumerate(small_swaps):
+        r.small_swap[2 * i] = r.small_total[...]
+        copy.start()
+        copy.wait()
+        r.small_total[...] = r.small_swap[2 * i] + r.small_swap[2 * i + 1]
+
+    for n, target in enumerate((r.g_gate, r.g_up, r.g_down)):
+        for t in range(groups):
+            arriving = target.at[1 - core, :, columns_of(t)]
+            remote(
+                arriving, arriving, r.grad_send.at[0], r.grad_recv.at[n * groups + t], core_peer
+            ).wait_recv()
+
+    last_at = 2 * (far - 1) - 1
+    arrived(ring_up[1], last_at, all_rows, 0)
+    arrived(ring_down[1], last_at + 1, all_rows, 1)
+
+    def last(rows):
+        value = r.stage[0, rows, :].astype(f32) + r.stage_core[0, rows, :].astype(f32)
+        value = value + r.stage_ring[0, rows, :].astype(f32)
+        value = value + r.stage_ring[1, rows, :].astype(f32)
+        r.total[rows, :] = value.astype(bf16)
+
+    tiles(half, 32, last)
+    for i, copy in enumerate(home_chip):
+        copy.start()
+        copy.wait()
+        copy.sent()
+
+        def join(rows, i=i):
+            value = r.total[rows, :].astype(f32) + r.from_chip[i, rows, :].astype(f32)
+            if i + 1 < len(bits):
+                r.total[rows, :] = value.astype(bf16)
+            else:
+                r.wide[rows, :] = value
+
+        tiles(half, 32, join)
+    keep_total = local(r.wide, r.d_total, 0)
+    keep_total.start()
+    ring_up[1].sent()
+    ring_down[1].sent()
     copies.finish()
-
-
-def gather_tokens(groups, lanes, part, hidden_half, gain, grad, ids):
+    keep_total.wait()
+
+
+def pad_last(array, size):
+    return jnp.pad(array, [(0, 0)] * (array.ndim - 1) + [(0, size - array.shape[-1])])
+
+
+def round_up(value, unit):
+    return -(-value // unit) * unit
+
+
+def run_experts(groups, lanes, part, hidden, gain, grad, ids, weights, router, capacity):
+    gate, up, down, s_gate, s_up, s_down = weights
     seq, width = grad.shape
+    ff_own = gate.shape[1]
+    units_true = s_gate.shape[1]
+    experts = router.shape[1] - 1
+    ff, units = 2 * ff_own, round_up(units_true, 128)
     half = seq // 2
     bits = (lanes // 2).bit_length() - 1
-    copies = 2 * groups + 2 + bits + groups * (bits + 4)
-    return pl.pallas_call(
-        functools.partial(gather_kernel, groups, lanes),
-        out_shape=(
-            jax.ShapeDtypeStruct((half, width), f32),
-            jax.ShapeDtypeStruct((half, width), bf16),
-            jax.ShapeDtypeStruct((groups, seq, width), bf16),
-            jax.ShapeDtypeStruct((groups, seq, width), bf16),
-            jax.ShapeDtypeStruct((groups,) + ids.shape, jnp.int32),
+    far = groups // 2
+    small_rows = round_up(experts + 1, 8)
+    z = Sizes(
+        groups=groups, lanes=lanes, seq=seq, width=width, ff=ff, units=units,
+        capacity=capacity, experts=experts,
+    )
+    s_in = jnp.concatenate([pad_last(s_gate, units), pad_last(s_up, units)], axis=1)
+    s_out = jnp.pad(s_down, ((0, units - units_true), (0, 0)))
+    router = pad_last(router, 128)
+    ins = {
+        "part": (part, in_place), "hidden": (hidden, in_place), "gain": (gain, whole),
+        "grad": (grad, in_place), "ids": (ids, whole), "gate": (gate, in_place),
+        "up": (up, in_place), "down": (down, in_place), "s_in_hbm": (s_in, in_place),
+        "s_out_hbm": (s_out, in_place), "router_hbm": (router, in_place),
+    }
+    rows_all = groups * capacity
+    outs = {
+        "normed": ((half, width), bf16, whole),
+        "small_total": ((small_rows, seq), f32, whole),
+        "resid": ((half, width), f32, in_place),
+        "d_total": ((half, width), f32, in_place),
+        "outs_all": ((groups, seq, width), bf16, in_place),
+        "g_gate": (gate.shape, f32, in_place),
+        "g_up": (up.shape, f32, in_place),
+        "g_down": (down.shape, f32, in_place),
+        "s_grads": ((groups, 3 * units, width // groups), bf16, in_place),
+        "tokens_all": ((groups, seq, width), bf16, in_place),
+        "grads_all": ((groups, seq, width), bf16, in_place),
+        "rows_all": ((rows_all, width), bf16, in_place),
+        "row_grads_all": ((rows_all, width), bf16, in_place),
+        "gated_all": ((rows_all, ff), bf16, in_place),
+        "d_a_all": ((rows_all, ff), bf16, in_place),
+        "d_b_all": ((rows_all, ff), bf16, in_place),
+        "s_gated_all": ((groups, seq, units), bf16, in_place),
+        "s_d_both_all": ((groups, seq, 2 * units), bf16, in_place),
+        "kept": ((groups, half, width), bf16, in_place),
+        "given": ((groups, half, width), bf16, in_place),
+        "from_ring": ((2 * far - 1, half, width), bf16, in_place),
+    }
+    copies = 3 + 2 * groups + (groups - 1) * (2 + bits) + groups + 1 + bits + 2 * far
+    copies += 2 * bits + 1
+    scratch = {
+        "ids_all": pltpu.VMEM((groups,) + ids.shape, jnp.int32),
+        "total": pltpu.VMEM((half, width), bf16),
+        "from_core": pltpu.VMEM((half, width), bf16),
+        "part_chip": pltpu.VMEM((max(bits, 1), half, width), bf16),
+        "from_chip": pltpu.VMEM((max(bits, 1), half, width), bf16),
+        "wide": pltpu.VMEM((half, width), f32),
+        "stage": pltpu.VMEM((4, half, width), bf16),
+        "stage_core": pltpu.VMEM((2, half, width), bf16),
+        "stage_ring": pltpu.VMEM((2, half, width), bf16),
+        "small_out": pltpu.VMEM((groups, 8, seq), f32),
+        "small_in": pltpu.VMEM((groups, 8, seq), f32),
+        "small_swap": pltpu.VMEM((2 * (1 + bits), small_rows, seq), f32),
+        "ranker": pltpu.VMEM((seq, seq), bf16),
+        "w_in": pltpu.VMEM((2 * ff, width), bf16),
+        "w_out": pltpu.VMEM((ff, width), bf16),
+        "s_in": pltpu.VMEM(s_in.shape, bf16),
+        "s_out": pltpu.VMEM(s_out.shape, bf16),
+        "router": pltpu.VMEM(router.shape, bf16),
+        "send_sems": pltpu.SemaphoreType.DMA((copies,)),
+        "recv_sems": pltpu.SemaphoreType.DMA((copies,)),
+        "local_sems": pltpu.SemaphoreType.DMA((25 + 2 * lanes,)),
+        "give_send": pltpu.SemaphoreType.DMA((groups,)),
+        "give_recv": pltpu.SemaphoreType.DMA((groups,)),
+        "small_send": pltpu.SemaphoreType.DMA((groups,)),
+        "small_recv": pltpu.SemaphoreType.DMA((groups,)),
+        "grad_send": pltpu.SemaphoreType.DMA((6,)),
+        "grad_recv": pltpu.SemaphoreType.DMA((3 * groups,)),
+    }
+    names = list(ins) + list(outs) + list(scratch)
+    results = pl.pallas_call(
+        functools.partial(experts_kernel, z, names),
+        out_shape=tuple(jax.ShapeDtypeStruct(s, d) for s, d, _ in outs.values()),
+        in_specs=[spec for _, spec in ins.values()],
+        out_specs=tuple(spec for _, _, spec in outs.values()),
+        scratch_shapes=list(scratch.values()),
+        compiler_params=pltpu.CompilerParams(
+            collective_id=0, has_side_effects=True, vmem_limit_bytes=63 * 1024 * 1024
         ),
-        in_specs=[whole, whole, whole, in_place, whole],
-        out_specs=(whole, whole, in_place, in_place, whole),
-        scratch_shapes=[
-            pltpu.VMEM((half, width), bf16),
-            pltpu.VMEM((half, width), bf16),
-            pltpu.VMEM((max(bits, 1), half, width), bf16),
-            pltpu.SemaphoreType.DMA((copies,)),
-            pltpu.SemaphoreType.DMA((copies,)),
-            pltpu.SemaphoreType.DMA((2,)),
-        ],
-        compiler_params=pltpu.CompilerParams(
-            collective_id=0, has_side_effects=True, vmem_limit_bytes=40 * 1024 * 1024
-        ),
-        name="gather_tokens",
-    )(part, hidden_half, gain, grad, ids)
+        name="run_experts",
+    )(*[array for array, _ in ins.values()])
+    return Sizes(**dict(zip(outs, results)), units=units)
 
 
 def reduce_kernel(
@@ -423,7 +1133,8 @@
         for i, bit in enumerate(bits):
             wait = copies.start(kept.at[home], from_chip.at[i], peers.other_chip(bit))
             wait()
-            copies.started.pop().wait_send()
+            copies.planned[-1][0].sent()
+            copies.planned[-1] = (copies.planned[-1][0], False)
 
             def join(rows, i=i):
                 value = kept[home, rows, :].astype(f32) + from_chip[i, rows, :].astype(f32)
@@ -497,95 +1208,6 @@
     inner = d_normed * gain
     mean = jnp.mean(inner * values, axis=-1, keepdims=True)
     return scale * inner - values * (scale * scale * scale) * mean
-
-
-def gated_backward(a, b, d_hidden):
-    sigma = jax.nn.sigmoid(a)
-    d_a = (d_hidden * b * sigma * (1.0 + a * (1.0 - sigma))).astype(bf16)
-    d_b = (d_hidden * a * sigma).astype(bf16)
-    return d_a, d_b
-
-
-class Experts:
-    def __init__(self, weights, router, w_sigmoid, first_expert, capacity):
-        (self.gate, self.up, self.down, self.s_gate, self.s_up, self.s_down) = weights
-        self.router = router
-        self.w_sigmoid = w_sigmoid
-        self.first = first_expert
-        self.capacity = capacity
-
-    def run(self, tokens, grads, ids):
-        held = self.gate.shape[0]
-        m, s, d = tokens.shape
-        local = jnp.arange(held, dtype=jnp.int32) + self.first
-        named = jnp.any(ids[:, None, :, :] == local[None, :, None, None], axis=2)
-        earlier = (jnp.arange(s)[:, None] < jnp.arange(s)[None, :]).astype(bf16)
-        rank = jnp.einsum(
-            "met,tu->meu", named.astype(bf16), earlier, preferred_element_type=f32
-        ).astype(jnp.int32)
-        place = jnp.where(named, rank, -1)
-        pick = (
-            place[:, :, None, :] == jnp.arange(self.capacity, dtype=jnp.int32)[None, None, :, None]
-        )
-        pick_flat = pick.astype(bf16).reshape(m, held * self.capacity, s)
-        shape4 = (m, held, self.capacity, d)
-        rows = jnp.einsum("mrt,mtd->mrd", pick_flat, tokens, preferred_element_type=f32)
-        rows = rows.astype(bf16).reshape(shape4)
-        row_grads = jnp.einsum("mrt,mtd->mrd", pick_flat, grads, preferred_element_type=f32)
-        row_grads = row_grads.astype(bf16).reshape(shape4)
-        logits = jnp.einsum("mtd,de->mte", tokens, self.router, preferred_element_type=f32)
-        probs = jax.nn.softmax(logits, axis=-1)
-        mine = lax.dynamic_slice_in_dim(probs, self.first, held, 2)
-        gate_rows = jnp.sum(
-            jnp.where(pick, jnp.swapaxes(mine, 1, 2)[:, :, None, :], 0.0), axis=-1, keepdims=True
-        )
-        sig = jax.nn.sigmoid(
-            jnp.einsum("mtd,d->mt", tokens, self.w_sigmoid, preferred_element_type=f32)
-        )[:, :, None]
-        a = jnp.einsum("mecd,edf->mecf", rows, self.gate, preferred_element_type=f32)
-        b = jnp.einsum("mecd,edf->mecf", rows, self.up, preferred_element_type=f32)
-        u = jnp.einsum("mecd,efd->mecf", row_grads, self.down, preferred_element_type=f32)
-        hidden = (jax.nn.silu(a) * b).astype(bf16).astype(f32)
-        d_gate_rows = jnp.sum(hidden * u, axis=-1, keepdims=True)
-        gated_hidden = (hidden * gate_rows).astype(bf16)
-        d_a, d_b = gated_backward(a, b, u * gate_rows)
-        out_rows = jnp.einsum(
-            "mecf,efd->mecd", gated_hidden, self.down, preferred_element_type=f32
-        ).astype(bf16)
-        in_rows = (
-            jnp.einsum("mecf,edf->mecd", d_a, self.gate, preferred_element_type=f32)
-            + jnp.einsum("mecf,edf->mecd", d_b, self.up, preferred_element_type=f32)
-        ).astype(bf16)
-        s_a = jnp.einsum("mtd,df->mtf", tokens, self.s_gate, preferred_element_type=f32)
-        s_b = jnp.einsum("mtd,df->mtf", tokens, self.s_up, preferred_element_type=f32)
-        s_u = jnp.einsum("mtd,fd->mtf", grads, self.s_down, preferred_element_type=f32)
-        s_hidden = (jax.nn.silu(s_a) * s_b).astype(bf16).astype(f32)
-        d_sig = jnp.sum(s_hidden * s_u, axis=-1)
-        s_gated = (s_hidden * sig).astype(bf16)
-        s_d_a, s_d_b = gated_backward(s_a, s_b, s_u * sig)
-        flat = (m, held * self.capacity, d)
-        outs = jnp.einsum(
-            "mrt,mrd->mtd", pick_flat, out_rows.reshape(flat), preferred_element_type=f32
-        ) + jnp.einsum("mtf,fd->mtd", s_gated, self.s_down, preferred_element_type=f32)
-        d_in = (
-            jnp.einsum("mrt,mrd->mtd", pick_flat, in_rows.reshape(flat), preferred_element_type=f32)
-            + jnp.einsum("mtf,df->mtd", s_d_a, self.s_gate, preferred_element_type=f32)
-            + jnp.einsum("mtf,df->mtd", s_d_b, self.s_up, preferred_element_type=f32)
-        )
-        d_gates = jnp.sum(jnp.where(pick, d_gate_rows, 0.0), axis=2)
-        saved = (rows, row_grads, gated_hidden, d_a, d_b, tokens, grads, s_gated, s_d_a, s_d_b)
-        return outs.astype(bf16), d_in.astype(bf16), d_gates, d_sig, saved
-
-    def weight_grads(self, saved):
-        rows, row_grads, gated_hidden, d_a, d_b, tokens, grads, s_gated, s_d_a, s_d_b = saved
-        return (
-            jnp.einsum("mecd,mecf->edf", rows, d_a, preferred_element_type=f32),
-            jnp.einsum("mecd,mecf->edf", rows, d_b, preferred_element_type=f32),
-            jnp.einsum("mecf,mecd->efd", gated_hidden, row_grads, preferred_element_type=f32),
-            jnp.einsum("mtd,mtf->df", tokens, s_d_a, preferred_element_type=f32),
-            jnp.einsum("mtd,mtf->df", tokens, s_d_b, preferred_element_type=f32),
-            jnp.einsum("mtf,mtd->fd", s_gated, grads, preferred_element_type=f32),
-        )
 
 
 def on_device(
@@ -673,51 +1295,36 @@
     context_flat = context.reshape(seq, head_all)
     gain_ffn = ffn_gain.astype(f32)
     ids = jnp.pad(expert_ids.T, ((0, -top_count % 8), (0, 0)), constant_values=-1)
-    resid, normed, tokens_all, grads_all, ids_all = gather_tokens(
+    units = shared_gate.shape[1] // groups
+    ex = run_experts(
         groups,
         lane_count,
         matmul(context_flat, w_output).astype(bf16),
-        half_of(hidden_in),
+        hidden_in,
         gain_ffn[None, :],
         grad_low,
         ids,
-    )
-
-    ffn_scale = rms_scale(resid)
-    logits = matmul(normed, w_router)
-    route_probs = jax.nn.softmax(logits, axis=-1)
-    sig = jax.nn.sigmoid(jnp.dot(normed, w_sigmoid, preferred_element_type=f32))
-
-    units = shared_gate.shape[1] // groups
-    experts = Experts(
         (
-            expert_gate,
-            expert_up,
+            jnp.swapaxes(expert_gate, 1, 2),
+            jnp.swapaxes(expert_up, 1, 2),
             expert_down,
             lax.dynamic_slice_in_dim(shared_gate, group * units, units, 1),
             lax.dynamic_slice_in_dim(shared_up, group * units, units, 1),
             lax.dynamic_slice_in_dim(shared_down, group * units, units, 0),
         ),
-        w_router,
-        w_sigmoid,
-        group * held,
+        jnp.concatenate([w_router, w_sigmoid[:, None]], axis=1),
         capacity,
     )
-    outs, d_in, d_gates, d_sig, saved = experts.run(tokens_all, grads_all, ids_all[:, :top_count])
-    g_gate, g_up, g_down, g_s_gate, g_s_up, g_s_down = experts.weight_grads(saved)
-
-    spread = (
-        (group * held + jnp.arange(held))[:, None] == jnp.arange(experts_all)[None, :]
-    ).astype(f32)
-    small = jnp.concatenate(
-        [
-            jnp.sum(d_gates[:, :, None, :] * spread[None, :, :, None], axis=1),
-            d_sig[:, None, :],
-            jnp.zeros((groups, -(experts_all + 1) % 8, seq), f32),
-        ],
-        axis=1,
-    )
-    d_in_sum, small = reduce_parts(groups, lane_count, d_in, small, True, 1)
+    resid, normed, outs, d_in_sum, small = (
+        ex.resid, ex.normed, ex.outs_all, ex.d_total, ex.small_total
+    )
+    g_gate, g_up, g_down = jnp.swapaxes(ex.g_gate, 1, 2), jnp.swapaxes(ex.g_up, 1, 2), ex.g_down
+
+    ffn_scale = rms_scale(resid)
+    logits = matmul(normed, w_router)
+    route_probs = jax.nn.softmax(logits, axis=-1)
+    sig = jax.nn.sigmoid(jnp.dot(normed, w_sigmoid, preferred_element_type=f32))
+
     small = half_of(small.T)
     d_probs_route, sig_grad = small[:, :experts_all], small[:, experts_all]
     d_logits = (
@@ -790,20 +1397,26 @@
     outs = lax.psum_scatter(
         outs.reshape(groups * seq, width), ("expert", "tensor"), scatter_dimension=0, tiled=True
     )
-    outs = lax.all_gather(outs, "tensor", axis=0, tiled=True)
-    layer_out = both_halves((resid + half_of(outs).astype(f32)).astype(bf16))
+    outs, grads = lax.optimization_barrier((outs, grads))
+    chip = lane // 2
+    piece = seq // lane_count
+    layer = lax.dynamic_slice_in_dim(resid, chip * piece, piece, 0) + outs.astype(f32)
+    layer = layer.astype(bf16)
+    for bit in range((lane_count // 2).bit_length() - 1):
+        other = swap(layer, 2 << bit)
+        low = (chip >> bit) % 2 == 0
+        layer = jnp.concatenate(
+            [jnp.where(low, layer, other), jnp.where(low, other, layer)], axis=0
+        )
+    layer_out = both_halves(layer)
     d_normed_in = sum_lanes(d_normed_attn.astype(bf16))
     grad_in = d_resid + norm_backward(half_of(hidden), half_of(attn_scale), gain_attn, d_normed_in)
     grad_in = both_halves(grad_in.astype(bf16))
 
-    wide = jnp.concatenate([g_s_gate, g_s_up], axis=1).astype(bf16)
-    wide = lax.all_to_all(wide, "expert", split_axis=0, concat_axis=1, tiled=True).astype(f32)
-    wide = wide.reshape(features, groups, 2, units)
-    grad_shared_gate = wide[:, :, 0].reshape(features, groups * units)
-    grad_shared_up = wide[:, :, 1].reshape(features, groups * units)
-    grad_shared_down = lax.all_to_all(
-        g_s_down.astype(bf16), "expert", split_axis=1, concat_axis=0, tiled=True
-    ).astype(f32)
+    shared = lax.all_to_all(ex.s_grads, "expert", split_axis=0, concat_axis=0, tiled=True)
+    shared = shared.reshape(groups, 3, ex.units, features)[:, :, :units].astype(f32)
+    shared = jnp.swapaxes(shared, 0, 1).reshape(3, groups * units, features)
+    grad_shared_gate, grad_shared_up, grad_shared_down = shared[0].T, shared[1].T, shared[2]
     return (
         layer_out,
         grad_in,

time: 937 us -> 733 us (0.78)
  the two profiles are of different devices: /device:TPU:21 before, /device:TPU:25 now
where the time goes in v2:
time: 733 us; the launch traced here: 722 us
  Pallas kernels  549 us (75%)
  local copies, waits for them, and re-layouts  55.6 us (8%)
  other arithmetic  45.7 us (6%)
  matrix products  31.9 us (4%)
  between operations  16.2 us (2%)
  starting transfers between devices  12.6 us (2%)
  waiting for transfers between devices  10.3 us (1%)
    pallas_call x1, Pallas kernels, run_experts(): pl.pallas_call(functools.partial(experts_kernel, z, names), out_shape=tup...  354 us
    pallas_call x1, Pallas kernels, reduce_parts(): pl.pallas_call(functools.partial(reduce_kernel, groups, lanes, tokens), o...  195 us
    unnamed x111, local copies, waits for them, and re-layouts  26.1 us
  transfers between devices with their start and end apart: 8, of which 1 were waited for; matrix products, arithmetic and copies ran while one was open for 11% of the time, Pallas kernels for 27%

profile of v2, /device:TPU:25, one launch (start us, length us, event | category | flops | bytes accessed | tf_op | source)
XLA Modules:
  0.0 721.8 jit_solution(15730501991923851246)
XLA Ops:
  8.1 2.1 multiply_reduce_fusion.2
  10.3 1.6 broadcast_multiply_fusion.2
  12.8 3.1 convolution_add_fusion.2
  15.9 1.4 convolution_add_fusion.1
  18.3 1.0 fusion.2
  19.4 0.9 exponential_reduce_fusion
  20.3 1.1 copy-done
  21.4 3.2 broadcast_select_fusion.refs_3_
  25.2 1.0 copy.72
  26.3 1.3 constant_dynamic-slice_fusion.6
  27.6 1.1 pad.26.refs_9_
  28.7 0.9 pad.27.refs_10_
  29.6 1.4 fusion.8
  31.7 1.4 convolution_convert_fusion.6
  33.3 2.6 convolution_convert_fusion.4.refs_0_
  35.9 2.9 constant_dynamic-slice_fusion.7
  38.9 1.7 fusion.5.refs_8_
  41.2 354.0 %run_experts.1 = (bf16[256,2048]{1,0:T(8,128)(2,1)}, f32[24,512]{1,0:T(8,128)}, f32[256,2048]{1,0:T(8,128)}, f32[256,2048]{1,0:T(8,128)}, bf16[8,512,2048]{2,1,0...) custom-call(bf16[512,2048]{1,0:T(8,128)(2,1)} %convolution_convert_f, ...), custom_call_target="tpu_custom_call" | custom-call | tf_op jit(solution)/shard_map/run_experts/pallas_call | solution.py:999
  397.4 2.6 multiply_reduce_fusion.5
  400.0 2.3 fusion.40
  402.3 1.9 collective-permute-start
  404.2 7.4 %all-to-all-start = ((bf16[8,768,256]{2,1,0:T(8,128)(2,1)}), bf16[8,768,256]{2,1,0:T(8,128)(2,1)}, u32[]{:S(2)}, u32[]{:S(2)}) async-start(bf16[8,768,256]{2,1,0:T(8,128)(2,1)} %get-tuple-element.41), calls=%async_computation.1 | async-start | bytes 6291456 | tf_op jit(solution)/shard_map/all_to_all | solution.py:1416
  411.6 2.5 convert_element_type.177
  415.6 1.7 fusion.10
  417.3 1.8 broadcast_select_fusion.6
  419.6 1.3 fusion.7
  421.0 1.2 copy-done.2
  422.3 1.6 multiply_reduce_fusion.1
  424.0 1.3 multiply_convert_fusion
  426.2 0.9 copy-done.17
  429.0 1.2 copy-done.25
  430.2 1.3 fusion.47
  431.9 1.3 fusion.48
  433.2 1.5 convert_reduce_fusion
  434.8 2.1 fusion.43
  436.9 1.3 copy-done.11
  438.2 1.0 constant_dynamic-slice_fusion.4
  439.7 3.0 convolution_convert_fusion
  442.6 1.4 convolution_convert_fusion.3
  444.0 1.4 convolution_convert_fusion.2
  445.5 1.4 convolution_convert_fusion.1
  447.0 1.6 add_convert_fusion.1
  448.9 4.1 pad_maximum_fusion
  453.1 12.4 %copy.78 = bf16[2048,2048]{1,0:T(8,128)(2,1)} copy(bf16[2048,2048]{0,1:T(8,128)(2,1)} %pad_maximum_fusion) | data formatting | bytes 16777216 | tf_op jit(solution)/shard_map/concatenate | solution.py:1360
  466.4 195.3 %reduce_weights.1 = (f32[256,2048]{1,0:T(8,128)}, f32[48,256]{1,0:T(8,128)}) custom-call(bf16[8,256,2048]{2,1,0:T(8,128)(2,1)} %bitcast.106, f32[8,48,256]{2,1,0:T(8,128)} %select_maximum_fusion.small), custom_call_target="tpu_custom_call" | custom-call | tf_op jit(solution)/shard_map/reduce_weights/pallas_call | solution.py:1157
  661.7 1.9 multiply_reduce_fusion.3
  664.2 3.7 add_convert_fusion
  667.9 2.0 collective-permute-start.5
  671.7 1.1 add_convert_fusion.2
  673.0 1.7 broadcast_select_fusion.2
  674.7 1.6 pad_maximum_fusion.3
  676.2 10.3 %collective-permute-done.1 = bf16[128,2048]{1,0:T(8,128)(2,1)S(1)} collective-permute-done((bf16[128,2048]{1,0:T(8,128)(2,1)S(1)}, bf16[128,2048]{1,0:T(8,128)(2,1)S(1)}, u32[]{:S(2)}, u32[]{:S(2)}) %collective-permute-start.1) | collective-permute-done | bytes 524320 | tf_op jit(solution)/shard_map/ppermute | solution.py:1257
  687.4 1.1 pad_maximum_fusion.8
  689.3 2.1 convert_bitcast_fusion
  691.4 1.5 fusion.42
  692.9 1.5 copy.82
  694.4 1.5 copy.83
  695.9 2.8 slice_bitcast_fusion
  698.8 1.0 copy.81
  699.8 1.8 broadcast_select_fusion.4
  701.6 1.6 pad_maximum_fusion.2
  703.1 6.3 copy.99
  709.5 2.5 copy.100
  712.0 2.5 copy.101
  (176 shorter events, 17.3 us)
Async XLA Ops:
  7.2 5.6 copy-start.3
  7.2 3.0 copy-start.42
  7.2 3.0 copy-start.43
  7.2 664.5 %reduce-scatter.2.cloned.1.call-start = ((), (), s32[]{:S(2)}) async-start(), calls=%async_computation.2 | async-start | bytes 17301504 | tf_op jit(solution)/shard_map/reduce_scatter | solution.py:1397
  12.0 5.7 copy-start.20
  12.8 3.1 copy-start.26
  18.3 1.0 copy-start.16
  18.3 1.0 copy-start.18
  19.3 2.0 copy-start
  19.3 2.0 copy-start.44
  21.4 3.2 copy-start.41
  21.4 3.8 copy-start.38
  21.4 3.8 copy-start.32
  26.3 2.4 copy-start.24
  26.3 3.3 copy-start.22
  29.6 2.2 copy-start.1
  31.0 2.1 copy-start.33
  31.7 1.6 copy-start.45
  33.1 2.8 copy-start.47
  38.9 1.7 copy-start.40
  395.2 1.2 copy-start.13
  395.2 2.1 copy-start.5
  395.2 2.1 copy-start.37
  397.4 2.6 copy-start.9
  399.9 2.4 copy-start.10
  402.3 15.0 %collective-permute-start = (bf16[256,2048]{1,0:T(8,128)(2,1)}, bf16[256,2048]{1,0:T(8,128)(2,1)}, u32[]{:S(2)}, u32[]{:S(2)}) collective-permute-start(bf16[256,2048]{1,0:T(8,128)(2,1)} %get-tuple-element.108), channel_id=1, source_target_pairs={{0,1},{1,0},{2,3},{3,2},{4,5},{5,4},{6,7},{7,6},{8,9},{9,8},{10,11... | collective-permute-start | bytes 3145736 | tf_op jit(solution)/shard_map/ppermute | solution.py:1257
  404.2 7.4 %copy-start.4 = (bf16[512,2048]{1,0:T(8,128)(2,1)S(1)}, bf16[512,2048]{1,0:T(8,128)(2,1)}, u32[]{:S(2)}) copy-start(bf16[512,2048]{1,0:T(8,128)(2,1)} %refs_1_.1) | copy-start | bytes 6291460
  404.2 285.1 %all-to-all-start = ((bf16[8,768,256]{2,1,0:T(8,128)(2,1)}), bf16[8,768,256]{2,1,0:T(8,128)(2,1)}, u32[]{:S(2)}, u32[]{:S(2)}) async-start(bf16[8,768,256]{2,1,0:T(8,128)(2,1)} %get-tuple-element.41), calls=%async_computation.1 | async-start | bytes 6291456 | tf_op jit(solution)/shard_map/all_to_all | solution.py:1416
  417.3 2.3 copy-start.46
  419.2 1.8 copy-start.28
  419.2 1.7 copy-start.29
  419.6 2.6 copy-start.2
  419.6 2.7 copy-start.34
  423.9 1.3 copy-start.19
  426.1 1.0 copy-start.17
  427.6 1.0 copy-start.21
  427.6 1.0 copy-start.30
  428.6 1.6 copy-start.25
  430.2 1.6 copy-start.27
  433.2 1.6 copy-start.23
  434.6 2.2 copy-start.35
  436.9 1.3 copy-start.11
  439.2 7.6 %collective-permute-start.3 = (bf16[256,2048]{1,0:T(8,128)(2,1)}, bf16[256,2048]{1,0:T(8,128)(2,1)}, u32[]{:S(2)}, u32[]{:S(2)}) collective-permute-start(bf16[256,2048]{1,0:T(8,128)(2,1)} %constant_dynamic-slice_fusion.4), channel_id=1, source_target_pairs={{0,1},{1,0},{2,3},{3,2},{4,5},{5,4},{6,7},{7,6},{8,9},{9,8},{10,11... | collective-permute-start | bytes 3145736 | tf_op jit(solution)/shard_map/ppermute | solution.py:1257
  444.0 1.4 copy-start.36
  445.4 1.6 copy-start.12
  448.7 213.0 %collective-permute-start.4 = (bf16[256,2048]{1,0:T(8,128)(2,1)S(1)}, bf16[256,2048]{1,0:T(8,128)(2,1)}, u32[]{:S(2)}, u32[]{:S(2)}) collective-permute-start(bf16[256,2048]{1,0:T(8,128)(2,1)S(1)} %add_convert_fusion.1), channel_id=1, source_target_pairs={{0,2},{1,3},{2,0},{3,1},{4,6},{5,7},{6,4},{7,5},{8,10},{9,11},{10,... | collective-permute-start | bytes 3145736 | tf_op jit(solution)/shard_map/ppermute | solution.py:1257
  453.1 12.4 %copy-start.31 = (f32[17,8,256]{2,0,1:T(8,128)S(1)}, f32[17,8,256]{2,0,1:T(8,128)}, u32[]{:S(2)}) copy-start(f32[17,8,256]{2,0,1:T(8,128)} %copy.79) | copy-start | bytes 417796
  466.4 195.4 %copy-start.7 = (f32[512,2048]{1,0:T(8,128)S(1)}, f32[512,2048]{1,0:T(8,128)}, u32[]{:S(2)}) copy-start(f32[512,2048]{1,0:T(8,128)} %convert_element_type.177) | copy-start | bytes 12582916
  661.7 2.5 copy-start.8
  664.2 5.7 copy-start.39
  664.2 7.5 %copy-start.6 = (f32[256,2048]{1,0:T(8,128)S(1)}, f32[256,2048]{1,0:T(8,128)}, u32[]{:S(2)}) copy-start(f32[256,2048]{1,0:T(8,128)} %get-tuple-element.32) | copy-start | bytes 6291460
  667.9 5.1 collective-permute-start.5
  672.9 13.6 %collective-permute-start.1 = (bf16[128,2048]{1,0:T(8,128)(2,1)S(1)}, bf16[128,2048]{1,0:T(8,128)(2,1)S(1)}, u32[]{:S(2)}, u32[]{:S(2)}) collective-permute-start(bf16[128,2048]{1,0:T(8,128)(2,1)S(1)} %add_convert_fusion.2), channel_id=1, source_target_pairs={{0,2},{1,3},{2,0},{3,1},{4,6},{5,7},{6,4},{7,5},{8,10},{9,11},{10,... | collective-permute-start | bytes 1572872 | tf_op jit(solution)/shard_map/ppermute | solution.py:1257
  686.6 0.8 copy-start.14
  688.5 11.3 %collective-permute-start.2 = (bf16[256,2048]{1,0:T(8,128)(2,1)}, bf16[256,2048]{1,0:T(8,128)(2,1)}, u32[]{:S(2)}, u32[]{:S(2)}) collective-permute-start(bf16[256,2048]{1,0:T(8,128)(2,1)} %pad_maximum_fusion.8), channel_id=1, source_target_pairs={{0,1},{1,0},{2,3},{3,2},{4,5},{5,4},{6,7},{7,6},{8,9},{9,8},{10,11... | collective-permute-start | bytes 3145736 | tf_op jit(solution)/shard_map/ppermute | solution.py:1257
  695.9 3.8 copy-start.15
  695.9 13.5 %slice-start.2 = ((s8[5767168]{0:T(1024)(128)(4,1)}), s8[1572864]{0:T(1024)(128)(4,1)S(1)}, s32[]{:S(2)}) async-start(s8[5767168]{0:T(1024)(128)(4,1)} %bitcast.110), calls=%async_computation.5 | async-start | bytes 3145728
  701.5 7.9 %slice-start.3 = ((s8[5767168]{0:T(1024)(128)(4,1)}), s8[4194304]{0:T(1024)(128)(4,1)S(1)}, s32[]{:S(2)}) async-start(s8[5767168]{0:T(1024)(128)(4,1)} %bitcast.110), calls=%async_computation.6 | async-start | bytes 8388608
  703.1 8.9 %slice-start = ((s8[5767168]{0:T(1024)(128)(4,1)}), s8[4194304]{0:T(1024)(128)(4,1)S(1)}, s32[]{:S(2)}) async-start(s8[5767168]{0:T(1024)(128)(4,1)} %bitcast.108), calls=%async_computation.3 | async-start | bytes 8388608
  709.5 2.5 slice-start.1
Sparse Core Ops, SparseCore 0:
  395.4 255.4 reduce-scatter.1

commit v3 on v2

--- a/solution.py
+++ b/solution.py
@@ -127,6 +127,70 @@
 class Planned:
     def __init__(self, mine, theirs):
         self.start, self.sent, self.wait = mine.start, mine.wait_send, theirs.wait_recv
+
+
+class RingSum:
+    def __init__(self, copies, peers, stage, received, rows, places, first=1, last=None, eager=False):
+        far = peers.far
+        self.far, self.size, self.first, self.eager = far, rows // 2, first, eager
+        self.places = places
+        self.copies = {}
+        for j in range(first, 2 * far if last is None else last + 1):
+            for way, peer in ((0, peers.at(1)), (1, peers.at(-1))):
+                at = pl.ds(self.start(j, way), self.size)
+                self.copies[j, way] = copies.plan(
+                    stage.at[self.place(j, way), at],
+                    received.at[way, j - 1],
+                    peer,
+                    ends=False,
+                )
+
+    def offset(self, j, way):
+        k = self.far - j // 2
+        return k if way == 0 or k == self.far else -k
+
+    def start(self, j, way):
+        return self.size * ((j + 1 + way) % 2)
+
+    def place(self, j, way):
+        return self.places(self.offset(j, way), way)
+
+    def step(self, j, prepare, merge):
+        if j % 2 == 0 or j == self.first:
+            for way in (0, 1):
+                for old in (j - 4, j - 3):
+                    if (old, way) in self.copies and j % 2 == 0:
+                        self.copies[old, way].sent()
+            for way in (0, 1) if j > 1 else (0,):
+                prepare(self.offset(j, way), way)
+        for way in (0, 1):
+            before = (way, j - 3) if j > 2 else None
+            if self.eager and j - 2 >= self.first:
+                self.copies[j - 2, way].wait()
+            merge(self.place(j, way), way if j > 1 else 0, self.start(j, way), self.size, before)
+            if self.eager:
+                self.copies[j, way].start()
+        if self.eager:
+            return
+        for way in (0, 1):
+            if j > self.first:
+                self.copies[j - 1, way].wait()
+            self.copies[j, way].start()
+
+    def arrived(self):
+        for j in (2 * self.far - 2, 2 * self.far - 1)[0 if self.eager else 1 :]:
+            for way in (0, 1):
+                self.copies[j, way].wait()
+        return [
+            (way, j - 1, self.start(j, way))
+            for j in (2 * self.far - 2, 2 * self.far - 1)
+            for way in (0, 1)
+        ]
+
+    def finish(self, unsent):
+        for j in unsent:
+            for way in (0, 1):
+                self.copies[j, way].sent()
 
 
 def tiles(rows, size, step):
@@ -386,21 +450,14 @@
         for i, b in enumerate(bits)
     ]
 
-    ring_up, ring_down = {}, {}
-    lower, upper, all_rows = pl.ds(0, half // 2), pl.ds(half // 2, half // 2), pl.ds(0, half)
-    for k in range(far, 0, -1):
-        rows_up, rows_down = (lower, upper) if k == far else (all_rows, all_rows)
-        at_up, at_down = (0, 0) if k == far else (2 * (far - k) - 1, 2 * (far - k))
-        odd = k % 2
-        ring_up[k] = copies.plan(
-            r.stage.at[odd, rows_up], r.from_ring.at[at_up, rows_up], ahead, ends=False
-        )
-        ring_down[k] = copies.plan(
-            r.stage.at[odd if k == far else 2 + odd, rows_down],
-            r.from_ring.at[at_down, rows_down],
-            behind,
-            ends=False,
-        )
+    d_ring = RingSum(
+        copies, peers, r.stage, r.from_ring, half,
+        lambda k, way: k % 2 + (2 * way if abs(k) < far else 0), eager=True,
+    )
+    y_ring = RingSum(
+        copies, peers, r.stage, r.y_early, half,
+        lambda k, way: k % 2 + (2 * way if abs(k) < far else 0), last=2,
+    )
     home_chip = [
         copies.plan(r.total, r.from_chip.at[i], chip_peer[b], ends=False)
         for i, b in enumerate(bits)
@@ -480,7 +537,7 @@
                     g_chip[k][i + 1].start()
             g_core[k].start()
 
-    def events(p):
+    def forward(p):
         for q in range(far):
 
             @pl.when(p == q)
@@ -493,7 +550,7 @@
                     if k + 1 == far:
                         x_ring[-far].start()
                         x_ring[far].start()
-                    for s in (-1, 1):
+                    for s in (1, -1):
                         x_core[s * k].start()
                 else:
                     x_ring[-far].wait()
@@ -508,12 +565,18 @@
                     g_ring[-far].wait()
                     g_ring[far].wait()
                     g_chip[far][0].start()
-                finish_grads([-k, k] if k < far else [far])
+                finish_grads([k, -k] if k < far else [far])
                 x_core[1 - k].wait()
+                if k > 1:
+                    g_core[1 - k].wait()
+
+    def complete(p):
+        for q in range(far):
+
+            @pl.when(p == q)
+            def _(k=q + 1):
                 x_core[k].wait()
                 g_core[k].wait()
-                if k > 1:
-                    g_core[1 - k].wait()
 
     def small_copy(i, peer):
         return remote(
@@ -522,6 +585,9 @@
 
     def given_copy(i, source):
         return remote(source, r.given.at[i], r.give_send.at[i], r.give_recv.at[i], core_peer)
+
+    def y_given_copy(i, source):
+        return remote(source, r.y_given.at[i], r.y_send.at[i], r.y_recv.at[i], core_peer)
 
     def main(tokens, grads, rows, row_grads, d_rows, out_rows, gated, d_a, d_b, s_gated,
              s_d_both, out, d_in, pick, put):
@@ -545,29 +611,36 @@
                 sent = given_copy(i, d_in.at[give])
                 kept = local(d_in.at[keep], r.kept.at[i], 12 + s)
                 found += [(kept.start, kept.wait), (sent.start, sent.wait_send)]
-                for lane in range(lanes):
-                    from_row = s * seq + (lane % 2 * peers.chips + lane // 2) * piece
-                    stored = local(
-                        out.at[pl.ds(from_row, piece)],
-                        r.outs_all.at[slots[s], pl.ds(lane * piece, piece)],
-                        25 + s * lanes + lane,
-                    )
-                    found.append((stored.start, stored.wait))
+                sent = y_given_copy(i, out.at[give])
+                found.append((sent.start, sent.wait_send))
+                stored = local(out.at[pl.ds(s * seq, seq)], r.outs_all.at[slots[s]], 14 + s)
+                found.append((stored.start, stored.wait))
             return found
+
+        def arrivals(p, s):
+            slot_now = peers.group_at(p + 1 if s else -p)
+            at = pl.ds(s * seq, seq)
+            return [
+                local(r.tokens_all.at[slot_now], tokens.at[at], s),
+                local(r.grads_all.at[slot_now], grads.at[at], 2 + s),
+            ]
+
+        def load(p, s):
+            @pl.when(p < far)
+            def _():
+                for copy in arrivals(p, s):
+                    copy.start()
+
+        forward(0)
+        load(0, 0)
+        complete(0)
+        load(0, 1)
 
         def loop(p, carry):
             slots = [peers.group_at(-p), peers.group_at(p + 1)]
-            events(p)
-            loads = []
-            for s in range(2):
-                at = pl.ds(s * seq, seq)
-                loads.append(local(r.tokens_all.at[slots[s]], tokens.at[at], s))
-                loads.append(local(r.grads_all.at[slots[s]], grads.at[at], 2 + s))
-            for copy in loads:
-                copy.start()
             for s in range(2):
                 work.place(s, r.ids_all[slots[s]])
-            for copy in loads:
+            for copy in arrivals(p, 0) + arrivals(p, 1):
                 copy.wait()
             at = pl.ds(pl.multiple_of(p * 2 * z.capacity, 2 * z.capacity), 2 * z.capacity)
             saves = [
@@ -596,6 +669,8 @@
             work.shared(small)
             for copy in saves[5:]:
                 copy.start()
+            forward(p + 1)
+            load(p + 1, 0)
             small_copy(2 * p + 1, (slots[1], peers.lane)).start()
 
             @pl.when(p > 0)
@@ -607,6 +682,8 @@
             work.give()
             for start, _ in leave(p, slots):
                 start()
+            complete(p + 1)
+            load(p + 1, 1)
             for copy in saves:
                 copy.wait()
             return carry
@@ -646,51 +723,29 @@
         for copy in loads:
             copy.wait()
 
-    def arrived(ring, index, rows, place):
-        ring.wait()
-        copy = local(r.from_ring.at[index, rows], r.stage_ring.at[place, rows], 2 + place)
-        copy.start()
-        copy.wait()
-
-    def add(place, core_place, start, size, ring_place=None):
+    def prepare(k, way):
+        fetch(k, d_ring.places(k, way), way)
+
+    def merge(place, core_place, start, size, before):
+        if before is not None:
+            copy = local(r.from_ring.at[before], r.stage_ring.at[core_place], 2)
+            copy.start()
+            copy.wait()
+
         def step(rows):
-            at = pl.ds(pl.multiple_of(start + rows.start, rows.size), rows.size)
+            at = pl.ds(start + rows.start, rows.size)
             value = r.stage[place, at, :].astype(f32) + r.stage_core[core_place, at, :].astype(f32)
-            if ring_place is not None:
-                value = value + r.stage_ring[ring_place, at, :].astype(f32)
+            if before is not None:
+                value = value + r.stage_ring[core_place, rows, :].astype(f32)
             r.stage[place, at, :] = value.astype(bf16)
 
         tiles(size, 32, step)
 
-    def ring_stage(k):
-        odd = k % 2
-        if k + 2 <= far:
-            ring_up[k + 2].sent()
-            ring_down[k + 2].sent()
-        fetch(k, odd, 0)
-        fetch(-k, 2 + odd, 1)
-        at = 0 if k == far - 1 else 2 * (far - k) - 3
-        if k == far - 1:
-            add(odd, 0, half // 2, half // 2)
-            add(2 + odd, 1, 0, half // 2)
-            arrived(ring_up[far], 0, lower, 0)
-            add(odd, 0, 0, half // 2, 0)
-        else:
-            arrived(ring_up[k + 1], at, all_rows, 0)
-            add(odd, 0, 0, half, 0)
-        ring_up[k].start()
-        if k == far - 1:
-            arrived(ring_down[far], 0, upper, 1)
-            add(2 + odd, 1, half // 2, half // 2, 1)
-        else:
-            arrived(ring_down[k + 1], at + 1, all_rows, 1)
-            add(2 + odd, 1, 0, half, 1)
-        ring_down[k].start()
-
-    fetch(far, far % 2, 0)
-    add(far % 2, 0, 0, half)
-    ring_up[far].start()
-    ring_down[far].start()
+    def ring_step(j):
+        d_ring.step(j, prepare, merge)
+
+    ring_step(1)
+    ring_step(2)
 
     features = z.width // groups
 
@@ -756,9 +811,9 @@
             def _():
                 settle(t - 2)
 
-            wide_in[odd, pl.ds(0, z.ff), :] = contract_rows(d_a[...], rows[odd])
-            wide_in[odd, pl.ds(z.ff, z.ff), :] = contract_rows(d_b[...], rows[odd])
-            wide_out[odd] = contract_rows(gated[...], row_grads[odd])
+            wide_in[odd, pl.ds(0, z.ff), :] = contract_rows(d_a[...], rows[odd]).astype(bf16)
+            wide_in[odd, pl.ds(z.ff, z.ff), :] = contract_rows(d_b[...], rows[odd]).astype(bf16)
+            wide_out[odd] = contract_rows(gated[...], row_grads[odd]).astype(bf16)
             for kept, sent in stores(t):
                 kept.start()
                 sent.start()
@@ -768,9 +823,10 @@
             copy.start()
         for copy in whole_loads:
             copy.wait()
-        lax.fori_loop(0, groups // 2, unit, 0)
-        ring_stage(far - 1)
-        lax.fori_loop(groups // 2, groups, unit, 0)
+        for n in range(3):
+            lax.fori_loop(groups * n // 3, groups * (n + 1) // 3, unit, 0)
+            if n < 2:
+                ring_step(3 + n)
         settle(groups - 2)
         settle(groups - 1)
 
@@ -782,8 +838,8 @@
         d_b=pltpu.VMEM((tile_rows, z.ff), bf16),
         rows=pltpu.VMEM((2, tile_rows, features), bf16),
         row_grads=pltpu.VMEM((2, tile_rows, features), bf16),
-        wide_in=pltpu.VMEM((2, 2 * z.ff, features), f32),
-        wide_out=pltpu.VMEM((2, z.ff, features), f32),
+        wide_in=pltpu.VMEM((2, 2 * z.ff, features), bf16),
+        wide_out=pltpu.VMEM((2, z.ff, features), bf16),
     )
 
     def shared_grads(s_gated, s_d_both, tokens, grads, wide):
@@ -820,9 +876,10 @@
                 store(t - 2).wait()
 
             both = contract_rows(flat(s_d_both[...]), flat(tokens[odd]))
-            wide[odd, pl.ds(0, 2 * z.units), :] = both.astype(bf16)
             out = contract_rows(flat(s_gated[...]), flat(grads[odd]))
-            wide[odd, pl.ds(2 * z.units, z.units), :] = out.astype(bf16)
+            used = z.units_used
+            for n, part in enumerate((both[:used], both[z.units : z.units + used], out[:used])):
+                wide[odd, pl.ds(n * used, used), :] = part.astype(bf16)
             store(t).start()
             return carry
 
@@ -830,13 +887,10 @@
             copy.start()
         for copy in whole_loads:
             copy.wait()
-        stages = list(range(far - 2, 0, -1))
-        done = 0
-        for n, k in enumerate(stages):
-            upto = groups * (n + 1) // len(stages) if n + 1 < len(stages) else groups
-            lax.fori_loop(done, upto, unit, 0)
-            done = upto
-            ring_stage(k)
+        todo = list(range(5, 2 * far))
+        for n, j in enumerate(todo):
+            ring_step(j)
+            lax.fori_loop(groups * n // len(todo), groups * (n + 1) // len(todo), unit, 0)
         store(groups - 2).wait()
         store(groups - 1).wait()
 
@@ -846,10 +900,9 @@
         s_d_both=pltpu.VMEM((groups, seq, 2 * z.units), bf16),
         tokens=pltpu.VMEM((2, groups, seq, features), bf16),
         grads=pltpu.VMEM((2, groups, seq, features), bf16),
-        wide=pltpu.VMEM((2, 3 * z.units, features), bf16),
-    )
-    ring_up[2].sent()
-    ring_down[2].sent()
+        wide=pltpu.VMEM((2, 3 * z.units_used, features), bf16),
+    )
+    d_ring.finish(range(2 * far - 4, 2 * far - 2))
     fetch(0, 0, 0)
 
     r.small_total[...] = jnp.zeros_like(r.small_total)
@@ -876,19 +929,47 @@
                 arriving, arriving, r.grad_send.at[0], r.grad_recv.at[n * groups + t], core_peer
             ).wait_recv()
 
-    last_at = 2 * (far - 1) - 1
-    arrived(ring_up[1], last_at, all_rows, 0)
-    arrived(ring_down[1], last_at + 1, all_rows, 1)
-
-    def last(rows):
-        value = r.stage[0, rows, :].astype(f32) + r.stage_core[0, rows, :].astype(f32)
-        value = value + r.stage_ring[0, rows, :].astype(f32)
-        value = value + r.stage_ring[1, rows, :].astype(f32)
-        r.total[rows, :] = value.astype(bf16)
-
-    tiles(half, 32, last)
+    def last(way, index, start):
+        copy = local(r.from_ring.at[way, index], r.stage_ring.at[0], 2)
+        copy.start()
+        copy.wait()
+
+        def step(rows):
+            at = pl.ds(start + rows.start, rows.size)
+            value = r.wide[at, :] + r.stage_ring[0, rows, :].astype(f32)
+            r.wide[at, :] = value
+            r.total[at, :] = value.astype(bf16)
+
+        tiles(half // 2, 32, step)
+
+    def first_of_home(rows):
+        both = r.stage[0, rows, :].astype(f32) + r.stage_core[0, rows, :].astype(f32)
+        r.wide[rows, :] = both
+
+    tiles(half, 32, first_of_home)
+    for chunk in d_ring.arrived():
+        last(*chunk)
+    d_ring.finish(range(2 * far - 2, 2 * far))
+
+    def y_prepare(k, way):
+        loads = [
+            local(r.outs_all.at[slot[k], half_rows], r.stage.at[y_ring.places(k, way)], 0),
+            local(r.y_given.at[step_of[k]], r.stage_core.at[way], 1),
+        ]
+        for copy in loads:
+            copy.start()
+        for copy in loads:
+            copy.wait()
+
+    home_chip[0].start()
+    for k in peers.offsets():
+        i = step_of[k]
+        y_given_copy(i, r.y_given.at[i]).wait_recv()
+    y_ring.step(1, y_prepare, merge)
+    y_ring.step(2, y_prepare, merge)
     for i, copy in enumerate(home_chip):
-        copy.start()
+        if i > 0:
+            copy.start()
         copy.wait()
         copy.sent()
 
@@ -902,8 +983,9 @@
         tiles(half, 32, join)
     keep_total = local(r.wide, r.d_total, 0)
     keep_total.start()
-    ring_up[1].sent()
-    ring_down[1].sent()
+    for way in (0, 1):
+        y_ring.copies[2, way].wait()
+    y_ring.finish((1, 2))
     copies.finish()
     keep_total.wait()
 
@@ -929,72 +1011,76 @@
     small_rows = round_up(experts + 1, 8)
     z = Sizes(
         groups=groups, lanes=lanes, seq=seq, width=width, ff=ff, units=units,
-        capacity=capacity, experts=experts,
+        capacity=capacity, experts=experts, units_used=round_up(units_true, 16),
     )
     s_in = jnp.concatenate([pad_last(s_gate, units), pad_last(s_up, units)], axis=1)
     s_out = jnp.pad(s_down, ((0, units - units_true), (0, 0)))
     router = pad_last(router, 128)
-    ins = {
-        "part": (part, in_place), "hidden": (hidden, in_place), "gain": (gain, whole),
-        "grad": (grad, in_place), "ids": (ids, whole), "gate": (gate, in_place),
-        "up": (up, in_place), "down": (down, in_place), "s_in_hbm": (s_in, in_place),
-        "s_out_hbm": (s_out, in_place), "router_hbm": (router, in_place),
-    }
+    ins = dict(
+        part=(part, in_place), hidden=(hidden, in_place), gain=(gain, whole),
+        grad=(grad, in_place), ids=(ids, whole), gate=(gate, in_place),
+        up=(up, in_place), down=(down, in_place), s_in_hbm=(s_in, in_place),
+        s_out_hbm=(s_out, in_place), router_hbm=(router, in_place),
+    )
     rows_all = groups * capacity
-    outs = {
-        "normed": ((half, width), bf16, whole),
-        "small_total": ((small_rows, seq), f32, whole),
-        "resid": ((half, width), f32, in_place),
-        "d_total": ((half, width), f32, in_place),
-        "outs_all": ((groups, seq, width), bf16, in_place),
-        "g_gate": (gate.shape, f32, in_place),
-        "g_up": (up.shape, f32, in_place),
-        "g_down": (down.shape, f32, in_place),
-        "s_grads": ((groups, 3 * units, width // groups), bf16, in_place),
-        "tokens_all": ((groups, seq, width), bf16, in_place),
-        "grads_all": ((groups, seq, width), bf16, in_place),
-        "rows_all": ((rows_all, width), bf16, in_place),
-        "row_grads_all": ((rows_all, width), bf16, in_place),
-        "gated_all": ((rows_all, ff), bf16, in_place),
-        "d_a_all": ((rows_all, ff), bf16, in_place),
-        "d_b_all": ((rows_all, ff), bf16, in_place),
-        "s_gated_all": ((groups, seq, units), bf16, in_place),
-        "s_d_both_all": ((groups, seq, 2 * units), bf16, in_place),
-        "kept": ((groups, half, width), bf16, in_place),
-        "given": ((groups, half, width), bf16, in_place),
-        "from_ring": ((2 * far - 1, half, width), bf16, in_place),
-    }
-    copies = 3 + 2 * groups + (groups - 1) * (2 + bits) + groups + 1 + bits + 2 * far
+    outs = dict(
+        normed=((half, width), bf16, whole),
+        small_total=((small_rows, seq), f32, whole),
+        resid=((half, width), f32, in_place),
+        d_total=((half, width), f32, in_place),
+        outs_all=((groups, seq, width), bf16, in_place),
+        g_gate=(gate.shape, bf16, in_place),
+        g_up=(up.shape, bf16, in_place),
+        g_down=(down.shape, bf16, in_place),
+        s_grads=((groups, 3 * z.units_used, width // groups), bf16, in_place),
+        tokens_all=((groups, seq, width), bf16, in_place),
+        grads_all=((groups, seq, width), bf16, in_place),
+        rows_all=((rows_all, width), bf16, in_place),
+        row_grads_all=((rows_all, width), bf16, in_place),
+        gated_all=((rows_all, ff), bf16, in_place),
+        d_a_all=((rows_all, ff), bf16, in_place),
+        d_b_all=((rows_all, ff), bf16, in_place),
+        s_gated_all=((groups, seq, units), bf16, in_place),
+        s_d_both_all=((groups, seq, 2 * units), bf16, in_place),
+        kept=((groups, half, width), bf16, in_place),
+        given=((groups, half, width), bf16, in_place),
+        y_given=((groups, half, width), bf16, in_place),
+        y_early=((2, 2, half // 2, width), bf16, in_place),
+        from_ring=((2, 2 * far - 1, half // 2, width), bf16, in_place),
+    )
+    copies = 4 + 3 + 2 * groups + (groups - 1) * (2 + bits) + groups + 1 + bits + 4 * far
     copies += 2 * bits + 1
-    scratch = {
-        "ids_all": pltpu.VMEM((groups,) + ids.shape, jnp.int32),
-        "total": pltpu.VMEM((half, width), bf16),
-        "from_core": pltpu.VMEM((half, width), bf16),
-        "part_chip": pltpu.VMEM((max(bits, 1), half, width), bf16),
-        "from_chip": pltpu.VMEM((max(bits, 1), half, width), bf16),
-        "wide": pltpu.VMEM((half, width), f32),
-        "stage": pltpu.VMEM((4, half, width), bf16),
-        "stage_core": pltpu.VMEM((2, half, width), bf16),
-        "stage_ring": pltpu.VMEM((2, half, width), bf16),
-        "small_out": pltpu.VMEM((groups, 8, seq), f32),
-        "small_in": pltpu.VMEM((groups, 8, seq), f32),
-        "small_swap": pltpu.VMEM((2 * (1 + bits), small_rows, seq), f32),
-        "ranker": pltpu.VMEM((seq, seq), bf16),
-        "w_in": pltpu.VMEM((2 * ff, width), bf16),
-        "w_out": pltpu.VMEM((ff, width), bf16),
-        "s_in": pltpu.VMEM(s_in.shape, bf16),
-        "s_out": pltpu.VMEM(s_out.shape, bf16),
-        "router": pltpu.VMEM(router.shape, bf16),
-        "send_sems": pltpu.SemaphoreType.DMA((copies,)),
-        "recv_sems": pltpu.SemaphoreType.DMA((copies,)),
-        "local_sems": pltpu.SemaphoreType.DMA((25 + 2 * lanes,)),
-        "give_send": pltpu.SemaphoreType.DMA((groups,)),
-        "give_recv": pltpu.SemaphoreType.DMA((groups,)),
-        "small_send": pltpu.SemaphoreType.DMA((groups,)),
-        "small_recv": pltpu.SemaphoreType.DMA((groups,)),
-        "grad_send": pltpu.SemaphoreType.DMA((6,)),
-        "grad_recv": pltpu.SemaphoreType.DMA((3 * groups,)),
-    }
+    scratch = dict(
+        ids_all=pltpu.VMEM((groups,) + ids.shape, jnp.int32),
+        total=pltpu.VMEM((half, width), bf16),
+        from_core=pltpu.VMEM((half, width), bf16),
+        part_chip=pltpu.VMEM((max(bits, 1), half, width), bf16),
+        from_chip=pltpu.VMEM((max(bits, 1), half, width), bf16),
+        wide=pltpu.VMEM((half, width), f32),
+        stage=pltpu.VMEM((4, half, width), bf16),
+        stage_core=pltpu.VMEM((2, half, width), bf16),
+        stage_ring=pltpu.VMEM((2, half // 2, width), bf16),
+        small_out=pltpu.VMEM((groups, 8, seq), f32),
+        small_in=pltpu.VMEM((groups, 8, seq), f32),
+        small_swap=pltpu.VMEM((2 * (1 + bits), small_rows, seq), f32),
+        ranker=pltpu.VMEM((seq, seq), bf16),
+        w_in=pltpu.VMEM((2 * ff, width), bf16),
+        w_out=pltpu.VMEM((ff, width), bf16),
+        s_in=pltpu.VMEM(s_in.shape, bf16),
+        s_out=pltpu.VMEM(s_out.shape, bf16),
+        router=pltpu.VMEM(router.shape, bf16),
+        send_sems=pltpu.SemaphoreType.DMA((copies,)),
+        recv_sems=pltpu.SemaphoreType.DMA((copies,)),
+        local_sems=pltpu.SemaphoreType.DMA((25,)),
+        give_send=pltpu.SemaphoreType.DMA((groups,)),
+        give_recv=pltpu.SemaphoreType.DMA((groups,)),
+        y_send=pltpu.SemaphoreType.DMA((groups,)),
+        y_recv=pltpu.SemaphoreType.DMA((groups,)),
+        small_send=pltpu.SemaphoreType.DMA((groups,)),
+        small_recv=pltpu.SemaphoreType.DMA((groups,)),
+        grad_send=pltpu.SemaphoreType.DMA((6,)),
+        grad_recv=pltpu.SemaphoreType.DMA((3 * groups,)),
+    )
     names = list(ins) + list(outs) + list(scratch)
     results = pl.pallas_call(
         functools.partial(experts_kernel, z, names),
@@ -1007,179 +1093,373 @@
         ),
         name="run_experts",
     )(*[array for array, _ in ins.values()])
-    return Sizes(**dict(zip(outs, results)), units=units)
-
-
-def reduce_kernel(
-    groups, lanes, tokens, parts, small,
-    total, small_total,
-    kept, from_core, from_ring, from_chip, small_in, small_swap,
-    send_sems, recv_sems, local_sems,
-):
+    return Sizes(**dict(zip(outs, results)), units=z.units_used)
+
+
+def finish_kernel(z, names, *refs):
+    r = Sizes(**dict(zip(names, refs)))
+    groups, lanes = z.groups, z.lanes
     peers = Peers(groups, lanes)
     far, bits = peers.far, peers.chip_bits()
-    rows_all = kept.shape[1]
-    half = rows_all // 2
+    seq, heads, head, features = z.seq, z.heads, z.head, z.features
+    head_all = heads * head
+    half = seq // 2
+    own = peers.core * half
+    half_rows = pl.ds(pl.multiple_of(own, half), half)
+    other_rows = pl.ds(pl.multiple_of(half - own, half), half)
     me = peers.group
-    offsets = [far] + [s * k for k in range(far - 1, 0, -1) for s in (1, -1)] + [0]
-    number = {k: i for i, k in enumerate(offsets)}
-    others = [k for k in offsets if k != 0]
-    peers.meet(
-        [peers.at(k) for k in others]
-        + [peers.other_core()]
-        + [peers.other_chip(b) for b in bits]
-    )
-    copies = Copies(send_sems, recv_sems)
-    if tokens:
-        keep_rows = pl.ds(pl.multiple_of(peers.core * rows_all, rows_all), rows_all)
-        give_rows = pl.ds(pl.multiple_of((1 - peers.core) * rows_all, rows_all), rows_all)
-    loads, given = {}, {}
-    for k in offsets:
-        slot = peers.group_at(k)
-        source = parts.at[slot, keep_rows] if tokens else parts.at[slot]
-        loads[k] = pltpu.make_async_copy(source, kept.at[number[k]], local_sems.at[number[k]])
-        loads[k].start()
-        if tokens:
-            given[k] = copies.start(
-                parts.at[slot, give_rows], from_core.at[number[k]], peers.other_core()
-            )
-    small_got = [
-        copies.start(small.at[peers.group_at(k)], small_in.at[number[k]], peers.at(k))
+    others = [k for k in peers.offsets() if k != 0]
+    step_of = {k: 2 * k - 1 if k > 0 else -2 * k for k in peers.offsets()}
+    slot = {k: peers.group_at(k) for k in range(-far, far + 1)}
+    ahead, behind = peers.at(1), peers.at(-1)
+    core_peer = peers.other_core()
+    chip_peer = {b: peers.other_chip(b) for b in bits}
+    peers.meet([peers.at(k) for k in others] + [core_peer] + [chip_peer[b] for b in bits])
+    copies = Copies(r.send_sems, r.recv_sems)
+
+    def local(source, target, number):
+        return pltpu.make_async_copy(source, target, r.local_sems.at[number])
+
+    attn_core = copies.plan(
+        r.d_attn_half, r.d_attn.at[half_rows], core_peer, r.d_attn.at[other_rows]
+    )
+    own_attn = local(r.d_attn_half, r.d_attn.at[half_rows], 0)
+
+    y_ring = RingSum(
+        copies, peers, r.stage, r.from_ring, half,
+        lambda k, way: k % 2 + (2 * way if abs(k) < far else 0), first=3, eager=True,
+    )
+    w_ring = RingSum(
+        copies, peers, r.w_parts, r.w_received, features, lambda k, way: step_of[k], eager=True
+    )
+    y_chip = [
+        copies.plan(r.total, r.from_chip.at[i], chip_peer[b], ends=False)
+        for i, b in enumerate(bits)
+    ]
+    layer_core = copies.plan(
+        r.layer_half, r.layer_out.at[half_rows], core_peer, r.layer_out.at[other_rows]
+    )
+    norm_core = copies.plan(r.d_norm.at[other_rows], r.norm_core, core_peer)
+    norm_chip = [
+        copies.plan(r.norm_total, r.norm_chip.at[i], chip_peer[b], ends=False)
+        for i, b in enumerate(bits)
+    ]
+    in_core = copies.plan(
+        r.in_half, r.grad_in.at[half_rows], core_peer, r.grad_in.at[other_rows]
+    )
+    small_got = {
+        k: copies.plan(r.small_out.at[slot[k]], r.small_in.at[step_of[k]], peers.at(k))
         for k in others
+    }
+    small_peers = [core_peer] + [chip_peer[b] for b in bits]
+    small_swaps = [
+        copies.plan(r.small_swap.at[2 * i], r.small_swap.at[2 * i + 1], peer)
+        for i, peer in enumerate(small_peers)
     ]
 
-    def ready(k):
-        loads[k].wait()
-        if tokens:
-            given[k]()
-
-    def add(k, start, size, arrived=None):
-        i = number[k]
+    own_attn.start()
+    attn_core.start()
+
+    def fetch(k, place, core_place):
+        loads = [
+            local(r.outs_all.at[slot[k], half_rows], r.stage.at[place], 1),
+            local(r.y_given.at[step_of[k]], r.stage_core.at[core_place], 2),
+        ]
+        for copy in loads:
+            copy.start()
+        for copy in loads:
+            copy.wait()
+
+    def y_merge(place, core_place, start, size, before):
+        if before is not None:
+            received = r.y_early if before[1] < 2 else r.from_ring
+            copy = local(received.at[before], r.stage_ring.at[core_place], 3)
+            copy.start()
+            copy.wait()
 
         def step(rows):
-            at = pl.ds(pl.multiple_of(start + rows.start, rows.size), rows.size)
-            value = kept[i, at, :].astype(f32)
-            if tokens:
-                value = value + from_core[i, at, :].astype(f32)
-            if arrived is not None:
-                value = value + from_ring[arrived, at, :].astype(f32)
-            kept[i, at, :] = value.astype(bf16)
+            at = pl.ds(start + rows.start, rows.size)
+            value = r.stage[place, at, :].astype(f32) + r.stage_core[core_place, at, :].astype(f32)
+            if before is not None:
+                value = value + r.stage_ring[core_place, rows, :].astype(f32)
+            r.stage[place, at, :] = value.astype(bf16)
 
         tiles(size, 32, step)
 
-    def send(k, start, size, ahead, arriving):
-        rows = pl.ds(start, size)
-        return copies.start(
-            kept.at[number[k], rows],
-            from_ring.at[arriving, rows],
-            peers.at(1) if ahead else peers.at(-1),
-        )
-
-    ready(far)
-    add(far, 0, half)
-    up = send(far, 0, half, True, 0)
-    add(far, half, half)
-    down = send(far, half, half, False, 0)
-    up_at = down_at = 0
-    for k in range(far - 1, 0, -1):
-        ready(k)
-        ready(-k)
-        if k == far - 1:
-            add(k, half, half)
-            add(-k, 0, half)
-            up()
-            add(k, 0, half, up_at)
-        else:
-            up()
-            add(k, 0, rows_all, up_at)
-        up = send(k, 0, rows_all, True, 2 * (far - k) - 1)
-        down()
-        if k == far - 1:
-            add(-k, half, half, down_at)
-        else:
-            add(-k, 0, rows_all, down_at)
-        down = send(-k, 0, rows_all, False, 2 * (far - k))
-        up_at, down_at = 2 * (far - k) - 1, 2 * (far - k)
-    ready(0)
-
-    for wait in small_got:
-        wait()
-    small_sum = small[me]
+    def y_step(j):
+        y_ring.step(j, lambda k, way: fetch(k, y_ring.places(k, way), way), y_merge)
+
+    def w_merge(place, core_place, start, size, before):
+        if before is None:
+            return
+
+        def step(rows):
+            at = pl.ds(start + rows.start, rows.size)
+            value = r.w_parts[place, at, :].astype(f32)
+            value = value + r.w_received[before[0], before[1], rows, :].astype(f32)
+            r.w_parts[place, at, :] = value.astype(bf16)
+
+        tiles(size, 32, step)
+
+    def w_step(j):
+        w_ring.step(j, lambda k, way: None, w_merge)
+
+    y_step(3)
+    y_step(4)
+
+    def scales(rows):
+        scale = rms_scale(r.hidden[rows, :].astype(f32))
+        r.scale[rows, :] = jnp.broadcast_to(scale, (scale.shape[0], 128))
+
+    tiles(seq, 64, scales)
+    own_attn.wait()
+    attn_core.wait()
+    query_at = lax.broadcasted_iota(jnp.int32, (seq, seq), 0)
+    key_at = lax.broadcasted_iota(jnp.int32, (seq, seq), 1)
+    allowed = (key_at <= query_at) & (key_at < r.length[0:1, 0:1])
+    r.mask[...] = jnp.where(allowed, 0.0, -1e30)
+
+    def one_head(h, carry):
+        query, key, value = r.query[h], r.key[h], r.value[h]
+        at = pl.ds(pl.multiple_of(h * head, head), head)
+        d_context = nt(r.d_attn[...], r.w_output[at, :]).astype(bf16)
+        scores = nt(query, key) * z.score_scale + r.mask[...]
+        scores = jnp.exp(scores - jnp.max(scores, axis=1, keepdims=True))
+        probs = scores / jnp.sum(scores, axis=1, keepdims=True)
+        d_probs = nt(d_context, value)
+        row_dot = jnp.sum(probs * d_probs, axis=1, keepdims=True)
+        d_scores = (probs * (d_probs - row_dot)).astype(bf16)
+        d_query = matmul(d_scores, key) * z.score_scale
+        d_key = contract_rows(d_scores, query) * z.score_scale
+        d_value = contract_rows(probs.astype(bf16), d_context)
+
+        def unrope(values):
+            return values * r.cosine[...] - pltpu.roll(values, head // 2, 1) * r.sine[...]
+
+        for n, values in enumerate((unrope(d_query), unrope(d_key), d_value)):
+            cols = pl.ds(pl.multiple_of(n * head_all + h * head, head), head)
+            r.d_qkv[:, cols] = values.astype(bf16)
+        return carry
+
+    lax.fori_loop(0, heads, one_head, 0)
+
+    def parts(i, carry):
+        k = lax.div(i + 1, 2) * (1 - 2 * lax.rem(i + 1, 2))
+        cols = pl.ds(pl.multiple_of(peers.group_at(k) * features, features), features)
+        part = contract_rows(r.normed[:, cols], r.d_qkv[...])
+        r.w_parts[i, :, pl.ds(0, 3 * head_all)] = part.astype(bf16)
+        part = contract_rows(r.d_attn[:, cols], r.context[...])
+        r.w_parts[i, :, pl.ds(3 * head_all, head_all)] = part.astype(bf16)
+        return carry
+
+    lax.fori_loop(0, groups, parts, 0)
+    w_step(1)
+    w_step(2)
+
+    r.small_out[...] = r.small_start[...]
+    bias = jnp.sum(r.d_qkv[...].astype(f32), axis=0, keepdims=True)
+    bias_rows = 3 * head_all // features
+    gain_row = z.experts + 2
+
+    def back(g, carry):
+        cols = pl.ds(pl.multiple_of(g * features, features), features)
+        total = nt(r.d_qkv[:, pl.ds(0, head_all)], r.w_query[cols, :])
+        total = total + nt(r.d_qkv[:, pl.ds(head_all, head_all)], r.w_key[cols, :])
+        total = total + nt(r.d_qkv[:, pl.ds(2 * head_all, head_all)], r.w_value[cols, :])
+        r.d_norm[:, cols] = total.astype(bf16)
+        scaled = total * (r.hidden[:, cols].astype(f32) * r.scale[:, 0:1])
+        r.small_out[g, pl.ds(gain_row, 1), :] = jnp.sum(scaled, axis=0, keepdims=True)
+        for i in range(bias_rows):
+            row = gain_row + 1 + peers.lane * bias_rows + i
+            r.small_out[g, pl.ds(row, 1), :] = bias[:, i * features : (i + 1) * features]
+        return carry
+
+    lax.fori_loop(0, groups, back, 0)
+    norm_core.start()
     for k in others:
-        small_sum = small_sum + small_in[number[k]]
-    small_total[...] = small_sum
-    for i, peer in enumerate([peers.other_core()] + [peers.other_chip(b) for b in bits]):
-        small_swap[2 * i] = small_total[...]
-        copies.start(small_swap.at[2 * i], small_swap.at[2 * i + 1], peer)()
-        small_total[...] = small_swap[2 * i] + small_swap[2 * i + 1]
-
-    up()
-    down()
-    home = number[0]
-
-    def last(rows):
-        value = kept[home, rows, :].astype(f32)
-        if tokens:
-            value = value + from_core[home, rows, :].astype(f32)
-        value = value + from_ring[up_at, rows, :].astype(f32)
-        value = value + from_ring[down_at, rows, :].astype(f32)
-        if tokens:
-            kept[home, rows, :] = value.astype(bf16)
-        else:
-            total[rows, :] = value
-
-    tiles(rows_all, 32, last)
-    if tokens:
-        for i, bit in enumerate(bits):
-            wait = copies.start(kept.at[home], from_chip.at[i], peers.other_chip(bit))
-            wait()
-            copies.planned[-1][0].sent()
-            copies.planned[-1] = (copies.planned[-1][0], False)
+        small_got[k].start()
+
+    norm_core.wait()
+
+    def add_core(rows):
+        mine = pl.ds(pl.multiple_of(own + rows.start, rows.size), rows.size)
+        both = r.d_norm[mine, :].astype(f32) + r.norm_core[rows, :].astype(f32)
+        r.norm_total[rows, :] = both.astype(bf16)
+
+    tiles(half, 32, add_core)
+    norm_chip[0].start()
+    load_resid = local(r.d_resid, r.wide, 5)
+    load_resid.start()
+
+    def norm_finish():
+        for i, copy in enumerate(norm_chip):
+            copy.wait()
+            copy.sent()
+            if i + 1 == len(bits):
+                load_resid.wait()
 
             def join(rows, i=i):
-                value = kept[home, rows, :].astype(f32) + from_chip[i, rows, :].astype(f32)
+                total = r.norm_total[rows, :].astype(f32) + r.norm_chip[i, rows, :].astype(f32)
                 if i + 1 < len(bits):
-                    kept[home, rows, :] = value.astype(bf16)
-                else:
-                    total[rows, :] = value
-
-            tiles(rows_all, 32, join)
+                    r.norm_total[rows, :] = total.astype(bf16)
+                    return
+                mine = pl.ds(pl.multiple_of(own + rows.start, rows.size), rows.size)
+                hidden = r.hidden[mine, :].astype(f32)
+                scale = r.scale[mine, 0:1]
+                inner = total * r.gain[...]
+                mean = jnp.mean(inner * hidden, axis=-1, keepdims=True)
+                total = r.wide[rows, :] + scale * inner - hidden * (scale * scale * scale) * mean
+                r.in_half[rows, :] = total.astype(bf16)
+
+            tiles(half, 32, join)
+            if i + 1 < len(bits):
+                norm_chip[i + 1].start()
+        in_core.start()
+        own_in.start()
+
+    own_in = local(r.in_half, r.grad_in.at[half_rows], 6)
+    own_layer = local(r.layer_half, r.layer_out.at[half_rows], 7)
+    for j in range(3, 2 * far):
+        w_step(j)
+        if j + 2 < 2 * far:
+            y_step(j + 2)
+        if j == 3:
+            norm_finish()
+
+    y_ring.finish(range(2 * far - 4, 2 * far - 2))
+    fetch(0, 0, 0)
+
+    def first_of_home(rows):
+        both = r.stage[0, rows, :].astype(f32) + r.stage_core[0, rows, :].astype(f32)
+        r.wide[rows, :] = both
+
+    tiles(half, 32, first_of_home)
+
+    def last(way, index, start):
+        copy = local(r.from_ring.at[way, index], r.stage_ring.at[0], 3)
+        copy.start()
+        copy.wait()
+
+        def step(rows):
+            at = pl.ds(start + rows.start, rows.size)
+            value = r.wide[at, :] + r.stage_ring[0, rows, :].astype(f32)
+            r.wide[at, :] = value
+            r.total[at, :] = value.astype(bf16)
+
+        tiles(half // 2, 32, step)
+
+    for chunk in y_ring.arrived():
+        last(*chunk)
+    y_chip[0].start()
+    load_out = local(r.resid, r.wide, 8)
+    load_out.start()
+
+    for k in others:
+        small_got[k].wait()
+    small_sum = r.small_out[me]
+    for k in others:
+        small_sum = small_sum + r.small_in[step_of[k]]
+    r.small_total[...] = small_sum
+    for i, copy in enumerate(small_swaps):
+        r.small_swap[2 * i] = r.small_total[...]
+        copy.start()
+        copy.wait()
+        r.small_total[...] = r.small_swap[2 * i] + r.small_swap[2 * i + 1]
+
+    arrived = w_ring.arrived()
+    size = features // 2
+    for start in (0, size):
+        found = [(way, index) for way, index, at in arrived if at == start]
+
+        def w_last(rows, start=start, found=found):
+            at = pl.ds(start + rows.start, rows.size)
+            value = r.w_parts[0, at, :].astype(f32)
+            for way, index in found:
+                value = value + r.w_received[way, index, rows, :].astype(f32)
+            r.w_total[at, :] = value
+
+        tiles(size, 32, w_last)
+    load_out.wait()
+    for i, copy in enumerate(y_chip):
+        copy.wait()
+        copy.sent()
+
+        def join(rows, i=i):
+            value = r.total[rows, :].astype(f32) + r.from_chip[i, rows, :].astype(f32)
+            if i + 1 < len(bits):
+                r.total[rows, :] = value.astype(bf16)
+            else:
+                r.layer_half[rows, :] = (r.wide[rows, :] + value).astype(bf16)
+
+        tiles(half, 32, join)
+        if i + 1 < len(bits):
+            y_chip[i + 1].start()
+    layer_core.start()
+    own_layer.start()
+    layer_core.wait()
+    in_core.wait()
+    own_in.wait()
+    own_layer.wait()
+    y_ring.finish(range(2 * far - 2, 2 * far))
+    w_ring.finish(range(2 * far - 4, 2 * far))
     copies.finish()
 
 
-def reduce_parts(groups, lanes, parts, small, tokens, collective_id):
-    rows = parts.shape[1] // 2 if tokens else parts.shape[1]
-    width = parts.shape[2]
+def finish(groups, lanes, sizes, vmem_ins, hbm_ins):
+    z = Sizes(groups=groups, lanes=lanes, **sizes)
+    seq, width = z.seq, z.width
+    half = seq // 2
     bits = (lanes // 2).bit_length() - 1
     far = groups // 2
-    copies = (groups if tokens else 0) + (groups - 1) + 2 * far + (1 + bits) + bits
-    shape = (rows, width)
-    return pl.pallas_call(
-        functools.partial(reduce_kernel, groups, lanes, tokens),
-        out_shape=(
-            jax.ShapeDtypeStruct(shape, f32),
-            jax.ShapeDtypeStruct(small.shape[1:], f32),
+    head_all = z.heads * z.head
+    outs = dict(
+        layer_out=((seq, width), bf16, in_place),
+        grad_in=((seq, width), bf16, in_place),
+        w_total=((z.features, 4 * head_all), f32, whole),
+        small_total=(vmem_ins["small_start"].shape[1:], f32, whole),
+        from_ring=((2, 2 * far - 1, half // 2, width), bf16, in_place),
+    )
+    small_shape = vmem_ins["small_start"].shape
+    copies = groups + 1 + 8 * far + 2 * bits + 3 + (groups - 1) + 1 + bits
+    scratch = dict(
+        d_attn=pltpu.VMEM((seq, width), bf16),
+        d_qkv=pltpu.VMEM((seq, 3 * head_all), bf16),
+        d_norm=pltpu.VMEM((seq, width), bf16),
+        scale=pltpu.VMEM((seq, 128), f32),
+        mask=pltpu.VMEM((seq, seq), f32),
+        stage=pltpu.VMEM((4, half, width), bf16),
+        stage_core=pltpu.VMEM((2, half, width), bf16),
+        stage_ring=pltpu.VMEM((2, half // 2, width), bf16),
+        total=pltpu.VMEM((half, width), bf16),
+        from_chip=pltpu.VMEM((max(bits, 1), half, width), bf16),
+        layer_half=pltpu.VMEM((half, width), bf16),
+        norm_core=pltpu.VMEM((half, width), bf16),
+        norm_total=pltpu.VMEM((half, width), bf16),
+        norm_chip=pltpu.VMEM((max(bits, 1), half, width), bf16),
+        in_half=pltpu.VMEM((half, width), bf16),
+        wide=pltpu.VMEM((half, width), f32),
+        w_parts=pltpu.VMEM((groups, z.features, 4 * head_all), bf16),
+        w_received=pltpu.VMEM((2, 2 * far - 1, z.features // 2, 4 * head_all), bf16),
+        small_out=pltpu.VMEM(small_shape, f32),
+        small_in=pltpu.VMEM(small_shape, f32),
+        small_swap=pltpu.VMEM((2 * (1 + bits),) + small_shape[1:], f32),
+        send_sems=pltpu.SemaphoreType.DMA((copies,)),
+        recv_sems=pltpu.SemaphoreType.DMA((copies,)),
+        local_sems=pltpu.SemaphoreType.DMA((9,)),
+    )
+    names = list(vmem_ins) + list(hbm_ins) + list(outs) + list(scratch)
+    results = pl.pallas_call(
+        functools.partial(finish_kernel, z, names),
+        out_shape=tuple(jax.ShapeDtypeStruct(s, d) for s, d, _ in outs.values()),
+        in_specs=[whole] * len(vmem_ins) + [in_place] * len(hbm_ins),
+        out_specs=tuple(spec for _, _, spec in outs.values()),
+        scratch_shapes=list(scratch.values()),
+        compiler_params=pltpu.CompilerParams(
+            collective_id=1, has_side_effects=True, vmem_limit_bytes=63 * 1024 * 1024
         ),
-        in_specs=[in_place, whole],
-        out_specs=(whole, whole),
-        scratch_shapes=[
-            pltpu.VMEM((groups,) + shape, bf16),
-            pltpu.VMEM(((groups if tokens else 1),) + shape, bf16),
-            pltpu.VMEM((2 * far - 1,) + shape, bf16),
-            pltpu.VMEM(((max(bits, 1) if tokens else 1),) + shape, bf16),
-            pltpu.VMEM(small.shape, f32),
-            pltpu.VMEM((2 * (1 + bits),) + small.shape[1:], f32),
-            pltpu.SemaphoreType.DMA((copies,)),
-            pltpu.SemaphoreType.DMA((copies,)),
-            pltpu.SemaphoreType.DMA((groups,)),
-        ],
-        compiler_params=pltpu.CompilerParams(
-            collective_id=collective_id,
-            has_side_effects=True,
-            vmem_limit_bytes=58 * 1024 * 1024,
-        ),
-        name="reduce_tokens" if tokens else "reduce_weights",
-    )(parts, small)
+        name="finish",
+    )(*vmem_ins.values(), *hbm_ins.values())
+    return Sizes(**dict(zip(outs, results)))
 
 
 def attend_forward(query, key, value, allowed, score_scale):
@@ -1190,18 +1470,6 @@
     probs = jnp.exp(scores - log_total)
     contexts = jnp.einsum("hqk,khd->qhd", probs.astype(bf16), value, preferred_element_type=f32)
     return contexts.astype(bf16), log_total
-
-
-def attend_backward(query, key, value, d_context, log_total, allowed, score_scale):
-    scores = jnp.einsum("qhd,khd->hqk", query, key, preferred_element_type=f32) * score_scale
-    probs = jnp.exp(jnp.where(allowed[None], scores, -1e30) - log_total)
-    d_probs = jnp.einsum("qhd,khd->hqk", d_context, value, preferred_element_type=f32)
-    row_dot = jnp.sum(probs * d_probs, axis=-1, keepdims=True)
-    d_scores = (probs * (d_probs - row_dot)).astype(bf16)
-    d_query = jnp.einsum("hqk,khd->qhd", d_scores, key, preferred_element_type=f32) * score_scale
-    d_key = jnp.einsum("hqk,qhd->khd", d_scores, query, preferred_element_type=f32) * score_scale
-    d_value = jnp.einsum("hqk,qhd->khd", probs.astype(bf16), d_context, preferred_element_type=f32)
-    return d_query, d_key, d_value
 
 
 def norm_backward(values, scale, gain, d_normed):
@@ -1253,23 +1521,6 @@
     def half_of(array):
         return lax.dynamic_slice_in_dim(array, half_start, half, 0)
 
-    def swap(values, bit):
-        return lax.ppermute(values, "tensor", [(i, i ^ bit) for i in range(lane_count)])
-
-    def sum_lanes(values):
-        other = lax.dynamic_slice_in_dim(values, half - half_start, half, 0)
-        total = (half_of(values).astype(f32) + swap(other, 1).astype(f32)).astype(bf16)
-        for bit in range(1, (lane_count // 2).bit_length()):
-            total32 = total.astype(f32) + swap(total, 1 << bit).astype(f32)
-            total = total32.astype(bf16)
-        return total32
-
-    def both_halves(mine):
-        other = swap(mine, 1)
-        lower = jnp.where(half_start == 0, mine, other)
-        upper = jnp.where(half_start == 0, other, mine)
-        return jnp.concatenate([lower, upper], axis=0)
-
     hidden = hidden_in.astype(f32)
     position = jnp.arange(seq, dtype=jnp.int32)
     grad_low = jnp.where((position < length)[:, None], out_grad, jnp.zeros_like(out_grad))
@@ -1318,7 +1569,9 @@
     resid, normed, outs, d_in_sum, small = (
         ex.resid, ex.normed, ex.outs_all, ex.d_total, ex.small_total
     )
-    g_gate, g_up, g_down = jnp.swapaxes(ex.g_gate, 1, 2), jnp.swapaxes(ex.g_up, 1, 2), ex.g_down
+    g_gate = jnp.swapaxes(ex.g_gate, 1, 2).astype(f32)
+    g_up = jnp.swapaxes(ex.g_up, 1, 2).astype(f32)
+    g_down = ex.g_down.astype(f32)
 
     ffn_scale = rms_scale(resid)
     logits = matmul(normed, w_router)
@@ -1338,26 +1591,6 @@
     )
     d_normed = d_in_sum + d_from_gates
     d_resid = half_of(grad_low).astype(f32) + norm_backward(resid, ffn_scale, gain_ffn, d_normed)
-    d_attn = both_halves(d_resid.astype(bf16))
-
-    d_context = times_transposed(d_attn, w_output).astype(bf16).reshape(by_head)
-    d_query_rot, d_key_rot, d_value_all = attend_backward(
-        query, key, value, d_context, log_total, allowed, score_scale
-    )
-
-    def unrope(values):
-        return (values * cosine - rotate(values) * sine).astype(bf16).reshape(seq, head_all)
-
-    d_query, d_key = unrope(d_query_rot), unrope(d_key_rot)
-    d_value = d_value_all.astype(bf16).reshape(seq, head_all)
-    d_normed_attn = (
-        times_transposed(d_query, w_query)
-        + times_transposed(d_key, w_key)
-        + times_transposed(d_value, w_value)
-    )
-    grads = [contract_rows(normed_attn, d) for d in (d_query, d_key, d_value)]
-    grads.append(contract_rows(d_attn, context_flat))
-    grads = jnp.concatenate([g.astype(bf16) for g in grads], axis=1)
 
     rows = half // (lane_count // 2)
     start = (lane // 2) * rows
@@ -1366,52 +1599,51 @@
         for a in (d_normed * resid * ffn_scale, normed, d_logits, d_sig_logit[:, None])
     ]
     router_part = contract_rows(jnp.concatenate([mine[2], mine[3]], axis=1), mine[1])
-    bias_part = jnp.concatenate(
-        [jnp.sum(d.astype(f32), axis=0) for d in (d_query, d_key, d_value)]
-    ).reshape(-1, features)
-    to_groups = jnp.concatenate(
-        [
-            router_part,
-            jnp.sum(mine[0], axis=0)[None],
-            jnp.sum(d_normed_attn * hidden * attn_scale, axis=0)[None],
-        ],
-        axis=0,
-    )
+    to_groups = jnp.concatenate([router_part, jnp.sum(mine[0], axis=0)[None]], axis=0)
     to_groups = jnp.swapaxes(to_groups.reshape(-1, groups, features), 0, 1)
-    lane_slots = (jnp.arange(lane_count) == lane).astype(f32)[:, None, None] * bias_part[None]
-    lane_slots = lane_slots.reshape(-1, features)
-    small = jnp.concatenate(
-        [to_groups, jnp.broadcast_to(lane_slots[None], (groups,) + lane_slots.shape)], axis=1
-    )
-    small = jnp.pad(small, ((0, 0), (0, -small.shape[1] % 8), (0, 0)))
-    grads, small = reduce_parts(
-        groups, lane_count, grads.reshape(groups, features, -1), small, False, 2
+    bias_rows = 3 * head_all // features
+    small_rows = round_up(experts_all + 3 + lane_count * bias_rows, 8)
+    small_start = jnp.pad(to_groups, ((0, 0), (0, small_rows - to_groups.shape[1]), (0, 0)))
+
+    signed_sine = jnp.concatenate([-sine[..., : head_width // 2], sine[..., head_width // 2 :]], -1)
+    done = finish(
+        groups,
+        lane_count,
+        dict(
+            seq=seq, width=width, heads=heads, head=head_width, features=features,
+            experts=experts_all, score_scale=score_scale,
+        ),
+        dict(
+            query=jnp.swapaxes(query, 0, 1),
+            key=jnp.swapaxes(key, 0, 1),
+            value=jnp.swapaxes(value, 0, 1),
+            context=context_flat,
+            normed=normed_attn,
+            hidden=hidden_in,
+            gain=gain_attn[None, :],
+            w_output=w_output,
+            w_query=w_query,
+            w_key=w_key,
+            w_value=w_value,
+            cosine=cosine[:, 0],
+            sine=signed_sine[:, 0],
+            length=jnp.broadcast_to(length, (8, 128)),
+            small_start=small_start,
+        ),
+        dict(
+            outs_all=outs, y_given=ex.y_given, y_early=ex.y_early,
+            d_attn_half=d_resid.astype(bf16), d_resid=d_resid, resid=resid,
+        ),
+    )
+    grads, small, layer_out, grad_in = (
+        done.w_total, done.small_total, done.layer_out, done.grad_in
     )
     biases = lax.dynamic_slice_in_dim(
-        small, experts_all + 3 + lane * bias_part.shape[0], bias_part.shape[0], 0
+        small, experts_all + 3 + lane * bias_rows, bias_rows, 0
     ).reshape(3, heads, head_width)
     biases = lax.dynamic_slice_in_dim(
         biases, group * (head_width // groups), head_width // groups, 2
     )
-
-    outs = lax.psum_scatter(
-        outs.reshape(groups * seq, width), ("expert", "tensor"), scatter_dimension=0, tiled=True
-    )
-    outs, grads = lax.optimization_barrier((outs, grads))
-    chip = lane // 2
-    piece = seq // lane_count
-    layer = lax.dynamic_slice_in_dim(resid, chip * piece, piece, 0) + outs.astype(f32)
-    layer = layer.astype(bf16)
-    for bit in range((lane_count // 2).bit_length() - 1):
-        other = swap(layer, 2 << bit)
-        low = (chip >> bit) % 2 == 0
-        layer = jnp.concatenate(
-            [jnp.where(low, layer, other), jnp.where(low, other, layer)], axis=0
-        )
-    layer_out = both_halves(layer)
-    d_normed_in = sum_lanes(d_normed_attn.astype(bf16))
-    grad_in = d_resid + norm_backward(half_of(hidden), half_of(attn_scale), gain_attn, d_normed_in)
-    grad_in = both_halves(grad_in.astype(bf16))
 
     shared = lax.all_to_all(ex.s_grads, "expert", split_axis=0, concat_axis=0, tiled=True)
     shared = shared.reshape(groups, 3, ex.units, features)[:, :, :units].astype(f32)

time: 733 us -> 603 us (0.82)
  the two profiles are of different devices: /device:TPU:25 before, /device:TPU:21 now
where the time goes in v3:
time: 603 us; the launch traced here: 597 us
  Pallas kernels  505 us (84%)
  local copies, waits for them, and re-layouts  35.5 us (6%)
  other arithmetic  31 us (5%)
  matrix products  17.6 us (3%)
  starting transfers between devices  6.2 us (1%)
    pallas_call x1, Pallas kernels, run_experts(): pl.pallas_call(functools.partial(experts_kernel, z, names), out_shape=tup...  318 us
    pallas_call x1, Pallas kernels, finish(): pl.pallas_call(functools.partial(finish_kernel, z, names), out_shape=tupl...  187 us
    unnamed x72, local copies, waits for them, and re-layouts  12.7 us
  transfers between devices with their start and end apart: 1, of which 0 were waited for; matrix products, arithmetic and copies ran while one was open for 6% of the time, Pallas kernels for 31%

profile of v3, /device:TPU:21, one launch (start us, length us, event | category | flops | bytes accessed | tf_op | source)
XLA Modules:
  0.0 597.2 jit_solution(16255190152063038114)
XLA Ops:
  0.7 0.8 convert_element_type.123
  1.5 2.1 fusion
  3.7 0.5 fusion.2.refs_4_
  4.2 1.0 copy-done.17
  5.3 2.3 convolution_add_fusion.3
  7.6 1.6 copy.63
  9.2 3.9 convolution_add_fusion.2
  13.0 1.5 copy.66
  14.6 0.1 fusion.26
  14.7 1.4 fusion.25
  16.8 0.1 fusion.21
  16.9 0.7 slice_negate_fusion
  17.7 0.7 fusion.20
  18.4 0.9 fusion.5
  19.3 0.9 exponential_reduce_fusion
  20.2 1.2 copy-done.2
  21.5 1.0 copy-done.14
  22.5 1.5 broadcast_select_fusion.refs_3_
  24.0 0.6 convert_element_type.139
  24.6 0.3 copy.72
  25.0 1.3 constant_dynamic-slice_fusion.5
  26.3 1.1 pad.26.refs_9_
  27.3 0.9 pad.27.refs_10_
  28.3 1.3 fusion.13
  29.6 0.9 copy-done.3
  30.4 1.4 fusion.14
  31.8 0.2 copy-done.19
  32.0 2.6 convolution_convert_fusion.refs_0_
  34.6 2.9 constant_dynamic-slice_fusion.6
  37.6 1.7 fusion.7.refs_8_
  39.3 0.6 pad.23.refs_4_
  39.9 317.7 %run_experts.1 = (bf16[256,2048]{1,0:T(8,128)(2,1)}, f32[24,512]{1,0:T(8,128)}, f32[256,2048]{1,0:T(8,128)}, f32[256,2048]{1,0:T(8,128)}, bf16[8,512,2048]{2,1,0...) custom-call(bf16[512,2048]{1,0:T(8,128)(2,1)} %convolution_convert_f, ...), custom_call_target="tpu_custom_call" | custom-call | tf_op jit(solution)/shard_map/run_experts/pallas_call | solution.py:1085
  357.5 6.2 %all-to-all-start = ((bf16[8,528,256]{2,1,0:T(8,128)(2,1)}), bf16[8,528,256]{2,1,0:T(8,128)(2,1)}, u32[]{:S(2)}, u32[]{:S(2)}) async-start(bf16[8,528,256]{2,1,0:T(8,128)(2,1)} %get-tuple-element.45), calls=%async_computation | async-start | bytes 4325376 | tf_op jit(solution)/shard_map/all_to_all | solution.py:1648
  363.8 0.4 fusion.43
  364.2 0.4 fusion.44
  364.5 0.8 dynamic-slice_bitcast_fusion
  365.4 3.6 multiply_reduce_fusion
  369.2 1.4 fusion.16
  370.6 0.9 fusion.22
  371.5 2.1 copy.79.refs_3_
  373.5 2.0 copy.69
  375.8 0.8 pad.28.refs_14_
  376.6 0.9 maximum_sine_fusion
  377.5 0.1 slice_negate_fusion.2
  377.6 0.8 maximum_bitcast_fusion.refs_12_
  378.5 2.3 fusion.39
  380.8 0.6 broadcast_in_dim.33.refs_13_
  381.4 187.2 %finish.1 = (bf16[512,2048]{1,0:T(8,128)(2,1)}, bf16[512,2048]{1,0:T(8,128)(2,1)}, f32[256,2048]{1,0:T(8,128)}, f32[48,256]{1,0:T(8,128)}, bf16[2,7,128,2048]{3,2,1,0:T(8,128)(2,1)}) custom-call(bf16[4,512,128]{2,1,0:T(8,128)(2,1)} %bitcast.90, bf16[4,512,128]{2,1,0:T(8,128)(2,1)} %bitcast.89, bf16[4,512,128]{2,1,0:T(8,128)(2,1)} %bitcast.93, ...), custom_call_target="tpu_custom_call" | custom-call | tf_op jit(solution)/shard_map/finish/pallas_call | solution.py:1451
  568.6 2.7 slice_bitcast_fusion
  571.3 1.0 copy.75
  572.4 5.3 convert_element_type.151
  577.6 0.7 fusion.33
  578.3 0.6 fusion.42
  578.9 0.6 slice_bitcast_fusion.1
  579.5 3.3 convert_bitcast_fusion
  582.8 3.3 convert_bitcast_fusion.1
  586.1 2.1 copy_bitcast_fusion
  588.2 1.5 fusion.41
  589.7 1.5 copy.76
  591.2 1.5 copy.77
  592.7 0.5 copy-done.16
  593.2 1.3 copy.85
  594.5 1.0 copy-done.15
  595.6 1.3 copy.86
  (87 shorter events, 0.7 us)
Async XLA Ops:
  0.7 3.0 copy-start
  0.7 3.0 copy-start.30
  1.5 2.7 copy-start.25
  3.7 1.6 copy-start.17
  5.3 3.9 copy-start.6
  7.6 1.6 copy-start.31
  16.1 1.5 copy-start.13
  18.4 0.9 copy-start.9
  18.4 1.0 copy-start.10
  19.3 2.1 copy-start.2
  19.3 2.1 copy-start.32
  19.3 3.1 copy-start.14
  22.4 1.5 copy-start.29
  22.5 2.1 copy-start.26
  22.5 2.1 copy-start.21
  24.9 3.3 copy-start.7
  24.9 3.3 copy-start.18
  28.3 2.2 copy-start.3
  29.6 2.3 copy-start.22
  30.4 1.6 copy-start.19
  31.8 2.8 copy-start.23
  37.6 1.7 copy-start.28
  357.5 6.2 %copy-start.8 = (bf16[256,2048]{1,0:T(8,128)(2,1)S(1)}, bf16[256,2048]{1,0:T(8,128)(2,1)}, u32[]{:S(2)}) copy-start(bf16[256,2048]{1,0:T(8,128)(2,1)} %get-tuple-element.34) | copy-start | bytes 3145732
  357.5 228.5 %all-to-all-start = ((bf16[8,528,256]{2,1,0:T(8,128)(2,1)}), bf16[8,528,256]{2,1,0:T(8,128)(2,1)}, u32[]{:S(2)}, u32[]{:S(2)}) async-start(bf16[8,528,256]{2,1,0:T(8,128)(2,1)} %get-tuple-element.45), calls=%async_computation | async-start | bytes 4325376 | tf_op jit(solution)/shard_map/all_to_all | solution.py:1648
  363.7 1.6 copy-start.1
  363.7 1.7 copy-start.24
  371.5 4.1 copy-start.20
  375.6 2.9 copy-start.4
  375.6 2.9 copy-start.5
  568.6 3.7 copy-start.27
  572.3 7.1 %copy-start.12 = (bf16[2,352,2048]{2,1,0:T(8,128)(2,1)S(1)}, bf16[2,352,2048]{2,1,0:T(8,128)(2,1)}, u32[]{:S(2)}) copy-start(bf16[2,352,2048]{2,1,0:T(8,128)(2,1)} %get-tuple-element.47) | copy-start | bytes 8650756
  579.5 3.3 copy-start.11
  591.2 2.0 copy-start.16
  593.2 2.3 copy-start.15

commit v4 on v3

--- a/solution.py
+++ b/solution.py
@@ -74,6 +74,14 @@
 
     def other_chip(self, bit):
         return (self.group, 2 * flip_bit(self.chip, bit) + self.core)
+
+    def chip_on(self, step):
+        return lax.rem(self.chip + step, self.chips)
+
+    def chip_peers(self):
+        return [
+            (self.group, 2 * self.chip_on(step) + self.core) for step in range(1, self.chips)
+        ]
 
     def offsets(self):
         return [0] + [s * k for k in range(1, self.far) for s in (1, -1)] + [self.far]
@@ -349,7 +357,7 @@
     ahead, behind = peers.at(1), peers.at(-1)
     core_peer = peers.other_core()
     chip_peer = {b: peers.other_chip(b) for b in bits}
-    peers.meet([peers.at(k) for k in others] + [core_peer] + [chip_peer[b] for b in bits])
+    peers.meet([peers.at(k) for k in others] + [core_peer] + peers.chip_peers())
     copies = Copies(r.send_sems, r.recv_sems)
 
     def local(source, target, number):
@@ -384,7 +392,11 @@
         )
     weights += [
         local(r.s_in_hbm, r.s_in, 3),
-        local(r.s_out_hbm, r.s_out, 4),
+        local(
+            r.s_out_hbm.at[pl.ds(pl.multiple_of(peers.group * z.down_step, 16), z.down_rows)],
+            r.s_out.at[pl.ds(0, z.down_rows)],
+            4,
+        ),
         local(r.router_hbm, r.router, 5),
     ]
     own_part = local(r.part.at[half_rows], r.total, 6)
@@ -434,9 +446,16 @@
     }
     g_ring[-far] = hop(r.grads_all, -far, first, piece // 2)
     g_ring[far] = hop(r.grads_all, far, first + piece // 2, piece // 2)
-    x_ring = {
-        k: hop(r.tokens_all, k, own, half, r.normed if abs(k) == 1 else None) for k in signed
-    }
+    steps = range(1, peers.chips)
+    own_piece_rows = pl.ds(pl.multiple_of(peers.chip * piece, 32), piece)
+    pieces = [own_piece_rows] + [
+        pl.ds(pl.multiple_of(peers.chip_on(peers.chips - n) * piece, 32), piece) for n in steps
+    ]
+    x_first = [
+        {s: hop(r.tokens_all, s, own + at.start, piece, r.normed.at[at]) for s in (-1, 1)}
+        for at in pieces
+    ]
+    x_ring = {k: hop(r.tokens_all, k, own, half) for k in signed if abs(k) > 1}
     x_ring[-far] = hop(r.tokens_all, -far, own, half // 2)
     x_ring[far] = hop(r.tokens_all, far, own + half // 2, half // 2)
     g_chip = {k: [chip_swap(r.grads_all, k, b) for b in bits] for k in others}
@@ -445,9 +464,24 @@
         k: core_swap(r.tokens_all, k, r.normed if k == 0 else None) for k in peers.offsets()
     }
     part_core = copies.plan(r.part.at[other_rows], r.from_core, core_peer)
-    part_chip = [
-        copies.plan(r.total, r.part_chip.at[i], chip_peer[b], ends=False)
-        for i, b in enumerate(bits)
+    part_out = [
+        copies.plan(
+            r.total.at[pl.ds(pl.multiple_of(peers.chip_on(n) * piece, 32), piece)],
+            r.part_in.at[n - 1],
+            peers.chip_peers()[n - 1],
+            ends=False,
+        )
+        for n in steps
+    ]
+    part_back = [
+        copies.plan(
+            r.total.at[own_piece_rows],
+            r.part_all.at[own_piece_rows],
+            peers.chip_peers()[n - 1],
+            r.part_all.at[pieces[n]],
+            ends=False,
+        )
+        for n in steps
     ]
 
     d_ring = RingSum(
@@ -483,6 +517,9 @@
     other = lax.broadcasted_iota(jnp.int32, (seq, seq), 1)
     ranks = jnp.where(other < token, 1.0, jnp.where(other == token, 1024.0, 0.0))
     r.ranker[...] = ranks.astype(bf16)
+    if z.down_rows < z.units:
+        at = pl.ds(z.down_rows, z.units - z.down_rows)
+        r.s_out[at, :] = jnp.zeros((z.units - z.down_rows, z.width), bf16)
 
     own_part.wait()
     part_core.wait()
@@ -492,35 +529,48 @@
         r.total[rows, :] = both.astype(bf16)
 
     tiles(half, 32, add_core)
-    part_chip[0].start()
+    for copy in part_out:
+        copy.start()
     own_hidden.wait()
+
+    def norm_piece(source, start):
+        def step(rows):
+            at = pl.ds(pl.multiple_of(start + rows.start, rows.size), rows.size)
+            both = r.stage[0, at, :].astype(f32) + source[at, :].astype(f32)
+            r.wide[at, :] = both
+            r.normed[at, :] = (both * rms_scale(both) * r.gain[...]).astype(bf16)
+
+        tiles(piece, 32, step)
+
+    def add_chips(rows):
+        at = pl.ds(pl.multiple_of(own_piece_rows.start + rows.start, rows.size), rows.size)
+        total = r.total[at, :].astype(f32)
+        for n in steps:
+            total = total + r.part_in[n - 1, rows, :].astype(f32)
+        r.total[at, :] = total.astype(bf16)
+
     for k in range(2, far):
         for s in (-1, 1):
             g_ring[s * (k - 1)].wait()
             g_ring[s * k].start()
         if k != 2:
             continue
-        for i, bit in enumerate(bits):
-            part_chip[i].wait()
-            part_chip[i].sent()
-
-            def add_chip(rows, i=i):
-                both = r.total[rows, :].astype(f32) + r.part_chip[i, rows, :].astype(f32)
-                if i + 1 < len(bits):
-                    r.total[rows, :] = both.astype(bf16)
-                    return
-                both = r.stage[0, rows, :].astype(f32) + both
-                r.wide[rows, :] = both
-                r.normed[rows, :] = (both * rms_scale(both) * r.gain[...]).astype(bf16)
-
-            tiles(half, 32, add_chip)
-            if i + 1 < len(bits):
-                part_chip[i + 1].start()
-        x_ring[-1].start()
-        x_ring[1].start()
-        x_core[0].start()
-        own_tokens.start()
-        keep_resid.start()
+        for copy in part_out:
+            copy.wait()
+        tiles(piece, 32, add_chips)
+        for copy in part_back:
+            copy.start()
+        norm_piece(r.total, own_piece_rows.start)
+        for s in (-1, 1):
+            x_first[0][s].start()
+    for n in steps:
+        part_back[n - 1].wait()
+        norm_piece(r.part_all, pieces[n].start)
+        for s in (-1, 1):
+            x_first[n][s].start()
+    x_core[0].start()
+    own_tokens.start()
+    keep_resid.start()
     for k in signed[:-2]:
         g_chip[k][0].start()
     for copy in ids_got + weights + traded:
@@ -528,6 +578,8 @@
     own_grad.wait()
     own_tokens.wait()
     keep_resid.wait()
+    for copy in part_out + part_back:
+        copy.sent()
 
     def finish_grads(ks):
         for k in ks:
@@ -544,7 +596,8 @@
             def _(k=q + 1):
                 if k < far:
                     for s in (-1, 1):
-                        x_ring[s * k].wait()
+                        for copy in [one[s] for one in x_first] if k == 1 else [x_ring[s * k]]:
+                            copy.wait()
                         if k + 1 < far:
                             x_ring[s * (k + 1)].start()
                     if k + 1 == far:
@@ -727,16 +780,11 @@
         fetch(k, d_ring.places(k, way), way)
 
     def merge(place, core_place, start, size, before):
-        if before is not None:
-            copy = local(r.from_ring.at[before], r.stage_ring.at[core_place], 2)
-            copy.start()
-            copy.wait()
-
         def step(rows):
             at = pl.ds(start + rows.start, rows.size)
             value = r.stage[place, at, :].astype(f32) + r.stage_core[core_place, at, :].astype(f32)
             if before is not None:
-                value = value + r.stage_ring[core_place, rows, :].astype(f32)
+                value = value + r.from_ring[before[0], before[1], rows, :].astype(f32)
             r.stage[place, at, :] = value.astype(bf16)
 
         tiles(size, 32, step)
@@ -930,13 +978,9 @@
             ).wait_recv()
 
     def last(way, index, start):
-        copy = local(r.from_ring.at[way, index], r.stage_ring.at[0], 2)
-        copy.start()
-        copy.wait()
-
         def step(rows):
             at = pl.ds(start + rows.start, rows.size)
-            value = r.wide[at, :] + r.stage_ring[0, rows, :].astype(f32)
+            value = r.wide[at, :] + r.from_ring[way, index, rows, :].astype(f32)
             r.wide[at, :] = value
             r.total[at, :] = value.astype(bf16)
 
@@ -1009,12 +1053,19 @@
     bits = (lanes // 2).bit_length() - 1
     far = groups // 2
     small_rows = round_up(experts + 1, 8)
+    whole_down = units_true % 16 == 0
+    if whole_down:
+        s_out = s_down
+    else:
+        mine = lax.axis_index("expert") * units_true
+        s_out = lax.dynamic_slice_in_dim(s_down, mine, units_true, 0)
+        s_out = jnp.pad(s_out, ((0, units - units_true), (0, 0)))
     z = Sizes(
         groups=groups, lanes=lanes, seq=seq, width=width, ff=ff, units=units,
-        capacity=capacity, experts=experts, units_used=round_up(units_true, 16),
+        capacity=capacity, experts=experts, units_used=round_up(units_true, 16), down_step=units_true if whole_down else 0,
+        down_rows=units_true if whole_down else units,
     )
     s_in = jnp.concatenate([pad_last(s_gate, units), pad_last(s_up, units)], axis=1)
-    s_out = jnp.pad(s_down, ((0, units - units_true), (0, 0)))
     router = pad_last(router, 128)
     ins = dict(
         part=(part, in_place), hidden=(hidden, in_place), gain=(gain, whole),
@@ -1046,20 +1097,20 @@
         given=((groups, half, width), bf16, in_place),
         y_given=((groups, half, width), bf16, in_place),
         y_early=((2, 2, half // 2, width), bf16, in_place),
-        from_ring=((2, 2 * far - 1, half // 2, width), bf16, in_place),
-    )
-    copies = 4 + 3 + 2 * groups + (groups - 1) * (2 + bits) + groups + 1 + bits + 4 * far
+    )
+    copies = 2 * lanes + 4 + 3 + 2 * groups + (groups - 1) * (2 + bits) + groups + 1 + bits + 4 * far
     copies += 2 * bits + 1
     scratch = dict(
         ids_all=pltpu.VMEM((groups,) + ids.shape, jnp.int32),
         total=pltpu.VMEM((half, width), bf16),
         from_core=pltpu.VMEM((half, width), bf16),
-        part_chip=pltpu.VMEM((max(bits, 1), half, width), bf16),
+        part_in=pltpu.VMEM((lanes // 2 - 1, seq // lanes, width), bf16),
+        part_all=pltpu.VMEM((half, width), bf16),
         from_chip=pltpu.VMEM((max(bits, 1), half, width), bf16),
         wide=pltpu.VMEM((half, width), f32),
         stage=pltpu.VMEM((4, half, width), bf16),
         stage_core=pltpu.VMEM((2, half, width), bf16),
-        stage_ring=pltpu.VMEM((2, half // 2, width), bf16),
+        from_ring=pltpu.VMEM((2, 2 * far - 1, half // 2, width), bf16),
         small_out=pltpu.VMEM((groups, 8, seq), f32),
         small_in=pltpu.VMEM((groups, 8, seq), f32),
         small_swap=pltpu.VMEM((2 * (1 + bits), small_rows, seq), f32),
@@ -1067,7 +1118,7 @@
         w_in=pltpu.VMEM((2 * ff, width), bf16),
         w_out=pltpu.VMEM((ff, width), bf16),
         s_in=pltpu.VMEM(s_in.shape, bf16),
-        s_out=pltpu.VMEM(s_out.shape, bf16),
+        s_out=pltpu.VMEM((units, width), bf16),
         router=pltpu.VMEM(router.shape, bf16),
         send_sems=pltpu.SemaphoreType.DMA((copies,)),
         recv_sems=pltpu.SemaphoreType.DMA((copies,)),
@@ -1137,7 +1188,7 @@
         for i, b in enumerate(bits)
     ]
     layer_core = copies.plan(
-        r.layer_half, r.layer_out.at[half_rows], core_peer, r.layer_out.at[other_rows]
+        r.norm_total, r.layer_out.at[half_rows], core_peer, r.layer_out.at[other_rows]
     )
     norm_core = copies.plan(r.d_norm.at[other_rows], r.norm_core, core_peer)
     norm_chip = [
@@ -1145,7 +1196,7 @@
         for i, b in enumerate(bits)
     ]
     in_core = copies.plan(
-        r.in_half, r.grad_in.at[half_rows], core_peer, r.grad_in.at[other_rows]
+        r.norm_core, r.grad_in.at[half_rows], core_peer, r.grad_in.at[other_rows]
     )
     small_got = {
         k: copies.plan(r.small_out.at[slot[k]], r.small_in.at[step_of[k]], peers.at(k))
@@ -1159,6 +1210,11 @@
 
     own_attn.start()
     attn_core.start()
+    early = [local(r.y_early.at[way], r.from_ring.at[way, pl.ds(0, 2)], 3 + way) for way in (0, 1)]
+    for copy in early:
+        copy.start()
+    for copy in early:
+        copy.wait()
 
     def fetch(k, place, core_place):
         loads = [
@@ -1171,17 +1227,12 @@
             copy.wait()
 
     def y_merge(place, core_place, start, size, before):
-        if before is not None:
-            received = r.y_early if before[1] < 2 else r.from_ring
-            copy = local(received.at[before], r.stage_ring.at[core_place], 3)
-            copy.start()
-            copy.wait()
 
         def step(rows):
             at = pl.ds(start + rows.start, rows.size)
             value = r.stage[place, at, :].astype(f32) + r.stage_core[core_place, at, :].astype(f32)
             if before is not None:
-                value = value + r.stage_ring[core_place, rows, :].astype(f32)
+                value = value + r.from_ring[before[0], before[1], rows, :].astype(f32)
             r.stage[place, at, :] = value.astype(bf16)
 
         tiles(size, 32, step)
@@ -1214,19 +1265,21 @@
     tiles(seq, 64, scales)
     own_attn.wait()
     attn_core.wait()
-    query_at = lax.broadcasted_iota(jnp.int32, (seq, seq), 0)
-    key_at = lax.broadcasted_iota(jnp.int32, (seq, seq), 1)
-    allowed = (key_at <= query_at) & (key_at < r.length[0:1, 0:1])
-    r.mask[...] = jnp.where(allowed, 0.0, -1e30)
+    lanes_at = lax.broadcasted_iota(jnp.int32, (seq, head), 1)
+    r.signed_sine[...] = jnp.where(lanes_at < head // 2, -r.sine[...], r.sine[...])
 
     def one_head(h, carry):
+        signed_sine = r.signed_sine[...]
         query, key, value = r.query[h], r.key[h], r.value[h]
         at = pl.ds(pl.multiple_of(h * head, head), head)
         d_context = nt(r.d_attn[...], r.w_output[at, :]).astype(bf16)
-        scores = nt(query, key) * z.score_scale + r.mask[...]
+        query_at = lax.broadcasted_iota(jnp.int32, (seq, seq), 0)
+        key_at = lax.broadcasted_iota(jnp.int32, (seq, seq), 1)
+        allowed = (key_at <= query_at) & (key_at < r.length[0:1, 0:1])
+        scores = jnp.where(allowed, nt(query, key) * z.score_scale, -1e30)
         scores = jnp.exp(scores - jnp.max(scores, axis=1, keepdims=True))
         probs = scores / jnp.sum(scores, axis=1, keepdims=True)
-        d_probs = nt(d_context, value)
+        d_probs = matmul(d_context, value)
         row_dot = jnp.sum(probs * d_probs, axis=1, keepdims=True)
         d_scores = (probs * (d_probs - row_dot)).astype(bf16)
         d_query = matmul(d_scores, key) * z.score_scale
@@ -1234,7 +1287,7 @@
         d_value = contract_rows(probs.astype(bf16), d_context)
 
         def unrope(values):
-            return values * r.cosine[...] - pltpu.roll(values, head // 2, 1) * r.sine[...]
+            return values * r.cosine[...] - pltpu.roll(values, head // 2, 1) * signed_sine
 
         for n, values in enumerate((unrope(d_query), unrope(d_key), d_value)):
             cols = pl.ds(pl.multiple_of(n * head_all + h * head, head), head)
@@ -1309,7 +1362,7 @@
                 inner = total * r.gain[...]
                 mean = jnp.mean(inner * hidden, axis=-1, keepdims=True)
                 total = r.wide[rows, :] + scale * inner - hidden * (scale * scale * scale) * mean
-                r.in_half[rows, :] = total.astype(bf16)
+                r.norm_core[rows, :] = total.astype(bf16)
 
             tiles(half, 32, join)
             if i + 1 < len(bits):
@@ -1317,8 +1370,8 @@
         in_core.start()
         own_in.start()
 
-    own_in = local(r.in_half, r.grad_in.at[half_rows], 6)
-    own_layer = local(r.layer_half, r.layer_out.at[half_rows], 7)
+    own_in = local(r.norm_core, r.grad_in.at[half_rows], 6)
+    own_layer = local(r.norm_total, r.layer_out.at[half_rows], 7)
     for j in range(3, 2 * far):
         w_step(j)
         if j + 2 < 2 * far:
@@ -1336,13 +1389,9 @@
     tiles(half, 32, first_of_home)
 
     def last(way, index, start):
-        copy = local(r.from_ring.at[way, index], r.stage_ring.at[0], 3)
-        copy.start()
-        copy.wait()
-
         def step(rows):
             at = pl.ds(start + rows.start, rows.size)
-            value = r.wide[at, :] + r.stage_ring[0, rows, :].astype(f32)
+            value = r.wide[at, :] + r.from_ring[way, index, rows, :].astype(f32)
             r.wide[at, :] = value
             r.total[at, :] = value.astype(bf16)
 
@@ -1389,7 +1438,7 @@
             if i + 1 < len(bits):
                 r.total[rows, :] = value.astype(bf16)
             else:
-                r.layer_half[rows, :] = (r.wide[rows, :] + value).astype(bf16)
+                r.norm_total[rows, :] = (r.wide[rows, :] + value).astype(bf16)
 
         tiles(half, 32, join)
         if i + 1 < len(bits):
@@ -1417,7 +1466,6 @@
         grad_in=((seq, width), bf16, in_place),
         w_total=((z.features, 4 * head_all), f32, whole),
         small_total=(vmem_ins["small_start"].shape[1:], f32, whole),
-        from_ring=((2, 2 * far - 1, half // 2, width), bf16, in_place),
     )
     small_shape = vmem_ins["small_start"].shape
     copies = groups + 1 + 8 * far + 2 * bits + 3 + (groups - 1) + 1 + bits
@@ -1426,17 +1474,15 @@
         d_qkv=pltpu.VMEM((seq, 3 * head_all), bf16),
         d_norm=pltpu.VMEM((seq, width), bf16),
         scale=pltpu.VMEM((seq, 128), f32),
-        mask=pltpu.VMEM((seq, seq), f32),
+        signed_sine=pltpu.VMEM((seq, z.head), f32),
         stage=pltpu.VMEM((4, half, width), bf16),
         stage_core=pltpu.VMEM((2, half, width), bf16),
-        stage_ring=pltpu.VMEM((2, half // 2, width), bf16),
+        from_ring=pltpu.VMEM((2, 2 * far - 1, half // 2, width), bf16),
         total=pltpu.VMEM((half, width), bf16),
         from_chip=pltpu.VMEM((max(bits, 1), half, width), bf16),
-        layer_half=pltpu.VMEM((half, width), bf16),
         norm_core=pltpu.VMEM((half, width), bf16),
         norm_total=pltpu.VMEM((half, width), bf16),
         norm_chip=pltpu.VMEM((max(bits, 1), half, width), bf16),
-        in_half=pltpu.VMEM((half, width), bf16),
         wide=pltpu.VMEM((half, width), f32),
         w_parts=pltpu.VMEM((groups, z.features, 4 * head_all), bf16),
         w_received=pltpu.VMEM((2, 2 * far - 1, z.features // 2, 4 * head_all), bf16),
@@ -1561,7 +1607,7 @@
             expert_down,
             lax.dynamic_slice_in_dim(shared_gate, group * units, units, 1),
             lax.dynamic_slice_in_dim(shared_up, group * units, units, 1),
-            lax.dynamic_slice_in_dim(shared_down, group * units, units, 0),
+            shared_down,
         ),
         jnp.concatenate([w_router, w_sigmoid[:, None]], axis=1),
         capacity,
@@ -1605,7 +1651,6 @@
     small_rows = round_up(experts_all + 3 + lane_count * bias_rows, 8)
     small_start = jnp.pad(to_groups, ((0, 0), (0, small_rows - to_groups.shape[1]), (0, 0)))
 
-    signed_sine = jnp.concatenate([-sine[..., : head_width // 2], sine[..., head_width // 2 :]], -1)
     done = finish(
         groups,
         lane_count,
@@ -1616,7 +1661,7 @@
         dict(
             query=jnp.swapaxes(query, 0, 1),
             key=jnp.swapaxes(key, 0, 1),
-            value=jnp.swapaxes(value, 0, 1),
+            value=jnp.transpose(value, (1, 2, 0)),
             context=context_flat,
             normed=normed_attn,
             hidden=hidden_in,
@@ -1626,7 +1671,7 @@
             w_key=w_key,
             w_value=w_value,
             cosine=cosine[:, 0],
-            sine=signed_sine[:, 0],
+            sine=sine[:, 0],
             length=jnp.broadcast_to(length, (8, 128)),
             small_start=small_start,
         ),

time: 603 us -> 593 us (0.983)
    unnamed x72 -> x70, local copies, waits for them, and re-layouts: 12.7 us -> 12 us
  transfers between devices with their start and end apart: 1 -> 1, of which waited for: 0 -> 0; matrix products, arithmetic and copies ran while one was open for 6% -> 5% of each run, Pallas kernels for 31% -> 32%
where the time goes in v4:
time: 593 us; the launch traced here: 589 us
  Pallas kernels  501 us (84%)
  other arithmetic  31.2 us (5%)
  local copies, waits for them, and re-layouts  29.5 us (5%)
  matrix products  18.6 us (3%)
  starting transfers between devices  6.51 us (1%)
    pallas_call x1, Pallas kernels, run_experts(): pl.pallas_call(functools.partial(experts_kernel, z, names), out_shape=tup...  314 us
    pallas_call x1, Pallas kernels, finish(): pl.pallas_call(functools.partial(finish_kernel, z, names), out_shape=tupl...  187 us
    dot_general x5, matrix products, matmul(): return jnp.dot(left, right, preferred_element_type=f32)  12.2 us
    unnamed x70, local copies, waits for them, and re-layouts  12 us
  transfers between devices with their start and end apart: 1, of which 0 were waited for; matrix products, arithmetic and copies ran while one was open for 5% of the time, Pallas kernels for 32%

profile of v4, /device:TPU:21, one launch (start us, length us, event | category | flops | bytes accessed | tf_op | source)
XLA Modules:
  0.0 589.0 jit_solution(13352254694307731134)
XLA Ops:
  0.7 0.0 copy-start
  0.7 0.8 convert_element_type.117
  1.5 2.1 fusion
  3.7 0.0 copy-start.17
  3.7 0.5 fusion.2.refs_4_
  4.2 1.0 copy-done.17
  5.3 2.3 convolution_add_fusion.3
  7.6 1.6 copy.61
  9.2 3.9 convolution_add_fusion.2
  13.0 1.5 copy.64
  14.6 0.1 broadcast_multiply_fusion
  14.7 1.6 fusion.25
  16.3 0.0 copy-start.14
  17.0 0.1 fusion.21
  17.2 0.7 slice_negate_fusion
  17.9 0.7 fusion.20
  18.6 0.9 fusion.5
  19.5 0.0 copy-done.10
  19.6 0.9 exponential_reduce_fusion
  20.5 1.1 copy-done.2
  21.6 0.0 copy-start.19
  21.7 3.3 broadcast_select_fusion.refs_3_
  24.9 0.6 convert_element_type.133
  25.6 0.3 copy.69
  25.9 3.0 fusion.13
  29.0 1.4 fusion.14
  30.4 0.8 copy-done.20
  31.2 2.6 convolution_convert_fusion.refs_0_
  33.8 2.9 constant_dynamic-slice_fusion.5
  36.7 1.7 fusion.7.refs_8_
  38.4 0.9 pad.22.refs_10_
  39.3 0.6 pad.19.refs_4_
  39.9 313.6 %run_experts.1 = (bf16[256,2048]{1,0:T(8,128)(2,1)}, f32[24,512]{1,0:T(8,128)}, f32[256,2048]{1,0:T(8,128)}, f32[256,2048]{1,0:T(8,128)}, bf16[8,512,2048]{2,1,0...) custom-call(bf16[512,2048]{1,0:T(8,128)(2,1)} %convolution_convert_f, ...), custom_call_target="tpu_custom_call" | custom-call | tf_op jit(solution)/shard_map/run_experts/pallas_call | solution.py:1136
  353.5 6.5 %all-to-all-start = ((bf16[8,528,256]{2,1,0:T(8,128)(2,1)}), bf16[8,528,256]{2,1,0:T(8,128)(2,1)}, u32[]{:S(2)}, u32[]{:S(2)}) async-start(bf16[8,528,256]{2,1,0:T(8,128)(2,1)} %get-tuple-element.45), calls=%async_computation | async-start | bytes 4325376 | tf_op jit(solution)/shard_map/all_to_all | solution.py:1693
  360.0 0.4 fusion.42
  360.4 0.4 fusion.43
  361.0 0.6 copy-done.1
  361.6 3.6 multiply_reduce_fusion
  365.2 0.1 dynamic-slice_bitcast_fusion.1
  365.3 2.0 copy.76.refs_3_
  367.4 0.2 fusion.22
  367.5 0.1 copy.77
  367.7 0.1 dynamic-slice.8
  367.8 1.6 fusion.16
  369.4 0.8 pad.23.refs_14_
  370.2 2.3 fusion.38
  372.5 0.6 broadcast_in_dim.33.refs_13_
  373.1 187.1 %finish.1 = (bf16[512,2048]{1,0:T(8,128)(2,1)}, bf16[512,2048]{1,0:T(8,128)(2,1)}, f32[256,2048]{1,0:T(8,128)}, f32[48,256]{1,0:T(8,128)}) custom-call(bf16[4,512,128]{2,1,0:T(8,128)(2,1)} %bitcast.87, bf16[4,512,128]{2,1,0:T(8,128)(2,1)} %bitcast.86, bf16[4,128,512]{2,1,0:T(8,128)(2,1)} %bitcast.98, bf16[512,512]{1,0:T(8,128)(2,1)} %copy.76.refs_3_, ...), custom_call_target="tpu_custom_call" | custom-call | tf_op jit(solution)/shard_map/finish/pallas_call | solution.py:1497
  560.3 2.7 slice_bitcast_fusion
  563.0 1.0 copy.72
  564.0 5.3 convert_element_type.145
  569.3 0.7 fusion.32
  569.9 0.6 fusion.41
  570.5 0.6 slice_bitcast_fusion.1
  571.1 3.3 convert_bitcast_fusion
  574.4 3.3 convert_bitcast_fusion.1
  577.7 2.1 copy_bitcast_fusion
  579.9 1.5 fusion.40
  581.3 1.5 copy.73
  582.9 1.5 copy.74
  584.4 0.5 copy-done.16
  584.9 1.3 copy.82
  586.2 1.0 copy-done.15
  587.2 1.3 copy.83
  (79 shorter events, 0.4 us)
Async XLA Ops:
  0.7 3.0 copy-start
  0.7 3.0 copy-start.29
  1.5 2.7 copy-start.23
  3.7 1.6 copy-start.17
  5.3 3.9 copy-start.6
  7.6 1.6 copy-start.30
  16.3 1.6 copy-start.13
  16.3 1.6 copy-start.14
  18.6 0.9 copy-start.9
  18.6 1.0 copy-start.10
  19.6 2.0 copy-start.2
  19.6 2.0 copy-start.31
  21.6 3.3 copy-start.28
  21.6 3.9 copy-start.24
  21.6 3.9 copy-start.19
  21.7 4.2 copy-start.7
  25.9 3.1 copy-start.3
  29.0 1.4 copy-start.21
  29.0 2.2 copy-start.18
  30.4 0.8 copy-start.20
  36.7 2.6 copy-start.27
  353.5 6.6 %copy-start.8 = (bf16[256,2048]{1,0:T(8,128)(2,1)S(1)}, bf16[256,2048]{1,0:T(8,128)(2,1)}, u32[]{:S(2)}) copy-start(bf16[256,2048]{1,0:T(8,128)(2,1)} %get-tuple-element.34) | copy-start | bytes 3145732
  353.5 224.3 %all-to-all-start = ((bf16[8,528,256]{2,1,0:T(8,128)(2,1)}), bf16[8,528,256]{2,1,0:T(8,128)(2,1)}, u32[]{:S(2)}, u32[]{:S(2)}) async-start(bf16[8,528,256]{2,1,0:T(8,128)(2,1)} %get-tuple-element.45), calls=%async_computation | async-start | bytes 4325376 | tf_op jit(solution)/shard_map/all_to_all | solution.py:1693
  360.0 0.8 copy-start.26
  360.0 1.6 copy-start.1
  360.0 1.6 copy-start.22
  367.4 2.9 copy-start.5
  367.5 2.7 copy-start.4
  560.3 3.7 copy-start.25
  564.0 7.1 %copy-start.12 = (bf16[2,352,2048]{2,1,0:T(8,128)(2,1)S(1)}, bf16[2,352,2048]{2,1,0:T(8,128)(2,1)}, u32[]{:S(2)}) copy-start(bf16[2,352,2048]{2,1,0:T(8,128)(2,1)} %get-tuple-element.47) | copy-start | bytes 8650756
  571.1 3.3 copy-start.11
  582.9 2.0 copy-start.16
  584.9 2.3 copy-start.15
